TPU v7x, 128 devices: a whole 4x4x4 slice. The times are simulated.
128 devices in a mesh: song: 2 (over y_lo), seq: 64 (over z, x, y_hi, core).
Axes of the slice: x: 4, y: 4 (y_hi: 2, y_lo: 2; y = y_hi * 2 + y_lo), z: 4, core: 2. Of those that a mesh axis runs over, the one named last changes fastest.
Arguments:
- song_ids: int32 [16384], P(('song', 'seq')), parts along dimension 0, may hold values from 0 to 2047
- table: bfloat16 [2048, 2432], P(None, 'seq'), may hold values from -6 to 6
- position_table: bfloat16 [8192, 2432], P('seq'), may hold values from -4 to 4
- w_qkv: bfloat16 [2, 2432, 1800], replicated, may hold values from -4 to 4
- w_out: bfloat16 [2, 600, 2432], replicated, may hold values from -0.25 to 0.25
Outputs:
- stream_out: bfloat16 [16384, 2432], P(('song', 'seq')), parts along dimension 0
There are 2 independent parts, one for each index of `song`. A program takes and returns all parts, laid end to end along the dimension named above; an argument that names none is the same for every part. Nothing has to cross between parts.
All inputs are finite; a program needn't handle non-finite values.
Results may differ from a plain program's by a relative error of at most 0.0065.
Values may be sent and summed in bfloat16 or wider, within the bound.
No kernel may reach another device: no remote copies, remote signals or barrier semaphores. Data moves between devices by JAX's collectives and lax.ppermute only.
A program may use at most 192 MiB of HBM per device.

v0:
```python
import math

import jax
import jax.numpy as jnp
from jax import lax
from jax.sharding import PartitionSpec as P

HEADS = 4
HEAD = 150


epsilon = 1e-05


def from_behind(value, axis, by):
    length = lax.axis_size(axis)
    pairs = [(i, i + by) for i in range(length) if 0 <= i + by < length]
    return lax.ppermute(value, axis, pairs)


def normalize(residual):
    center_mean = jnp.mean(residual, axis=-1, keepdims=True)
    centered = residual - center_mean
    variance = jnp.mean(centered * centered, axis=-1, keepdims=True)
    return (centered * lax.rsqrt(variance + epsilon)).astype(jnp.bfloat16)


def project(residual, weight):
    joined = jnp.dot(normalize(residual), weight, preferred_element_type=jnp.float32).astype(
        jnp.bfloat16
    )
    return joined.reshape(residual.shape[0], HEADS, 3 * HEAD)


def softmax_rounded(scores):
    top_score = jnp.max(scores, axis=-1, keepdims=True)
    lifted = jnp.exp(scores - top_score)
    return (lifted / jnp.sum(lifted, axis=-1, keepdims=True)).astype(jnp.bfloat16)


def shards(song_ids, table, position_table, w_qkv, w_out):
    inv_root = 1.0 / math.sqrt(HEAD)
    axis_count = lax.axis_size("seq")
    row_index = lax.axis_index("seq")
    all_codes = lax.all_gather(song_ids, "seq", axis=0, tiled=True)
    picked = jnp.take(table, all_codes, axis=0)
    embedded = lax.all_to_all(picked, "seq", split_axis=0, concat_axis=1, tiled=True)
    residual = embedded.astype(jnp.float32) + position_table.astype(jnp.float32)
    local_tokens = residual.shape[0]
    joined = project(residual, w_qkv[0])
    every_row = lax.all_gather(joined[:, :, HEAD:], "seq", axis=0, tiled=True)
    row_grid = every_row.reshape(axis_count, local_tokens, HEADS, 2 * HEAD)
    scores = (
        jnp.einsum(
            "chd,rchd->chr",
            joined[:, :, :HEAD],
            row_grid[..., :HEAD],
            preferred_element_type=jnp.float32,
        )
        * inv_root
    )
    allowed = jnp.arange(axis_count) <= row_index
    probs = softmax_rounded(jnp.where(allowed, scores, -jnp.inf))
    mixed = jnp.einsum(
        "chr,rchd->chd", probs, row_grid[..., HEAD:], preferred_element_type=jnp.float32
    ).astype(jnp.bfloat16)
    residual = residual + jnp.dot(
        mixed.reshape(local_tokens, HEADS * HEAD), w_out[0], preferred_element_type=jnp.float32
    )
    joined = project(residual, w_qkv[1])
    before = from_behind(joined[:, :, HEAD:], "seq", 1)
    query = joined[:, :, :HEAD]
    far_scores = (
        jnp.einsum("chd,khd->hck", query, before[..., :HEAD], preferred_element_type=jnp.float32)
        * inv_root
    )
    far_scores = jnp.where(row_index > 0, far_scores, -jnp.inf)
    own_scores = (
        jnp.einsum(
            "chd,chd->hc", query, joined[:, :, HEAD : 2 * HEAD], preferred_element_type=jnp.float32
        )
        * inv_root
    )
    top_score = jnp.maximum(jnp.max(far_scores, axis=-1), own_scores)
    far_lifted = jnp.exp(far_scores - top_score[..., None])
    own_lifted = jnp.exp(own_scores - top_score)
    total = jnp.sum(far_lifted, axis=-1) + own_lifted
    far_probs = (far_lifted / total[..., None]).astype(jnp.bfloat16)
    own_probs = (own_lifted / total).astype(jnp.bfloat16)
    far_part = jnp.einsum(
        "hck,khd->chd", far_probs, before[..., HEAD:], preferred_element_type=jnp.float32
    )
    own_part = jnp.transpose(own_probs.astype(jnp.float32))[..., None] * joined[
        :, :, 2 * HEAD :
    ].astype(jnp.float32)
    mixed = (far_part + own_part).astype(jnp.bfloat16)
    residual = residual + jnp.dot(
        mixed.reshape(local_tokens, HEADS * HEAD), w_out[1], preferred_element_type=jnp.float32
    )
    return residual.astype(jnp.bfloat16)


def solution(mesh):
    in_specs = (P(("song", "seq")), P(None, "seq"), P("seq", None), P(), P())
    out_specs = P(("song", "seq"), None)
    return jax.shard_map(shards, mesh=mesh, in_specs=in_specs, out_specs=out_specs, check_vma=False)
```

profile of v0, /device:TPU:1, one launch (start us, length us, event | category | flops | bytes accessed | tf_op | source)
XLA Modules:
  0.0 347.4 jit_solution(981527527557596328)
XLA Ops:
  6.5 98.1 %all-gather = s32[64,1,128]{2,1,0:T(1,128)S(1)} all-gather(s32[1,1,128]{2,1,0:T(1,128)} %bitcast.80), channel_id=1, replica_groups=mesh['song'=2,'seq'=64] {'seq'}, dimensions={0}, use_global_device_ids=true | all-gather | bytes 33280 | tf_op jit(solution)/shard_map/all_gather | solution.py:45
  104.6 1.2 copy.17
  105.9 24.0 %gather_fusion = bf16[8192,38]{1,0:T(8,128)(2,1)S(1)} fusion(bf16[2048,38]{1,0:T(8,128)(2,1)S(1)} %copy.17, s32[8192]{0:T(1024)S(1)} %fusion.43), kind=kCustom, calls=%fused_computation | custom fusion | bytes 1277952 | tf_op jit(solution)/shard_map/jit(_take)/gather | solution.py:46
  129.9 1.0 copy.18
  131.0 18.8 %all_to_all.10 = bf16[64,128,38]{1,2,0:T(8,128)(2,1)S(1)} all-to-all(bf16[64,128,38]{1,2,0:T(8,128)(2,1)S(1)} %broadcast_select_fusion), channel_id=1, replica_groups=mesh['song'=2,'seq'=64] {'seq'}, dimensions={0} | all-to-all | bytes 1245184 | tf_op jit(solution)/shard_map/all_to_all | solution.py:47
  150.0 0.4 copy.19
  150.4 0.7 copy-done
  151.1 0.2 fusion.39
  151.3 0.3 multiply_reduce_fusion.3
  151.6 6.2 %fusion.13 = bf16[128,1800]{0,1:T(8,128)(2,1)S(1)} fusion(bf16[2,2432,1800]{1,2,0:T(8,128)(2,1)} %param.8, f32[128]{0:T(128)S(1)} %add_rsqrt_fusion.1, f32[128]{0:T(128)S(1)} %broadcast_multiply_fusion.1, f32[128,2432]{1,0:T(8,128)S(1)} %copy.19, bf16[128,2432]{1,0:T(8,128)(2,1)S(1)} %copy-done), kind=kOutput, calls=%fused_computation.20 | convolution fusion | flops 1122452480 | bytes 11084800 | tf_op jit(solution)/shard_map/dot_general | solution.py:29
  157.9 0.8 slice.59
  158.8 117.0 %all-gather.3.cloned.1.call-done = bf16[8192,4,300]{0,2,1:T(8,128)(2,1)} async-done(((bf16[128,4,300]{0,2,1:T(8,128)(2,1)}), bf16[8192,4,300]{0,2,1:T(8,128)(2,1)}) %all-gather.3.cloned.1.call-update) | async-done | bytes 19660816 | tf_op jit(solution)/shard_map/all_gather | solution.py:51
  275.8 27.6 %reshape.61 = bf16[64,128,4,300]{1,0,3,2:T(8,128)(2,1)} reshape(bf16[8192,4,300]{0,2,1:T(8,128)(2,1)} %all-gather.3.cloned.1.call-done) | data formatting | bytes 39321600 | tf_op jit(solution)/shard_map/reshape | solution.py:52
  303.4 6.7 %multiply_reduce_fusion.1 = f32[128,4,64]{0,2,1:T(8,128)S(1)} fusion(bf16[64,128,4,300]{1,0,3,2:T(8,128)(2,1)} %reshape.61, f32[128,4,150]{0,2,1:T(8,128)S(1)} %slice_convert_fusion), kind=kLoop, calls=%fused_computation.4 | loop fusion | flops 14712832 | bytes 10268672 | tf_op jit(solution)/shard_map/chd,rchd->chr/dot_general | solution.py:54
  310.1 0.1 fusion.26
  310.2 8.3 %multiply_reduce_fusion = bf16[128,4,150]{0,2,1:T(8,128)(2,1)S(1)} fusion(bf16[64,128,4,300]{1,0,3,2:T(8,128)(2,1)} %reshape.61, f32[128,4,64]{0,2,1:T(8,128)S(1)} %fusion.26), kind=kLoop, calls=%fused_computation.3 | loop fusion | flops 14668800 | bytes 10115072 | tf_op jit(solution)/shard_map/chr,rchd->chd/dot_general | solution.py:64
  318.6 2.6 fusion.53
  321.2 0.3 multiply_reduce_fusion.2
  321.5 6.2 %fusion.16 = bf16[128,1800]{0,1:T(8,128)(2,1)S(1)} fusion(bf16[2,2432,1800]{1,2,0:T(8,128)(2,1)} %param.8, f32[128,2432]{1,0:T(8,128)S(1)} %get-tuple-element.6, f32[128]{0:T(128)S(1)} %add_rsqrt_fusion, f32[128]{0:T(128)S(1)} %broadcast_multiply_fusion), kind=kOutput, calls=%fused_computation.21 | convolution fusion | flops 1121829888 | bytes 10462208 | tf_op jit(solution)/shard_map/dot_general | solution.py:29
  327.9 4.8 %collective-permute-start = (bf16[128,4,300]{0,2,1:T(8,128)(2,1)S(1)}, bf16[128,4,300]{0,2,1:T(8,128)(2,1)S(1)}, u32[]{:S(2)}, u32[]{:S(2)}) collective-permute-start(bf16[128,4,300]{0,2,1:T(8,128)(2,1)S(1)} %slice.62), channel_id=1, source_target_pairs={{0,1},{1,2},{2,3},{3,4},{4,5},{5,6},{6,7},{7,8},{8,9},{9,10},{10,1... | collective-permute-start | bytes 921608 | tf_op jit(solution)/shard_map/ppermute | solution.py:18
  332.8 3.7 %collective-permute-done = bf16[128,4,300]{0,2,1:T(8,128)(2,1)S(1)} collective-permute-done((bf16[128,4,300]{0,2,1:T(8,128)(2,1)S(1)}, bf16[128,4,300]{0,2,1:T(8,128)(2,1)S(1)}, u32[]{:S(2)}, u32[]{:S(2)}) %collective-permute-start) | collective-permute-done | bytes 307232 | tf_op jit(solution)/shard_map/ppermute | solution.py:18
  336.5 0.3 fusion.54
  336.9 0.3 fusion.21
  337.2 3.4 fusion.8
  (24 shorter events, 1.0 us)
Async XLA Ops:
  6.5 269.2 %all-gather.3.cloned.1.call-start = ((), (), s32[]{:S(2)}) async-start(), calls=%async_computation.1 | async-start | bytes 20234240 | tf_op jit(solution)/shard_map/all_gather | solution.py:51
  150.0 1.1 copy-start
  327.9 8.6 %collective-permute-start = (bf16[128,4,300]{0,2,1:T(8,128)(2,1)S(1)}, bf16[128,4,300]{0,2,1:T(8,128)(2,1)S(1)}, u32[]{:S(2)}, u32[]{:S(2)}) collective-permute-start(bf16[128,4,300]{0,2,1:T(8,128)(2,1)S(1)} %slice.62), channel_id=1, source_target_pairs={{0,1},{1,2},{2,3},{3,4},{4,5},{5,6},{6,7},{7,8},{8,9},{9,10},{10,1... | collective-permute-start | bytes 921608 | tf_op jit(solution)/shard_map/ppermute | solution.py:18
Sparse Core Ops, SparseCore 0:
  158.9 116.8 all-gather.2
where the time goes:
time: 350 us; the launch traced here: 347 us
  waiting for transfers between devices  121 us (35%)
  blocking collectives  117 us (33%)
  local copies, waits for them, and re-layouts  56.2 us (16%)
  matrix products  18.9 us (5%)
  other arithmetic  16.4 us (5%)
  between operations  13.6 us (4%)
  starting transfers between devices  4.78 us (1%)
    all_gather x1, waiting for transfers between devices, shards(): every_row = lax.all_gather(joined[:, :, HEAD:], 'seq', axis=0, tiled=True)  117 us
    all_gather x1, blocking collectives, shards(): all_codes = lax.all_gather(song_ids, 'seq', axis=0, tiled=True)  98.1 us
    reshape x1, local copies, waits for them, and re-layouts, shards(): row_grid = every_row.reshape(axis_count, local_tokens, HEADS, 2 * HEAD)  27.6 us
    gather x2, local copies, waits for them, and re-layouts, shards(): picked = jnp.take(table, all_codes, axis=0)  25 us
    all_to_all x1, blocking collectives, shards(): lax.all_to_all(picked, 'seq', split_axis=0, concat_axis=1, tiled=True)  18.8 us
    dot_general x2, matrix products, project(): jnp.dot(normalize(residual), weight, preferred_element_type=jnp.float32)  12.3 us
    dot_general x1, other arithmetic, shards(): jnp.einsum('chr,rchd->chd', probs, row_grid[..., HEAD:], preferred_elemen...  8.34 us
  transfers between devices with their start and end apart: 2, of which 2 were waited for; matrix products, arithmetic and copies ran while one was open for 0% of the time, Pallas kernels for 0%

commit v1 on v0

v1 whole, which is shorter than its diff:
```python
import functools
import math

import jax
import jax.numpy as jnp
from jax import lax
from jax.experimental import pallas as pl
from jax.experimental.pallas import tpu as pltpu
from jax.sharding import PartitionSpec as P

HEADS = 4
HEAD = 150
GROUPS = 8

epsilon = 1e-05


def normalize(residual):
    center_mean = jnp.mean(residual, axis=-1, keepdims=True)
    centered = residual - center_mean
    variance = jnp.mean(centered * centered, axis=-1, keepdims=True)
    return (centered * lax.rsqrt(variance + epsilon)).astype(jnp.bfloat16)


def project(residual, weight):
    return jnp.dot(normalize(residual), weight, preferred_element_type=jnp.float32).astype(
        jnp.bfloat16
    )


def lookup_kernel(codes_ref, table_ref, out_ref):
    depth = table_ref.shape[1]
    step = table_ref.shape[0] // GROUPS
    count = out_ref.shape[0]
    table_rows = table_ref[...].astype(jnp.float32)
    padded = (depth + 7) // 8 * 8
    flipped = jnp.transpose(
        jnp.concatenate(
            [table_rows, jnp.zeros((table_rows.shape[0], 128 - depth), jnp.float32)], axis=1
        )
    )[:padded]
    stacked = jnp.concatenate(
        [flipped[:, g * step : (g + 1) * step] for g in range(GROUPS)], axis=0
    ).astype(jnp.bfloat16)
    slots = lax.broadcasted_iota(jnp.int32, (step, 128), 0)
    for d in range(count):
        codes = codes_ref[d : d + 1, :]
        low = codes % step
        high = codes // step
        onehot = jnp.where(slots == low, 1.0, 0.0).astype(jnp.bfloat16)
        found = jnp.dot(stacked, onehot, preferred_element_type=jnp.float32)
        chosen = jnp.zeros((padded, 128), jnp.float32)
        for g in range(GROUPS):
            chosen = jnp.where(high == g, found[g * padded : (g + 1) * padded], chosen)
        out_ref[d] = chosen[:depth].astype(jnp.bfloat16)


def lookup(codes, table):
    count = codes.shape[0]
    depth = table.shape[1]
    return pl.pallas_call(
        lookup_kernel,
        out_shape=jax.ShapeDtypeStruct((count, depth, 128), jnp.bfloat16),
        in_specs=[pl.BlockSpec(memory_space=pltpu.VMEM)] * 2,
        out_specs=pl.BlockSpec(memory_space=pltpu.VMEM),
        compiler_params=pltpu.CompilerParams(vmem_limit_bytes=16 * 1024 * 1024),
    )(codes, table)


def exchange(value):
    return lax.all_to_all(value, "seq", split_axis=0, concat_axis=0, tiled=True)


def shards(song_ids, table, position_table, w_qkv, w_out):
    inv_root = 1.0 / math.sqrt(HEAD)
    rows = lax.axis_size("seq")
    row_index = lax.axis_index("seq")
    tokens, width = position_table.shape
    per = tokens // rows
    attended = HEADS * HEAD

    digits = jnp.stack([song_ids // 64, song_ids % 64]).astype(jnp.bfloat16)
    sent = jnp.concatenate(
        [
            position_table.reshape(rows, per, width),
            jnp.broadcast_to(digits[None], (rows, 2, tokens)),
        ],
        axis=-1,
    )
    got = exchange(sent)
    position = got[:, :, :width].reshape(tokens, width)
    codes = got[:, 0, width:].astype(jnp.int32) * 64 + got[:, 1, width:].astype(jnp.int32)
    codes = jnp.transpose(codes.reshape(rows, rows, per), (1, 2, 0)).reshape(rows, tokens)
    found = exchange(lookup(codes, table))
    embedded = jnp.transpose(found.reshape(rows, -1, per, rows), (3, 2, 0, 1)).reshape(
        tokens, width
    )
    residual = embedded.astype(jnp.float32) + position.astype(jnp.float32)

    joined = project(residual, w_qkv[0]).reshape(tokens, HEADS, 3 * HEAD)
    scores = (
        jnp.einsum(
            "thd,uhd->htu",
            joined[:, :, :HEAD],
            joined[:, :, HEAD : 2 * HEAD],
            preferred_element_type=jnp.float32,
        )
        * inv_root
    )
    place = jnp.arange(tokens)
    allowed = (place[:, None] % per == place[None, :] % per) & (place[:, None] >= place[None, :])
    scores = jnp.where(allowed, scores, -jnp.inf)
    lifted = jnp.exp(scores - jnp.max(scores, axis=-1, keepdims=True))
    probs = (lifted / jnp.sum(lifted, axis=-1, keepdims=True)).astype(jnp.bfloat16)
    mixed = jnp.einsum(
        "htu,uhd->thd", probs, joined[:, :, 2 * HEAD :], preferred_element_type=jnp.float32
    ).astype(jnp.bfloat16)
    residual = residual + jnp.dot(
        mixed.reshape(tokens, attended), w_out[0], preferred_element_type=jnp.float32
    )

    residual = exchange(residual.astype(jnp.bfloat16).reshape(rows, per, width))
    residual = residual.reshape(tokens, width).astype(jnp.float32)
    joined = project(residual, w_qkv[1]).reshape(tokens, HEADS, 3 * HEAD)
    before = lax.ppermute(
        joined[:, :, HEAD:], "seq", [(i, i + 1) for i in range(rows - 1)]
    )
    query = joined[:, :, :HEAD]
    far_scores = (
        jnp.einsum("chd,khd->hck", query, before[..., :HEAD], preferred_element_type=jnp.float32)
        * inv_root
    )
    far_scores = jnp.where(row_index > 0, far_scores, -jnp.inf)
    own_scores = (
        jnp.einsum(
            "chd,chd->hc", query, joined[:, :, HEAD : 2 * HEAD], preferred_element_type=jnp.float32
        )
        * inv_root
    )
    top_score = jnp.maximum(jnp.max(far_scores, axis=-1), own_scores)
    far_lifted = jnp.exp(far_scores - top_score[..., None])
    own_lifted = jnp.exp(own_scores - top_score)
    total = jnp.sum(far_lifted, axis=-1) + own_lifted
    far_probs = (far_lifted / total[..., None]).astype(jnp.bfloat16)
    own_probs = (own_lifted / total).astype(jnp.bfloat16)
    far_part = jnp.einsum(
        "hck,khd->chd", far_probs, before[..., HEAD:], preferred_element_type=jnp.float32
    )
    own_part = jnp.transpose(own_probs.astype(jnp.float32))[..., None] * joined[
        :, :, 2 * HEAD :
    ].astype(jnp.float32)
    mixed = (far_part + own_part).astype(jnp.bfloat16)
    residual = residual + jnp.dot(
        mixed.reshape(tokens, attended), w_out[1], preferred_element_type=jnp.float32
    )
    return residual.astype(jnp.bfloat16)


def solution(mesh):
    in_specs = (P(("song", "seq")), P(None, "seq"), P("seq", None), P(), P())
    out_specs = P(("song", "seq"), None)
    return jax.shard_map(shards, mesh=mesh, in_specs=in_specs, out_specs=out_specs, check_vma=False)
```

time: 350 us -> 152 us (0.43)
  the two profiles are of different devices: /device:TPU:1 before, /device:TPU:32 now
where the time goes in v1:
time: 152 us; the launch traced here: 151 us
  local copies, waits for them, and re-layouts  44.4 us (29%)
  waiting for transfers between devices  24.3 us (16%)
  blocking collectives  24.1 us (16%)
  matrix products  19.9 us (13%)
  starting transfers between devices  18.9 us (12%)
  other arithmetic  15.4 us (10%)
  Pallas kernels  3.88 us (3%)
    convert_element_type x7, local copies, waits for them, and re-layouts, shards(): residual = embedded.astype(jnp.float32) + position.astype(jnp.float32)  29.4 us
    all_to_all x1, blocking collectives, exchange(): return lax.all_to_all(value, 'seq', split_axis=0, concat_axis=0, tiled=True)  24.1 us
    all_to_all x2, starting transfers between devices, exchange(): return lax.all_to_all(value, 'seq', split_axis=0, concat_axis=0, tiled=True)  16.9 us
    all_to_all x2, waiting for transfers between devices, exchange(): return lax.all_to_all(value, 'seq', split_axis=0, concat_axis=0, tiled=True)  13.9 us
    dot_general x2, matrix products, project(): jnp.dot(normalize(residual), weight, preferred_element_type=jnp.float32)  12.9 us
    convert_element_type x3, local copies, waits for them, and re-layouts, normalize(): return (centered * lax.rsqrt(variance + epsilon)).astype(jnp.bfloat16)  10.5 us
    ppermute x1, waiting for transfers between devices, shards(): lax.ppermute(joined[:, :, HEAD:], 'seq', [(i, i + 1) for i in range(rows...  10.4 us
    reduce_sum x2, other arithmetic, normalize(): center_mean = jnp.mean(residual, axis=-1, keepdims=True)  4.99 us
  transfers between devices with their start and end apart: 3, of which 2 were waited for; matrix products, arithmetic and copies ran while one was open for 11% of the time, Pallas kernels for 0%

profile of v1, /device:TPU:32, one launch (start us, length us, event | category | flops | bytes accessed | tf_op | source)
XLA Modules:
  0.0 151.3 jit_solution(10857609703401596231)
XLA Ops:
  0.7 1.9 %reshape.170 = bf16[64,2,2432]{2,1,0:T(2,128)(2,1)S(1)} reshape(bf16[128,2432]{1,0:T(8,128)(2,1)} %param.7) | data formatting | bytes 1245184 | tf_op jit(solution)/shard_map/reshape | solution.py:85
  2.7 1.4 pad_maximum_fusion
  4.1 11.1 %all-to-all-start = ((bf16[64,2,2560]{2,1,0:T(2,128)(2,1)}), bf16[64,2,2560]{2,1,0:T(2,128)(2,1)S(1)}, u32[]{:S(2)}, u32[]{:S(2)}) async-start(bf16[64,2,2560]{2,1,0:T(2,128)(2,1)} %pad_maximum_fusion), calls=%async_computation | async-start | bytes 1310720 | tf_op jit(solution)/shard_map/all_to_all | solution.py:71
  15.6 13.9 %all-to-all-done = bf16[64,2,2560]{2,1,0:T(2,128)(2,1)S(1)} async-done(((bf16[64,2,2560]{2,1,0:T(2,128)(2,1)}), bf16[64,2,2560]{2,1,0:T(2,128)(2,1)S(1)}, u32[]{:S(2)}, u32[]{:S(2)}) %all-to-all-start) | async-done | bytes 655392 | tf_op jit(solution)/shard_map/all_to_all | solution.py:71
  29.9 3.9 %shard_map.55 = bf16[64,38,128]{2,1,0:T(8,128)(2,1)} custom-call(s32[64,128]{1,0:T(8,128)S(1)} %reshape.171.codes_ref, bf16[2048,38]{1,0:T(8,128)(2,1)S(1)} %copy.73.table_ref), custom_call_target="tpu_custom_call" | custom-call | tf_op jit(solution)/shard_map/pallas_call | solution.py:61
  33.8 5.8 %all-to-all-start.1 = ((bf16[64,38,128]{2,1,0:T(8,128)(2,1)}), bf16[64,38,128]{2,1,0:T(8,128)(2,1)S(1)}, u32[]{:S(2)}, u32[]{:S(2)}) async-start(bf16[64,38,128]{2,1,0:T(8,128)(2,1)} %shard_map.55), calls=%async_computation.1 | async-start | bytes 1310720 | tf_op jit(solution)/shard_map/all_to_all | solution.py:71
  40.1 7.2 %reshape.186 = f32[64,2,64,38]{3,2,1,0:T(8,128)} reshape(f32[64,2,2432]{2,1,0:T(2,128)S(1)} %slice_convert_fusion) | data formatting | bytes 2490368 | tf_op jit(solution)/shard_map/convert_element_type | solution.py:98
  47.3 1.9 %reshape.178 = f32[128,2432]{1,0:T(8,128)} reshape(f32[64,2,2432]{2,1,0:T(2,128)S(1)} %slice_convert_fusion) | data formatting | bytes 2490368 | tf_op jit(solution)/shard_map/convert_element_type | solution.py:98
  49.2 7.2 %copy.77 = f32[64,2,64,38]{0,1,2,3:T(2,128)} copy(f32[64,2,64,38]{3,2,1,0:T(8,128)} %reshape.186) | data formatting | bytes 2490368 | tf_op jit(solution)/shard_map/convert_element_type | solution.py:98
  57.6 2.9 %reshape.182 = f32[64,38,2,64]{3,2,0,1:T(2,128)S(1)} reshape(f32[64,38,128]{2,0,1:T(8,128)} %copy.74) | data formatting | bytes 2490368 | tf_op jit(solution)/shard_map/convert_element_type | solution.py:98
  60.5 4.4 %fusion.44 = f32[64,2]{0,1:T(2,128)S(1)} fusion(f32[64,2,64,38]{0,1,2,3:T(2,128)} %copy.77, f32[64,38,2,64]{3,2,0,1:T(2,128)S(1)} %reshape.182), kind=kLoop, calls=%fused_computation.77 | loop fusion | flops 622464 | bytes 2490880 | tf_op jit(solution)/shard_map/reduce_sum | solution.py:19
  65.0 2.8 %multiply_reduce_fusion = f32[64,2]{0,1:T(2,128)S(1)} fusion(f32[64,2]{0,1:T(2,128)S(1)} %broadcast_multiply_fusion.1, f32[64,2,64,38]{0,1,2,3:T(2,128)S(1)} %copy-done, f32[64,38,2,64]{3,2,0,1:T(2,128)S(1)} %reshape.182), kind=kLoop, calls=%fused_computation.16 | loop fusion | flops 1245056 | bytes 2491392 | tf_op jit(solution)/shard_map/reduce_sum | solution.py:21
  67.8 3.0 %multiply_convert_fusion = bf16[64,2,64,38]{0,1,2,3:T(2,128)(2,1)} fusion(f32[64,2]{0,1:T(2,128)S(1)} %add_rsqrt_fusion.1, f32[64,2]{0,1:T(2,128)S(1)} %broadcast_multiply_fusion.1, f32[64,2,64,38]{0,1,2,3:T(2,128)S(1)} %copy-done, f32[64,38,2,64]{3,2,0,1:T(2,128)S(1)} %reshape.182), kind=kLoop, calls=%fused_computation.15 | loop fusion | flops 1245184 | bytes 3113984 | tf_op jit(solution)/shard_map/convert_element_type | solution.py:22
  70.8 6.6 %copy.78 = bf16[64,2,64,38]{3,2,1,0:T(8,128)(2,1)} copy(bf16[64,2,64,38]{0,1,2,3:T(2,128)(2,1)} %multiply_convert_fusion) | data formatting | bytes 1245184 | tf_op jit(solution)/shard_map/convert_element_type | solution.py:22
  77.3 3.7 %convert_element_type.121 = bf16[128,2432]{1,0:T(8,128)(2,1)S(1)} reshape(bf16[64,2,64,38]{3,2,1,0:T(8,128)(2,1)} %copy.78) | data formatting | bytes 1245184 | tf_op jit(solution)/shard_map/convert_element_type | solution.py:22
  81.0 6.8 %fusion.13 = bf16[128,1800]{0,1:T(8,128)(2,1)} fusion(bf16[128,2432]{1,0:T(8,128)(2,1)S(1)} %convert_element_type.121, bf16[2,2432,1800]{1,2,0:T(8,128)(2,1)} %param.8), kind=kOutput, calls=%fused_computation.17 | convolution fusion | flops 1120896000 | bytes 9838592 | tf_op jit(solution)/shard_map/dot_general | solution.py:26
  89.7 5.1 %copy.75 = f32[64,2,64,38]{3,2,1,0:T(8,128)} copy(f32[64,2,64,38]{0,1,2,3:T(2,128)S(1)} %bitcast.83) | data formatting | bytes 2490368 | tf_op jit(solution)/shard_map/convert_element_type | solution.py:98
  94.9 3.9 %reshape.177 = f32[128,2432]{1,0:T(8,128)S(1)} reshape(f32[64,2,64,38]{3,2,1,0:T(8,128)} %copy.75) | data formatting | bytes 2490368 | tf_op jit(solution)/shard_map/convert_element_type | solution.py:98
  98.7 2.5 %fusion.7 = bf16[128,2432]{1,0:T(8,128)(2,1)S(1)} fusion(bf16[128,600]{0,1:T(8,128)(2,1)S(1)} %reshape.173, bf16[2,600,2432]{2,1,0:T(8,128)(2,1)} %param.9, f32[128,2432]{1,0:T(8,128)S(1)} %reshape.177, f32[128,2432]{1,0:T(8,128)S(1)} %copy-done.1), kind=kOutput, calls=%fused_computation.9 | convolution fusion | flops 374489088 | bytes 6184960 | tf_op jit(solution)/shard_map/dot_general | solution.py:118
  101.5 24.1 %all_to_all.15 = bf16[64,2,2432]{2,1,0:T(2,128)(2,1)S(1)} all-to-all(bf16[64,2,2432]{2,1,0:T(2,128)(2,1)S(1)} %reshape.174), channel_id=1, replica_groups=mesh['song'=2,'seq'=64] {'seq'}, dimensions={0} | all-to-all | bytes 1245184 | tf_op jit(solution)/shard_map/all_to_all | solution.py:71
  128.1 6.1 %fusion.16 = bf16[128,1800]{0,1:T(8,128)(2,1)S(1)} fusion(bf16[128,2432]{1,0:T(8,128)(2,1)S(1)} %convert_element_type.131, bf16[2,2432,1800]{1,2,0:T(8,128)(2,1)} %param.8), kind=kOutput, calls=%fused_computation.18 | convolution fusion | flops 1120896000 | bytes 9838592 | tf_op jit(solution)/shard_map/dot_general | solution.py:26
  134.5 2.0 %collective-permute-start = (bf16[128,4,300]{0,2,1:T(8,128)(2,1)S(1)}, bf16[128,4,300]{0,2,1:T(8,128)(2,1)S(1)}, u32[]{:S(2)}, u32[]{:S(2)}) collective-permute-start(bf16[128,4,300]{0,2,1:T(8,128)(2,1)S(1)} %slice.70), channel_id=1, source_target_pairs={{0,1},{1,2},{2,3},{3,4},{4,5},{5,6},{6,7},{7,8},{8,9},{9,10},{10,1... | collective-permute-start | bytes 921608 | tf_op jit(solution)/shard_map/ppermute | solution.py:125
  136.8 10.4 %collective-permute-done = bf16[128,4,300]{0,2,1:T(8,128)(2,1)S(1)} collective-permute-done((bf16[128,4,300]{0,2,1:T(8,128)(2,1)S(1)}, bf16[128,4,300]{0,2,1:T(8,128)(2,1)S(1)}, u32[]{:S(2)}, u32[]{:S(2)}) %collective-permute-start) | collective-permute-done | bytes 307232 | tf_op jit(solution)/shard_map/ppermute | solution.py:125
  147.9 3.4 %fusion.8 = bf16[128,2432]{1,0:T(8,128)(2,1)} fusion(f32[128,2432]{1,0:T(8,128)S(1)} %reshape.180, bf16[128,600]{0,1:T(8,128)(2,1)S(1)} %reshape.176, bf16[2,600,2432]{2,1,0:T(8,128)(2,1)} %param.9), kind=kOutput, calls=%fused_computation.10 | convolution fusion | flops 374177792 | bytes 4939776 | tf_op jit(solution)/shard_map/dot_general | solution.py:153
  (45 shorter events, 8.9 us)
Async XLA Ops:
  0.0 15.2 %copy-start.2 = (bf16[2048,38]{0,1:T(8,128)(2,1)S(1)}, bf16[2048,38]{0,1:T(8,128)(2,1)}, u32[]{:S(2)}) copy-start(bf16[2048,38]{0,1:T(8,128)(2,1)} %param.6) | copy-start | bytes 466948
  4.1 25.4 %all-to-all-start = ((bf16[64,2,2560]{2,1,0:T(2,128)(2,1)}), bf16[64,2,2560]{2,1,0:T(2,128)(2,1)S(1)}, u32[]{:S(2)}, u32[]{:S(2)}) async-start(bf16[64,2,2560]{2,1,0:T(2,128)(2,1)} %pad_maximum_fusion), calls=%async_computation | async-start | bytes 1310720 | tf_op jit(solution)/shard_map/all_to_all | solution.py:71
  33.8 22.6 %all-to-all-start.1 = ((bf16[64,38,128]{2,1,0:T(8,128)(2,1)}), bf16[64,38,128]{2,1,0:T(8,128)(2,1)S(1)}, u32[]{:S(2)}, u32[]{:S(2)}) async-start(bf16[64,38,128]{2,1,0:T(8,128)(2,1)} %shard_map.55), calls=%async_computation.1 | async-start | bytes 1310720 | tf_op jit(solution)/shard_map/all_to_all | solution.py:71
  60.5 4.4 %copy-start = (f32[64,2,64,38]{0,1,2,3:T(2,128)S(1)}, f32[64,2,64,38]{0,1,2,3:T(2,128)}, u32[]{:S(2)}) copy-start(f32[64,2,64,38]{0,1,2,3:T(2,128)} %copy.77) | copy-start | bytes 3735556
  94.9 3.9 %copy-start.1 = (f32[128,2432]{1,0:T(8,128)S(1)}, f32[128,2432]{1,0:T(8,128)}, u32[]{:S(2)}) copy-start(f32[128,2432]{1,0:T(8,128)} %reshape.178) | copy-start | bytes 3735556
  134.5 12.7 %collective-permute-start = (bf16[128,4,300]{0,2,1:T(8,128)(2,1)S(1)}, bf16[128,4,300]{0,2,1:T(8,128)(2,1)S(1)}, u32[]{:S(2)}, u32[]{:S(2)}) collective-permute-start(bf16[128,4,300]{0,2,1:T(8,128)(2,1)S(1)} %slice.70), channel_id=1, source_target_pairs={{0,1},{1,2},{2,3},{3,4},{4,5},{5,6},{6,7},{7,8},{8,9},{9,10},{10,1... | collective-permute-start | bytes 921608 | tf_op jit(solution)/shard_map/ppermute | solution.py:125

commit v2 on v1

v2 whole, which is shorter than its diff:
```python
import functools
import math

import jax
import jax.numpy as jnp
from jax import lax
from jax.experimental import pallas as pl
from jax.experimental.pallas import tpu as pltpu
from jax.sharding import PartitionSpec as P

HEADS = 4
HEAD = 150
GROUPS = 8
DIGIT = 64
STRIPS = 4
VMEM_LIMIT = 32 * 1024 * 1024
WEIGHTS = pltpu.HBM

epsilon = 1e-05


def normalize(x_ref, normed_ref):
    width = x_ref.shape[1]
    blocks = [slice(i, min(i + 128, width)) for i in range(0, width, 128)]
    total = sum(x_ref[:, b] for b in blocks)
    mean = jnp.sum(total, axis=1, keepdims=True) * (1.0 / width)
    total = jnp.zeros_like(total)
    for b in blocks:
        centered = x_ref[:, b] - mean
        total += centered * centered
    scale = lax.rsqrt(jnp.sum(total, axis=1, keepdims=True) * (1.0 / width) + epsilon)
    for b in blocks:
        normed_ref[:, b] = ((x_ref[:, b] - mean) * scale).astype(jnp.bfloat16)


def strips(count):
    step = -(-count // (STRIPS * 128)) * 128
    return [(i, min(i + step, count)) for i in range(0, count, step)]


def fetches(layer, w_in_hbm, w_out_hbm, w_in_ref, w_out_ref, sem):
    parts = strips(w_in_hbm.shape[1])
    copies = [
        pltpu.make_async_copy(w_in_hbm.at[layer, lo:hi], w_in_ref.at[lo:hi], sem.at[i])
        for i, (lo, hi) in enumerate(parts)
    ]
    if w_out_hbm is not None:
        copies.append(pltpu.make_async_copy(w_out_hbm.at[layer], w_out_ref, sem.at[len(parts)]))
    return copies


def project_strips(normed_ref, w_in_ref, joined_ref, copies):
    for (lo, hi), copy in zip(strips(w_in_ref.shape[0]), copies):
        copy.wait()
        joined_ref[:, lo:hi] = lax.dot_general(
            normed_ref[...],
            w_in_ref[lo:hi],
            (((1,), (1,)), ((), ())),
            preferred_element_type=jnp.float32,
        ).astype(jnp.bfloat16)


def column_kernel(
    found_ref, got_ref, w_in_hbm, w_out_hbm, out_ref,
    flat_ref, x_ref, normed_ref, joined_ref, w_in_ref, w_out_ref, sem,
):
    rows, depth, tokens = found_ref.shape
    per = out_ref.shape[1]
    width = out_ref.shape[2]
    copies = fetches(0, w_in_hbm, w_out_hbm, w_in_ref, w_out_ref, sem)
    for copy in copies:
        copy.start()
    for s in range(rows):
        flat_ref[s * depth : (s + 1) * depth] = found_ref[s].astype(jnp.float32)
    for r in range(rows):
        x_ref[r * per : (r + 1) * per] = got_ref[r, :, :width].astype(jnp.float32)
    for i in range(0, width, 128):
        x_ref[:, i : i + 128] += jnp.transpose(flat_ref[i : i + 128])
    normalize(x_ref, normed_ref)
    project_strips(normed_ref, w_in_ref, joined_ref, copies)
    joined = joined_ref[...]
    row_of = lax.broadcasted_iota(jnp.int32, (tokens, tokens), 0)
    col_of = lax.broadcasted_iota(jnp.int32, (tokens, tokens), 1)
    allowed = (row_of % per == col_of % per) & (row_of >= col_of)
    pieces = []
    for h in range(HEADS):
        base = 3 * HEAD * h
        query = joined[:, base : base + HEAD]
        key = joined[:, base + HEAD : base + 2 * HEAD]
        value = joined[:, base + 2 * HEAD : base + 3 * HEAD]
        scores = lax.dot_general(
            query, key, (((1,), (1,)), ((), ())), preferred_element_type=jnp.float32
        ) * (1.0 / math.sqrt(HEAD))
        scores = jnp.where(allowed, scores, -jnp.inf)
        lifted = jnp.exp(scores - jnp.max(scores, axis=1, keepdims=True))
        probs = (lifted / jnp.sum(lifted, axis=1, keepdims=True)).astype(jnp.bfloat16)
        pieces.append(
            jnp.dot(probs, value, preferred_element_type=jnp.float32).astype(jnp.bfloat16)
        )
    mixed = jnp.concatenate(pieces, axis=1)
    copies[-1].wait()
    normed_ref[...] = (
        x_ref[...] + jnp.dot(mixed, w_out_ref[...], preferred_element_type=jnp.float32)
    ).astype(jnp.bfloat16)
    for r in range(rows):
        out_ref[r] = normed_ref[r * per : (r + 1) * per]


def column_sublayer(found, got, w_in, w_out):
    rows, depth, tokens = found.shape
    joint, width = w_in.shape[1:]
    per = tokens // rows
    return pl.pallas_call(
        column_kernel,
        out_shape=jax.ShapeDtypeStruct((rows, per, width), jnp.bfloat16),
        in_specs=[pl.BlockSpec(memory_space=pltpu.VMEM)] * 2
        + [pl.BlockSpec(memory_space=WEIGHTS)] * 2,
        out_specs=pl.BlockSpec(memory_space=pltpu.VMEM),
        scratch_shapes=[
            pltpu.VMEM((width, tokens), jnp.float32),
            pltpu.VMEM((tokens, width), jnp.float32),
            pltpu.VMEM((tokens, width), jnp.bfloat16),
            pltpu.VMEM((tokens, joint), jnp.bfloat16),
            pltpu.VMEM((joint, width), jnp.bfloat16),
            pltpu.VMEM(w_out.shape[1:], jnp.bfloat16),
            pltpu.SemaphoreType.DMA((STRIPS + 1,)),
        ],
        compiler_params=pltpu.CompilerParams(vmem_limit_bytes=VMEM_LIMIT),
    )(found, got, w_in, w_out)


def project_kernel(resid_ref, w_in_hbm, own_ref, sent_ref, x_ref, normed_ref, w_in_ref, sem):
    rows, per, width = resid_ref.shape
    copies = fetches(1, w_in_hbm, None, w_in_ref, None, sem)
    for copy in copies:
        copy.start()
    for r in range(rows):
        x_ref[r * per : (r + 1) * per] = resid_ref[r].astype(jnp.float32)
    normalize(x_ref, normed_ref)
    project_strips(normed_ref, w_in_ref, own_ref, copies)
    joined = own_ref[...]
    sent_ref[...] = jnp.concatenate(
        [joined[:, 3 * HEAD * h + HEAD : 3 * HEAD * (h + 1)] for h in range(HEADS)], axis=1
    )


def project(resid, w_in):
    rows, per, width = resid.shape
    tokens = rows * per
    return pl.pallas_call(
        project_kernel,
        out_shape=(
            jax.ShapeDtypeStruct((tokens, 3 * HEADS * HEAD), jnp.bfloat16),
            jax.ShapeDtypeStruct((tokens, 2 * HEADS * HEAD), jnp.bfloat16),
            jax.ShapeDtypeStruct((tokens, width), jnp.float32),
        ),
        in_specs=[pl.BlockSpec(memory_space=pltpu.VMEM), pl.BlockSpec(memory_space=WEIGHTS)],
        out_specs=(pl.BlockSpec(memory_space=pltpu.VMEM),) * 3,
        scratch_shapes=[
            pltpu.VMEM((tokens, width), jnp.bfloat16),
            pltpu.VMEM(w_in.shape[1:], jnp.bfloat16),
            pltpu.SemaphoreType.DMA((STRIPS,)),
        ],
        compiler_params=pltpu.CompilerParams(vmem_limit_bytes=VMEM_LIMIT),
    )(resid, w_in)


def row_kernel(own_ref, before_ref, x_ref, w_out_hbm, out_ref, w_out_ref, sem):
    has_before = lax.axis_index("seq") > 0
    copy = pltpu.make_async_copy(w_out_hbm.at[1], w_out_ref, sem)
    copy.start()
    inv_root = 1.0 / math.sqrt(HEAD)
    joined = own_ref[...]
    before = before_ref[...]
    pieces = []
    for h in range(HEADS):
        base = 3 * HEAD * h
        query = joined[:, base : base + HEAD]
        key = joined[:, base + HEAD : base + 2 * HEAD].astype(jnp.float32)
        value = joined[:, base + 2 * HEAD : base + 3 * HEAD].astype(jnp.float32)
        far_key = before[:, 2 * HEAD * h : 2 * HEAD * h + HEAD]
        far_value = before[:, 2 * HEAD * h + HEAD : 2 * HEAD * (h + 1)]
        far_scores = (
            lax.dot_general(
                query, far_key, (((1,), (1,)), ((), ())), preferred_element_type=jnp.float32
            )
            * inv_root
        )
        far_scores = jnp.where(has_before, far_scores, -jnp.inf)
        own_scores = jnp.sum(query.astype(jnp.float32) * key, axis=1, keepdims=True) * inv_root
        top_score = jnp.maximum(jnp.max(far_scores, axis=1, keepdims=True), own_scores)
        far_lifted = jnp.exp(far_scores - top_score)
        own_lifted = jnp.exp(own_scores - top_score)
        total = jnp.sum(far_lifted, axis=1, keepdims=True) + own_lifted
        far_probs = (far_lifted / total).astype(jnp.bfloat16)
        own_probs = (own_lifted / total).astype(jnp.bfloat16).astype(jnp.float32)
        far_part = jnp.dot(far_probs, far_value, preferred_element_type=jnp.float32)
        pieces.append((far_part + own_probs * value).astype(jnp.bfloat16))
    mixed = jnp.concatenate(pieces, axis=1)
    copy.wait()
    out_ref[...] = (
        x_ref[...] + jnp.dot(mixed, w_out_ref[...], preferred_element_type=jnp.float32)
    ).astype(jnp.bfloat16)


def row_sublayer(own, before, x, w_out):
    return pl.pallas_call(
        row_kernel,
        out_shape=jax.ShapeDtypeStruct(x.shape, jnp.bfloat16),
        in_specs=[pl.BlockSpec(memory_space=pltpu.VMEM)] * 3
        + [pl.BlockSpec(memory_space=WEIGHTS)],
        out_specs=pl.BlockSpec(memory_space=pltpu.VMEM),
        scratch_shapes=[
            pltpu.VMEM(w_out.shape[1:], jnp.bfloat16),
            pltpu.SemaphoreType.DMA(()),
        ],
        compiler_params=pltpu.CompilerParams(vmem_limit_bytes=VMEM_LIMIT),
    )(own, before, x, w_out)


def lookup_kernel(codes_ref, table_ref, out_ref):
    depth, entries = table_ref.shape
    step = entries // GROUPS
    count = out_ref.shape[0]
    padded = (depth + 7) // 8 * 8
    flipped = jnp.concatenate(
        [table_ref[...].astype(jnp.float32), jnp.zeros((padded - depth, entries), jnp.float32)],
        axis=0,
    )
    stacked = jnp.concatenate(
        [flipped[:, g * step : (g + 1) * step] for g in range(GROUPS)], axis=0
    ).astype(jnp.bfloat16)
    slots = lax.broadcasted_iota(jnp.int32, (step, 128), 0)
    for d in range(count):
        codes = codes_ref[d : d + 1, :]
        low = codes % step
        high = codes // step
        onehot = jnp.where(slots == low, 1.0, 0.0).astype(jnp.bfloat16)
        found = jnp.dot(stacked, onehot, preferred_element_type=jnp.float32)
        chosen = jnp.zeros((padded, 128), jnp.float32)
        for g in range(GROUPS):
            chosen = jnp.where(high == g, found[g * padded : (g + 1) * padded], chosen)
        out_ref[d] = chosen[:depth].astype(jnp.bfloat16)


def lookup(codes, table):
    count = codes.shape[0]
    depth = table.shape[0]
    return pl.pallas_call(
        lookup_kernel,
        out_shape=jax.ShapeDtypeStruct((count, depth, 128), jnp.bfloat16),
        in_specs=[pl.BlockSpec(memory_space=pltpu.VMEM)] * 2,
        out_specs=pl.BlockSpec(memory_space=pltpu.VMEM),
        compiler_params=pltpu.CompilerParams(vmem_limit_bytes=16 * 1024 * 1024),
    )(codes, table)


def pack_kernel(codes_ref, position_ref, out_ref):
    rows, per, _ = out_ref.shape
    width = position_ref.shape[1]
    codes = codes_ref[...]
    digits = jnp.concatenate([codes // DIGIT, codes % DIGIT], axis=0).astype(jnp.bfloat16)
    for r in range(rows):
        out_ref[r, :, :width] = position_ref[r * per : (r + 1) * per]
        out_ref[r, :, width:] = digits


def pack(song_ids, position_table, rows):
    tokens, width = position_table.shape
    return pl.pallas_call(
        pack_kernel,
        out_shape=jax.ShapeDtypeStruct((rows, tokens // rows, width + tokens), jnp.bfloat16),
        in_specs=[pl.BlockSpec(memory_space=pltpu.VMEM)] * 2,
        out_specs=pl.BlockSpec(memory_space=pltpu.VMEM),
        compiler_params=pltpu.CompilerParams(vmem_limit_bytes=VMEM_LIMIT),
    )(song_ids.reshape(1, tokens), position_table)


def exchange(value):
    return lax.all_to_all(value, "seq", split_axis=0, concat_axis=0, tiled=True)


def shards(song_ids, table, position_table, w_qkv, w_out):
    rows = lax.axis_size("seq")
    tokens, width = position_table.shape
    per = tokens // rows

    got = exchange(pack(song_ids, position_table, rows))
    codes = got[:, 0, width:].astype(jnp.int32) * DIGIT + got[:, 1, width:].astype(jnp.int32)
    codes = jnp.transpose(codes.reshape(rows, rows, per), (1, 0, 2)).reshape(rows, tokens)
    found = exchange(lookup(codes, jnp.transpose(table)))
    w_in = jnp.swapaxes(w_qkv, 1, 2)
    resid = exchange(column_sublayer(found, got, w_in, w_out))
    own, sent, x = project(resid, w_in)
    before = lax.ppermute(sent, "seq", [(i, i + 1) for i in range(rows - 1)])
    return row_sublayer(own, before, x, w_out)


def solution(mesh):
    in_specs = (P(("song", "seq")), P(None, "seq"), P("seq", None), P(), P())
    out_specs = P(("song", "seq"), None)
    return jax.shard_map(shards, mesh=mesh, in_specs=in_specs, out_specs=out_specs, check_vma=False)
```

time: 152 us -> 110 us (0.72)
  blocking collectives: 24.1 us -> 64.6 us
  local copies, waits for them, and re-layouts: 44.4 us -> 11.6 us
  matrix products: 19.9 us -> 0 us
  starting transfers between devices: 18.9 us -> 2.03 us
  Pallas kernels: 3.88 us -> 20.6 us
  other arithmetic: 15.4 us -> 0.11 us
  waiting for transfers between devices: 24.3 us -> 10.9 us
    all_to_all x1 -> x3, blocking collectives: 24.1 us -> 64.6 us  [exchange(): return lax.all_to_all(value, 'seq', split_axis=0, concat_axis=0, tiled=True)]
    convert_element_type x11 -> x0, local copies, waits for them, and re-layouts: 40.1 us -> none  [the longest x7 29.4 us: shards(): residual = embedded.astype(jnp.float32) + position.astype(jnp.float32)]
    dot_general x8 -> x0, matrix products: 19.9 us -> none  [the longest x2 12.9 us: project(): jnp.dot(normalize(residual), weight, preferred_element_type=jnp.float32)]
    pallas_call x0 -> x4, Pallas kernels: none -> 17.6 us  [the longest x1 7.49 us: column_sublayer(): pl.pallas_call(column_kernel, out_shape=jax.ShapeDtypeStruct((rows, per,...]
    all_to_all x2 -> x0, starting transfers between devices: 16.9 us -> none  [exchange(): return lax.all_to_all(value, 'seq', split_axis=0, concat_axis=0, tiled=True)]
    all_to_all x2 -> x0, waiting for transfers between devices: 13.9 us -> none  [exchange(): return lax.all_to_all(value, 'seq', split_axis=0, concat_axis=0, tiled=True)]
    unnamed x9 -> x14, local copies, waits for them, and re-layouts: 0.55 us -> 11.3 us
    reduce_sum x5 -> x0, other arithmetic: 8.79 us -> none  [the longest x2 4.99 us: normalize(): center_mean = jnp.mean(residual, axis=-1, keepdims=True)]
  transfers between devices with their start and end apart: 3 -> 1, of which waited for: 2 -> 1; matrix products, arithmetic and copies ran while one was open for 11% -> 0% of each run, Pallas kernels for 0% -> 0%
where the time goes in v2:
time: 110 us
  blocking collectives  64.6 us (59%)
  Pallas kernels  20.6 us (19%)
  local copies, waits for them, and re-layouts  11.6 us (11%)
  waiting for transfers between devices  10.9 us (10%)
  starting transfers between devices  2.03 us (2%)
    all_to_all x3, blocking collectives, exchange(): return lax.all_to_all(value, 'seq', split_axis=0, concat_axis=0, tiled=True)  64.6 us
    unnamed x14, local copies, waits for them, and re-layouts  11.3 us
    ppermute x1, waiting for transfers between devices, shards(): before = lax.ppermute(sent, 'seq', [(i, i + 1) for i in range(rows - 1)])  10.9 us
    pallas_call x1, Pallas kernels, column_sublayer(): pl.pallas_call(column_kernel, out_shape=jax.ShapeDtypeStruct((rows, per,...  7.49 us
    pallas_call x1, Pallas kernels, project(): pl.pallas_call(project_kernel, out_shape=(jax.ShapeDtypeStruct((tokens, 3...  5.89 us
    pallas_call x1, Pallas kernels, row_sublayer(): pl.pallas_call(row_kernel, out_shape=jax.ShapeDtypeStruct(x.shape, jnp.bf...  3.9 us
    pallas_call x1, Pallas kernels, lookup(): pl.pallas_call(lookup_kernel, out_shape=jax.ShapeDtypeStruct((count, dept...  2.92 us
  transfers between devices with their start and end apart: 1, of which 1 were waited for; matrix products, arithmetic and copies ran while one was open for 0% of the time, Pallas kernels for 0%

profile of v2, /device:TPU:32, one launch (start us, length us, event | category | flops | bytes accessed | tf_op | source)
XLA Modules:
  0.0 109.9 jit_solution(5129787758119076607)
XLA Ops:
  0.0 0.0 copy-start.2
  0.0 1.1 copy-done.2
  1.1 0.7 copy-done.4
  1.7 0.4 shard_map.55
  2.1 0.0 slice-start
  2.1 25.3 %all_to_all.15.got_ref = bf16[64,2,2560]{2,1,0:T(2,128)(2,1)S(1)} all-to-all(bf16[64,2,2560]{2,1,0:T(2,128)(2,1)S(1)} %shard_map.55), channel_id=1, replica_groups=mesh['song'=2,'seq'=64] {'seq'}, dimensions={0} | all-to-all | bytes 1310720 | tf_op jit(solution)/shard_map/all_to_all | solution.py:280
  27.4 0.1 fusion
  27.5 0.1 copy.10
  27.6 0.1 copy.11
  27.7 0.1 copy.12.codes_ref
  27.8 0.0 copy-start.3
  27.8 0.9 copy-done.3
  28.7 2.9 %shard_map.56 = bf16[64,38,128]{2,1,0:T(8,128)(2,1)S(1)} custom-call(s32[64,128]{1,0:T(8,128)S(1)} %copy.12.codes_ref, bf16[38,2048]{1,0:T(8,128)(2,1)S(1)} %bitcast.11), custom_call_target="tpu_custom_call" | custom-call | tf_op jit(solution)/shard_map/pallas_call | solution.py:249
  31.7 19.8 %all_to_all.16.found_ref = bf16[64,38,128]{2,1,0:T(8,128)(2,1)S(1)} all-to-all(bf16[64,38,128]{2,1,0:T(8,128)(2,1)S(1)} %shard_map.56), channel_id=1, replica_groups=mesh['song'=2,'seq'=64] {'seq'}, dimensions={0} | all-to-all | bytes 1245184 | tf_op jit(solution)/shard_map/all_to_all | solution.py:280
  51.5 2.7 %copy-done.1 = bf16[2,600,2432]{2,1,0:T(8,128)(2,1)S(1)} copy-done((bf16[2,600,2432]{2,1,0:T(8,128)(2,1)S(1)}, bf16[2,600,2432]{2,1,0:T(8,128)(2,1)}, u32[]{:S(2)}) %copy-start.1) | copy-done | bytes 5836824
  54.1 7.5 %shard_map.57 = bf16[64,2,2432]{2,1,0:T(2,128)(2,1)S(1)} custom-call(bf16[64,38,128]{2,1,0:T(8,128)(2,1)S(1)} %all_to_all.16.found_ref, bf16[64,2,2560]{2,1,0:T(2,128)(2,1)S(1)} %all_to_all.15.got_ref, bf16[2,1800,2432]{2,1,0:T(8,128)(2,1)} %bitcast.7, bf16[2,600,2432]{2,1,0:T(8,128)(2,1)S(1)} %copy-done.1), custom_call_target="tpu_custom_call" | custom-call | tf_op jit(solution)/shard_map/pallas_call | solution.py:113
  61.6 19.5 %all_to_all.17.resid_ref = bf16[64,2,2432]{2,1,0:T(2,128)(2,1)S(1)} all-to-all(bf16[64,2,2432]{2,1,0:T(2,128)(2,1)S(1)} %shard_map.57), channel_id=1, replica_groups=mesh['song'=2,'seq'=64] {'seq'}, dimensions={0} | all-to-all | bytes 1245184 | tf_op jit(solution)/shard_map/all_to_all | solution.py:280
  81.1 6.0 %copy-done = bf16[2,2432,1800]{1,2,0:T(8,128)(2,1)S(1)} copy-done((bf16[2,2432,1800]{1,2,0:T(8,128)(2,1)S(1)}, bf16[2,2432,1800]{1,2,0:T(8,128)(2,1)}, u32[]{:S(2)}) %copy-start) | copy-done | bytes 17510424
  87.1 5.9 %shard_map.58 = (bf16[128,1800]{1,0:T(8,128)(2,1)S(1)}, bf16[128,1200]{1,0:T(8,128)(2,1)S(1)}, f32[128,2432]{1,0:T(8,128)S(1)}) custom-call(bf16[64,2,2432]{2,1,0:T(2,128)(2,1)S(1)} %all_to_all.17.resid_ref, bf16[2,1800,2432]{2,1,0:T(8,128)(2,1)S(1)} %bitcast.8), custom_call_target="tpu_custom_call" | custom-call | tf_op jit(solution)/shard_map/pallas_call | solution.py:150
  93.0 2.0 %collective-permute-start = (bf16[128,1200]{1,0:T(8,128)(2,1)S(1)}, bf16[128,1200]{1,0:T(8,128)(2,1)S(1)}, u32[]{:S(2)}, u32[]{:S(2)}) collective-permute-start(bf16[128,1200]{1,0:T(8,128)(2,1)S(1)} %get-tuple-element.9), channel_id=1, source_target_pairs={{0,1},{1,2},{2,3},{3,4},{4,5},{5,6},{6,7},{7,8},{8,9},{9,10},{10,1... | collective-permute-start | bytes 921608 | tf_op jit(solution)/shard_map/ppermute | solution.py:295
  95.0 10.9 %collective-permute-done.before_ref = bf16[128,1200]{1,0:T(8,128)(2,1)S(1)} collective-permute-done((bf16[128,1200]{1,0:T(8,128)(2,1)S(1)}, bf16[128,1200]{1,0:T(8,128)(2,1)S(1)}, u32[]{:S(2)}, u32[]{:S(2)}) %collective-permute-start) | collective-permute-done | bytes 307232 | tf_op jit(solution)/shard_map/ppermute | solution.py:295
  105.9 0.0 slice-done
  105.9 0.0 slice-done.1
  105.9 3.9 %shard_map.59 = bf16[128,2432]{1,0:T(8,128)(2,1)} custom-call(bf16[128,1800]{1,0:T(8,128)(2,1)S(1)} %get-tuple-element.8.own_ref, bf16[128,1200]{1,0:T(8,128)(2,1)S(1)} %collective-permute-done.before_ref, f32[128,2432]{1,0:T(8,128)S(1)} %get-tuple-element.10.x_ref, bf16[2,600,2432]{2,1,0:T(8,128)(2,1)S(1)} %bitcast.10), custom_call_target="tpu_custom_call" | custom-call | tf_op jit(solution)/shard_map/pallas_call | solution.py:207
  (5 shorter events, 0.0 us)
Async XLA Ops:
  0.0 1.1 copy-start.2
  1.1 0.7 copy-start.4
  2.1 103.8 %slice-start = ((s8[5836800]{0:T(1024)(128)(4,1)}), s8[1642496]{0:T(1024)(128)(4,1)S(1)}, s32[]{:S(2)}) async-start(s8[5836800]{0:T(1024)(128)(4,1)} %bitcast.9), calls=%async_computation.3 | async-start | bytes 3284992
  27.8 0.9 copy-start.3
  51.5 2.7 %copy-start.1 = (bf16[2,600,2432]{2,1,0:T(8,128)(2,1)S(1)}, bf16[2,600,2432]{2,1,0:T(8,128)(2,1)}, u32[]{:S(2)}) copy-start(bf16[2,600,2432]{2,1,0:T(8,128)(2,1)} %w_out_hbm.3) | copy-start | bytes 17510404
  54.1 51.8 %slice-start.1 = ((s8[5836800]{0:T(1024)(128)(4,1)}), s8[4194304]{0:T(1024)(128)(4,1)S(1)}, s32[]{:S(2)}) async-start(s8[5836800]{0:T(1024)(128)(4,1)} %bitcast.9), calls=%async_computation.4 | async-start | bytes 8388608
  81.1 6.0 %copy-start = (bf16[2,2432,1800]{1,2,0:T(8,128)(2,1)S(1)}, bf16[2,2432,1800]{1,2,0:T(8,128)(2,1)}, u32[]{:S(2)}) copy-start(bf16[2,2432,1800]{1,2,0:T(8,128)(2,1)} %param.8) | copy-start | bytes 52531204
  93.0 12.9 %collective-permute-start = (bf16[128,1200]{1,0:T(8,128)(2,1)S(1)}, bf16[128,1200]{1,0:T(8,128)(2,1)S(1)}, u32[]{:S(2)}, u32[]{:S(2)}) collective-permute-start(bf16[128,1200]{1,0:T(8,128)(2,1)S(1)} %get-tuple-element.9), channel_id=1, source_target_pairs={{0,1},{1,2},{2,3},{3,4},{4,5},{5,6},{6,7},{7,8},{8,9},{9,10},{10,1... | collective-permute-start | bytes 921608 | tf_op jit(solution)/shard_map/ppermute | solution.py:295

commit v3 on v2

--- a/solution.py
+++ b/solution.py
@@ -12,9 +12,7 @@
 HEAD = 150
 GROUPS = 8
 DIGIT = 64
-STRIPS = 4
-VMEM_LIMIT = 32 * 1024 * 1024
-WEIGHTS = pltpu.HBM
+VMEM_LIMIT = 12 * 1024 * 1024
 
 epsilon = 1e-05
 
@@ -33,43 +31,22 @@
         normed_ref[:, b] = ((x_ref[:, b] - mean) * scale).astype(jnp.bfloat16)
 
 
-def strips(count):
-    step = -(-count // (STRIPS * 128)) * 128
-    return [(i, min(i + step, count)) for i in range(0, count, step)]
-
-
-def fetches(layer, w_in_hbm, w_out_hbm, w_in_ref, w_out_ref, sem):
-    parts = strips(w_in_hbm.shape[1])
-    copies = [
-        pltpu.make_async_copy(w_in_hbm.at[layer, lo:hi], w_in_ref.at[lo:hi], sem.at[i])
-        for i, (lo, hi) in enumerate(parts)
-    ]
-    if w_out_hbm is not None:
-        copies.append(pltpu.make_async_copy(w_out_hbm.at[layer], w_out_ref, sem.at[len(parts)]))
-    return copies
-
-
-def project_strips(normed_ref, w_in_ref, joined_ref, copies):
-    for (lo, hi), copy in zip(strips(w_in_ref.shape[0]), copies):
-        copy.wait()
-        joined_ref[:, lo:hi] = lax.dot_general(
-            normed_ref[...],
-            w_in_ref[lo:hi],
-            (((1,), (1,)), ((), ())),
-            preferred_element_type=jnp.float32,
-        ).astype(jnp.bfloat16)
-
-
-def column_kernel(
-    found_ref, got_ref, w_in_hbm, w_out_hbm, out_ref,
-    flat_ref, x_ref, normed_ref, joined_ref, w_in_ref, w_out_ref, sem,
-):
+def joint(normed_ref, weight):
+    return lax.dot_general(
+        normed_ref[...], weight, (((1,), (1,)), ((), ())), preferred_element_type=jnp.float32
+    ).astype(jnp.bfloat16)
+
+
+def hint(microseconds):
+    return pl.CostEstimate(
+        flops=int(microseconds * 1e9), bytes_accessed=int(microseconds * 3e6), transcendentals=0
+    )
+
+
+def column_kernel(found_ref, got_ref, w_in_ref, w_out_ref, out_ref, flat_ref, x_ref, normed_ref):
     rows, depth, tokens = found_ref.shape
     per = out_ref.shape[1]
     width = out_ref.shape[2]
-    copies = fetches(0, w_in_hbm, w_out_hbm, w_in_ref, w_out_ref, sem)
-    for copy in copies:
-        copy.start()
     for s in range(rows):
         flat_ref[s * depth : (s + 1) * depth] = found_ref[s].astype(jnp.float32)
     for r in range(rows):
@@ -77,8 +54,7 @@
     for i in range(0, width, 128):
         x_ref[:, i : i + 128] += jnp.transpose(flat_ref[i : i + 128])
     normalize(x_ref, normed_ref)
-    project_strips(normed_ref, w_in_ref, joined_ref, copies)
-    joined = joined_ref[...]
+    joined = joint(normed_ref, w_in_ref[0])
     row_of = lax.broadcasted_iota(jnp.int32, (tokens, tokens), 0)
     col_of = lax.broadcasted_iota(jnp.int32, (tokens, tokens), 1)
     allowed = (row_of % per == col_of % per) & (row_of >= col_of)
@@ -98,9 +74,8 @@
             jnp.dot(probs, value, preferred_element_type=jnp.float32).astype(jnp.bfloat16)
         )
     mixed = jnp.concatenate(pieces, axis=1)
-    copies[-1].wait()
     normed_ref[...] = (
-        x_ref[...] + jnp.dot(mixed, w_out_ref[...], preferred_element_type=jnp.float32)
+        x_ref[...] + jnp.dot(mixed, w_out_ref[0], preferred_element_type=jnp.float32)
     ).astype(jnp.bfloat16)
     for r in range(rows):
         out_ref[r] = normed_ref[r * per : (r + 1) * per]
@@ -108,37 +83,30 @@
 
 def column_sublayer(found, got, w_in, w_out):
     rows, depth, tokens = found.shape
-    joint, width = w_in.shape[1:]
+    width = w_in.shape[2]
     per = tokens // rows
     return pl.pallas_call(
         column_kernel,
         out_shape=jax.ShapeDtypeStruct((rows, per, width), jnp.bfloat16),
-        in_specs=[pl.BlockSpec(memory_space=pltpu.VMEM)] * 2
-        + [pl.BlockSpec(memory_space=WEIGHTS)] * 2,
+        in_specs=[pl.BlockSpec(memory_space=pltpu.VMEM)] * 4,
         out_specs=pl.BlockSpec(memory_space=pltpu.VMEM),
         scratch_shapes=[
             pltpu.VMEM((width, tokens), jnp.float32),
             pltpu.VMEM((tokens, width), jnp.float32),
             pltpu.VMEM((tokens, width), jnp.bfloat16),
-            pltpu.VMEM((tokens, joint), jnp.bfloat16),
-            pltpu.VMEM((joint, width), jnp.bfloat16),
-            pltpu.VMEM(w_out.shape[1:], jnp.bfloat16),
-            pltpu.SemaphoreType.DMA((STRIPS + 1,)),
         ],
+        cost_estimate=hint(20),
         compiler_params=pltpu.CompilerParams(vmem_limit_bytes=VMEM_LIMIT),
     )(found, got, w_in, w_out)
 
 
-def project_kernel(resid_ref, w_in_hbm, own_ref, sent_ref, x_ref, normed_ref, w_in_ref, sem):
+def project_kernel(resid_ref, w_in_ref, own_ref, sent_ref, x_ref, normed_ref):
     rows, per, width = resid_ref.shape
-    copies = fetches(1, w_in_hbm, None, w_in_ref, None, sem)
-    for copy in copies:
-        copy.start()
     for r in range(rows):
         x_ref[r * per : (r + 1) * per] = resid_ref[r].astype(jnp.float32)
     normalize(x_ref, normed_ref)
-    project_strips(normed_ref, w_in_ref, own_ref, copies)
-    joined = own_ref[...]
+    joined = joint(normed_ref, w_in_ref[1])
+    own_ref[...] = joined
     sent_ref[...] = jnp.concatenate(
         [joined[:, 3 * HEAD * h + HEAD : 3 * HEAD * (h + 1)] for h in range(HEADS)], axis=1
     )
@@ -154,21 +122,18 @@
             jax.ShapeDtypeStruct((tokens, 2 * HEADS * HEAD), jnp.bfloat16),
             jax.ShapeDtypeStruct((tokens, width), jnp.float32),
         ),
-        in_specs=[pl.BlockSpec(memory_space=pltpu.VMEM), pl.BlockSpec(memory_space=WEIGHTS)],
+        in_specs=[pl.BlockSpec(memory_space=pltpu.VMEM)] * 2,
         out_specs=(pl.BlockSpec(memory_space=pltpu.VMEM),) * 3,
         scratch_shapes=[
             pltpu.VMEM((tokens, width), jnp.bfloat16),
-            pltpu.VMEM(w_in.shape[1:], jnp.bfloat16),
-            pltpu.SemaphoreType.DMA((STRIPS,)),
         ],
+        cost_estimate=hint(20),
         compiler_params=pltpu.CompilerParams(vmem_limit_bytes=VMEM_LIMIT),
     )(resid, w_in)
 
 
-def row_kernel(own_ref, before_ref, x_ref, w_out_hbm, out_ref, w_out_ref, sem):
+def row_kernel(own_ref, before_ref, x_ref, w_out_ref, out_ref):
     has_before = lax.axis_index("seq") > 0
-    copy = pltpu.make_async_copy(w_out_hbm.at[1], w_out_ref, sem)
-    copy.start()
     inv_root = 1.0 / math.sqrt(HEAD)
     joined = own_ref[...]
     before = before_ref[...]
@@ -197,9 +162,8 @@
         far_part = jnp.dot(far_probs, far_value, preferred_element_type=jnp.float32)
         pieces.append((far_part + own_probs * value).astype(jnp.bfloat16))
     mixed = jnp.concatenate(pieces, axis=1)
-    copy.wait()
     out_ref[...] = (
-        x_ref[...] + jnp.dot(mixed, w_out_ref[...], preferred_element_type=jnp.float32)
+        x_ref[...] + jnp.dot(mixed, w_out_ref[1], preferred_element_type=jnp.float32)
     ).astype(jnp.bfloat16)
 
 
@@ -207,13 +171,9 @@
     return pl.pallas_call(
         row_kernel,
         out_shape=jax.ShapeDtypeStruct(x.shape, jnp.bfloat16),
-        in_specs=[pl.BlockSpec(memory_space=pltpu.VMEM)] * 3
-        + [pl.BlockSpec(memory_space=WEIGHTS)],
-        out_specs=pl.BlockSpec(memory_space=pltpu.VMEM),
-        scratch_shapes=[
-            pltpu.VMEM(w_out.shape[1:], jnp.bfloat16),
-            pltpu.SemaphoreType.DMA(()),
-        ],
+        in_specs=[pl.BlockSpec(memory_space=pltpu.VMEM)] * 4,
+        out_specs=pl.BlockSpec(memory_space=pltpu.VMEM),
+        cost_estimate=hint(20),
         compiler_params=pltpu.CompilerParams(vmem_limit_bytes=VMEM_LIMIT),
     )(own, before, x, w_out)
 
@@ -251,7 +211,8 @@
         out_shape=jax.ShapeDtypeStruct((count, depth, 128), jnp.bfloat16),
         in_specs=[pl.BlockSpec(memory_space=pltpu.VMEM)] * 2,
         out_specs=pl.BlockSpec(memory_space=pltpu.VMEM),
-        compiler_params=pltpu.CompilerParams(vmem_limit_bytes=16 * 1024 * 1024),
+        cost_estimate=hint(60),
+        compiler_params=pltpu.CompilerParams(vmem_limit_bytes=VMEM_LIMIT),
     )(codes, table)
 
 
@@ -272,6 +233,7 @@
         out_shape=jax.ShapeDtypeStruct((rows, tokens // rows, width + tokens), jnp.bfloat16),
         in_specs=[pl.BlockSpec(memory_space=pltpu.VMEM)] * 2,
         out_specs=pl.BlockSpec(memory_space=pltpu.VMEM),
+        cost_estimate=hint(60),
         compiler_params=pltpu.CompilerParams(vmem_limit_bytes=VMEM_LIMIT),
     )(song_ids.reshape(1, tokens), position_table)
 

time: 110 us -> 96.4 us (0.88)
  local copies, waits for them, and re-layouts: 11.6 us -> 2.01 us
  Pallas kernels: 20.6 us -> 16.3 us
    unnamed x14 -> x10, local copies, waits for them, and re-layouts: 11.3 us -> 1.76 us
    pallas_call x1, Pallas kernels: 5.89 us -> 3.55 us  [project(): pl.pallas_call(project_kernel, out_shape=(jax.ShapeDtypeStruct((tokens, 3...]
    pallas_call x1, Pallas kernels: 7.49 us -> 6.06 us  [column_sublayer(): pl.pallas_call(column_kernel, out_shape=jax.ShapeDtypeStruct((rows, per,...]
where the time goes in v3:
time: 96.4 us; the launch traced here: 96.1 us
  blocking collectives  64.7 us (67%)
  Pallas kernels  16.3 us (17%)
  waiting for transfers between devices  10.9 us (11%)
  starting transfers between devices  2.02 us (2%)
  local copies, waits for them, and re-layouts  2.01 us (2%)
    all_to_all x3, blocking collectives, exchange(): return lax.all_to_all(value, 'seq', split_axis=0, concat_axis=0, tiled=True)  64.7 us
    ppermute x1, waiting for transfers between devices, shards(): before = lax.ppermute(sent, 'seq', [(i, i + 1) for i in range(rows - 1)])  10.9 us
    pallas_call x1, Pallas kernels, column_sublayer(): pl.pallas_call(column_kernel, out_shape=jax.ShapeDtypeStruct((rows, per,...  6.06 us
    pallas_call x1, Pallas kernels, project(): pl.pallas_call(project_kernel, out_shape=(jax.ShapeDtypeStruct((tokens, 3...  3.55 us
    pallas_call x1, Pallas kernels, row_sublayer(): pl.pallas_call(row_kernel, out_shape=jax.ShapeDtypeStruct(x.shape, jnp.bf...  3.4 us
    pallas_call x1, Pallas kernels, lookup(): pl.pallas_call(lookup_kernel, out_shape=jax.ShapeDtypeStruct((count, dept...  2.92 us
    ppermute x1, starting transfers between devices, shards(): before = lax.ppermute(sent, 'seq', [(i, i + 1) for i in range(rows - 1)])  2.02 us
  transfers between devices with their start and end apart: 1, of which 1 were waited for; matrix products, arithmetic and copies ran while one was open for 0% of the time, Pallas kernels for 0%

profile of v3, /device:TPU:32, one launch (start us, length us, event | category | flops | bytes accessed | tf_op | source)
XLA Modules:
  0.0 96.1 jit_solution(3834427470909858960)
XLA Ops:
  0.0 0.0 copy-start.2
  0.0 1.1 %copy-done.2 = bf16[128,2432]{1,0:T(8,128)(2,1)S(1)} copy-done((bf16[128,2432]{1,0:T(8,128)(2,1)S(1)}, bf16[128,2432]{1,0:T(8,128)(2,1)}, u32[]{:S(2)}) %copy-start.2) | copy-done | bytes 622616
  1.1 0.0 copy-start.4
  1.1 0.7 copy-done.4
  1.7 0.0 copy-start.3
  1.7 0.4 shard_map.55
  2.1 25.2 %all_to_all.15.got_ref = bf16[64,2,2560]{2,1,0:T(2,128)(2,1)S(1)} all-to-all(bf16[64,2,2560]{2,1,0:T(2,128)(2,1)S(1)} %shard_map.55), channel_id=1, replica_groups=mesh['song'=2,'seq'=64] {'seq'}, dimensions={0} | all-to-all | bytes 1310720 | tf_op jit(solution)/shard_map/all_to_all | solution.py:242
  27.3 0.1 fusion
  27.4 0.1 copy.10
  27.5 0.1 copy.11
  27.6 0.1 copy.12.codes_ref
  27.6 0.0 copy-done.3
  27.7 0.0 copy-start
  27.7 0.0 copy-start.1
  27.7 2.9 %shard_map.56 = bf16[64,38,128]{2,1,0:T(8,128)(2,1)S(1)} custom-call(s32[64,128]{1,0:T(8,128)S(1)} %copy.12.codes_ref, bf16[38,2048]{1,0:T(8,128)(2,1)S(1)} %bitcast.9), custom_call_target="tpu_custom_call" | custom-call | flops 60000002048 | bytes 180000000 | tf_op jit(solution)/shard_map/pallas_call | solution.py:209
  30.6 20.1 %all_to_all.16.found_ref = bf16[64,38,128]{2,1,0:T(8,128)(2,1)S(1)} all-to-all(bf16[64,38,128]{2,1,0:T(8,128)(2,1)S(1)} %shard_map.56), channel_id=1, replica_groups=mesh['song'=2,'seq'=64] {'seq'}, dimensions={0} | all-to-all | bytes 1245184 | tf_op jit(solution)/shard_map/all_to_all | solution.py:242
  50.7 0.0 copy-done
  50.7 0.0 copy-done.1
  50.7 6.1 %shard_map.57 = bf16[64,2,2432]{2,1,0:T(2,128)(2,1)S(1)} custom-call(bf16[64,38,128]{2,1,0:T(8,128)(2,1)S(1)} %all_to_all.16.found_ref, bf16[64,2,2560]{2,1,0:T(2,128)(2,1)S(1)} %all_to_all.15.got_ref, bf16[2,1800,2432]{2,1,0:T(8,128)(2,1)S(1)} %bitcast.7, bf16[2,600,2432]{2,1,0:T(8,128)(2,1)S(1)} %copy-done.1), custom_call_target="tpu_custom_call" | custom-call | flops 20000000000 | bytes 60000000 | tf_op jit(solution)/shard_map/pallas_call | solution.py:88
  56.8 19.5 %all_to_all.17.resid_ref = bf16[64,2,2432]{2,1,0:T(2,128)(2,1)S(1)} all-to-all(bf16[64,2,2432]{2,1,0:T(2,128)(2,1)S(1)} %shard_map.57), channel_id=1, replica_groups=mesh['song'=2,'seq'=64] {'seq'}, dimensions={0} | all-to-all | bytes 1245184 | tf_op jit(solution)/shard_map/all_to_all | solution.py:242
  76.2 3.5 %shard_map.58 = (bf16[128,1800]{1,0:T(8,128)(2,1)S(1)}, bf16[128,1200]{1,0:T(8,128)(2,1)S(1)}, f32[128,2432]{1,0:T(8,128)S(1)}) custom-call(bf16[64,2,2432]{2,1,0:T(2,128)(2,1)S(1)} %all_to_all.17.resid_ref, bf16[2,1800,2432]{2,1,0:T(8,128)(2,1)S(1)} %bitcast.8), custom_call_target="tpu_custom_call" | custom-call | flops 20000000000 | bytes 60000000 | tf_op jit(solution)/shard_map/pallas_call | solution.py:118
  79.8 2.0 %collective-permute-start = (bf16[128,1200]{1,0:T(8,128)(2,1)S(1)}, bf16[128,1200]{1,0:T(8,128)(2,1)S(1)}, u32[]{:S(2)}, u32[]{:S(2)}) collective-permute-start(bf16[128,1200]{1,0:T(8,128)(2,1)S(1)} %get-tuple-element.9), channel_id=1, source_target_pairs={{0,1},{1,2},{2,3},{3,4},{4,5},{5,6},{6,7},{7,8},{8,9},{9,10},{10,1... | collective-permute-start | bytes 921608 | tf_op jit(solution)/shard_map/ppermute | solution.py:257
  81.8 10.9 %collective-permute-done.before_ref = bf16[128,1200]{1,0:T(8,128)(2,1)S(1)} collective-permute-done((bf16[128,1200]{1,0:T(8,128)(2,1)S(1)}, bf16[128,1200]{1,0:T(8,128)(2,1)S(1)}, u32[]{:S(2)}, u32[]{:S(2)}) %collective-permute-start) | collective-permute-done | bytes 307232 | tf_op jit(solution)/shard_map/ppermute | solution.py:257
  92.7 3.4 %shard_map.59 = bf16[128,2432]{1,0:T(8,128)(2,1)} custom-call(bf16[128,1800]{1,0:T(8,128)(2,1)S(1)} %get-tuple-element.8.own_ref, bf16[128,1200]{1,0:T(8,128)(2,1)S(1)} %collective-permute-done.before_ref, f32[128,2432]{1,0:T(8,128)S(1)} %get-tuple-element.10.x_ref, bf16[2,600,2432]{2,1,0:T(8,128)(2,1)S(1)} %copy-done.1), custom_call_target="tpu_custom_call" | custom-call | flops 20000000000 | bytes 60000000 | tf_op jit(solution)/shard_map/pallas_call | solution.py:171
Async XLA Ops:
  0.0 1.1 %copy-start.2 = (bf16[128,2432]{1,0:T(8,128)(2,1)S(1)}, bf16[128,2432]{1,0:T(8,128)(2,1)}, u32[]{:S(2)}) copy-start(bf16[128,2432]{1,0:T(8,128)(2,1)} %position_ref.1) | copy-start | bytes 1867780
  1.1 0.7 copy-start.4
  1.7 25.9 %copy-start.3 = (bf16[2048,38]{0,1:T(8,128)(2,1)S(1)}, bf16[2048,38]{0,1:T(8,128)(2,1)}, u32[]{:S(2)}) copy-start(bf16[2048,38]{0,1:T(8,128)(2,1)} %param.6) | copy-start | bytes 466948
  27.7 23.0 %copy-start = (bf16[2,2432,1800]{1,2,0:T(8,128)(2,1)S(1)}, bf16[2,2432,1800]{1,2,0:T(8,128)(2,1)}, u32[]{:S(2)}) copy-start(bf16[2,2432,1800]{1,2,0:T(8,128)(2,1)} %param.8) | copy-start | bytes 52531204
  27.7 23.0 %copy-start.1 = (bf16[2,600,2432]{2,1,0:T(8,128)(2,1)S(1)}, bf16[2,600,2432]{2,1,0:T(8,128)(2,1)}, u32[]{:S(2)}) copy-start(bf16[2,600,2432]{2,1,0:T(8,128)(2,1)} %w_out_ref.3) | copy-start | bytes 17510404
  79.8 12.9 %collective-permute-start = (bf16[128,1200]{1,0:T(8,128)(2,1)S(1)}, bf16[128,1200]{1,0:T(8,128)(2,1)S(1)}, u32[]{:S(2)}, u32[]{:S(2)}) collective-permute-start(bf16[128,1200]{1,0:T(8,128)(2,1)S(1)} %get-tuple-element.9), channel_id=1, source_target_pairs={{0,1},{1,2},{2,3},{3,4},{4,5},{5,6},{6,7},{7,8},{8,9},{9,10},{10,1... | collective-permute-start | bytes 921608 | tf_op jit(solution)/shard_map/ppermute | solution.py:257

commit v4 on v3

--- a/solution.py
+++ b/solution.py
@@ -46,7 +46,7 @@
 def column_kernel(found_ref, got_ref, w_in_ref, w_out_ref, out_ref, flat_ref, x_ref, normed_ref):
     rows, depth, tokens = found_ref.shape
     per = out_ref.shape[1]
-    width = out_ref.shape[2]
+    width = w_in_ref.shape[2]
     for s in range(rows):
         flat_ref[s * depth : (s + 1) * depth] = found_ref[s].astype(jnp.float32)
     for r in range(rows):
@@ -74,11 +74,18 @@
             jnp.dot(probs, value, preferred_element_type=jnp.float32).astype(jnp.bfloat16)
         )
     mixed = jnp.concatenate(pieces, axis=1)
-    normed_ref[...] = (
-        x_ref[...] + jnp.dot(mixed, w_out_ref[0], preferred_element_type=jnp.float32)
-    ).astype(jnp.bfloat16)
-    for r in range(rows):
-        out_ref[r] = normed_ref[r * per : (r + 1) * per]
+    x_ref[...] += jnp.dot(mixed, w_out_ref[0], preferred_element_type=jnp.float32)
+    normalize(x_ref, normed_ref)
+    joined = joint(normed_ref, w_in_ref[1])
+    keyed = jnp.concatenate(
+        [joined[:, 3 * HEAD * h + HEAD : 3 * HEAD * (h + 1)] for h in range(HEADS)], axis=1
+    )
+    resid = x_ref[...].astype(jnp.bfloat16)
+    out_ref[0, :, width:] = jnp.zeros((per, keyed.shape[1]), jnp.bfloat16)
+    for r in range(rows):
+        out_ref[r, :, :width] = resid[r * per : (r + 1) * per]
+        if r + 1 < rows:
+            out_ref[r + 1, :, width:] = keyed[r * per : (r + 1) * per]
 
 
 def column_sublayer(found, got, w_in, w_out):
@@ -87,7 +94,7 @@
     per = tokens // rows
     return pl.pallas_call(
         column_kernel,
-        out_shape=jax.ShapeDtypeStruct((rows, per, width), jnp.bfloat16),
+        out_shape=jax.ShapeDtypeStruct((rows, per, width + 2 * HEADS * HEAD), jnp.bfloat16),
         in_specs=[pl.BlockSpec(memory_space=pltpu.VMEM)] * 4,
         out_specs=pl.BlockSpec(memory_space=pltpu.VMEM),
         scratch_shapes=[
@@ -100,42 +107,16 @@
     )(found, got, w_in, w_out)
 
 
-def project_kernel(resid_ref, w_in_ref, own_ref, sent_ref, x_ref, normed_ref):
-    rows, per, width = resid_ref.shape
-    for r in range(rows):
-        x_ref[r * per : (r + 1) * per] = resid_ref[r].astype(jnp.float32)
+def row_kernel(got_ref, w_in_ref, w_out_ref, out_ref, x_ref, normed_ref, before_ref):
+    rows, per, _ = got_ref.shape
+    width = w_in_ref.shape[2]
+    has_before = lax.axis_index("seq") > 0
+    inv_root = 1.0 / math.sqrt(HEAD)
+    for r in range(rows):
+        x_ref[r * per : (r + 1) * per] = got_ref[r, :, :width].astype(jnp.float32)
+        before_ref[r * per : (r + 1) * per] = got_ref[r, :, width:]
     normalize(x_ref, normed_ref)
     joined = joint(normed_ref, w_in_ref[1])
-    own_ref[...] = joined
-    sent_ref[...] = jnp.concatenate(
-        [joined[:, 3 * HEAD * h + HEAD : 3 * HEAD * (h + 1)] for h in range(HEADS)], axis=1
-    )
-
-
-def project(resid, w_in):
-    rows, per, width = resid.shape
-    tokens = rows * per
-    return pl.pallas_call(
-        project_kernel,
-        out_shape=(
-            jax.ShapeDtypeStruct((tokens, 3 * HEADS * HEAD), jnp.bfloat16),
-            jax.ShapeDtypeStruct((tokens, 2 * HEADS * HEAD), jnp.bfloat16),
-            jax.ShapeDtypeStruct((tokens, width), jnp.float32),
-        ),
-        in_specs=[pl.BlockSpec(memory_space=pltpu.VMEM)] * 2,
-        out_specs=(pl.BlockSpec(memory_space=pltpu.VMEM),) * 3,
-        scratch_shapes=[
-            pltpu.VMEM((tokens, width), jnp.bfloat16),
-        ],
-        cost_estimate=hint(20),
-        compiler_params=pltpu.CompilerParams(vmem_limit_bytes=VMEM_LIMIT),
-    )(resid, w_in)
-
-
-def row_kernel(own_ref, before_ref, x_ref, w_out_ref, out_ref):
-    has_before = lax.axis_index("seq") > 0
-    inv_root = 1.0 / math.sqrt(HEAD)
-    joined = own_ref[...]
     before = before_ref[...]
     pieces = []
     for h in range(HEADS):
@@ -167,15 +148,23 @@
     ).astype(jnp.bfloat16)
 
 
-def row_sublayer(own, before, x, w_out):
+def row_sublayer(got, w_in, w_out):
+    rows, per, _ = got.shape
+    tokens = rows * per
+    width = w_in.shape[2]
     return pl.pallas_call(
         row_kernel,
-        out_shape=jax.ShapeDtypeStruct(x.shape, jnp.bfloat16),
-        in_specs=[pl.BlockSpec(memory_space=pltpu.VMEM)] * 4,
-        out_specs=pl.BlockSpec(memory_space=pltpu.VMEM),
+        out_shape=jax.ShapeDtypeStruct((tokens, width), jnp.bfloat16),
+        in_specs=[pl.BlockSpec(memory_space=pltpu.VMEM)] * 3,
+        out_specs=pl.BlockSpec(memory_space=pltpu.VMEM),
+        scratch_shapes=[
+            pltpu.VMEM((tokens, width), jnp.float32),
+            pltpu.VMEM((tokens, width), jnp.bfloat16),
+            pltpu.VMEM((tokens, 2 * HEADS * HEAD), jnp.bfloat16),
+        ],
         cost_estimate=hint(20),
         compiler_params=pltpu.CompilerParams(vmem_limit_bytes=VMEM_LIMIT),
-    )(own, before, x, w_out)
+    )(got, w_in, w_out)
 
 
 def lookup_kernel(codes_ref, table_ref, out_ref):
@@ -252,10 +241,8 @@
     codes = jnp.transpose(codes.reshape(rows, rows, per), (1, 0, 2)).reshape(rows, tokens)
     found = exchange(lookup(codes, jnp.transpose(table)))
     w_in = jnp.swapaxes(w_qkv, 1, 2)
-    resid = exchange(column_sublayer(found, got, w_in, w_out))
-    own, sent, x = project(resid, w_in)
-    before = lax.ppermute(sent, "seq", [(i, i + 1) for i in range(rows - 1)])
-    return row_sublayer(own, before, x, w_out)
+    got = exchange(column_sublayer(found, got, w_in, w_out))
+    return row_sublayer(got, w_in, w_out)
 
 
 def solution(mesh):

time: 96.4 us -> 91.6 us (0.950)
  the two profiles are of different devices: /device:TPU:32 before, /device:TPU:1 now
where the time goes in v4:
time: 91.6 us; the launch traced here: 91.4 us
  blocking collectives  70.3 us (77%)
  Pallas kernels  19 us (21%)
  local copies, waits for them, and re-layouts  2.01 us (2%)
    all_to_all x3, blocking collectives, exchange(): return lax.all_to_all(value, 'seq', split_axis=0, concat_axis=0, tiled=True)  70.3 us
    pallas_call x1, Pallas kernels, column_sublayer(): pl.pallas_call(column_kernel, out_shape=jax.ShapeDtypeStruct((rows, per,...  9.09 us
    pallas_call x1, Pallas kernels, row_sublayer(): pl.pallas_call(row_kernel, out_shape=jax.ShapeDtypeStruct((tokens, width)...  6.58 us
    pallas_call x1, Pallas kernels, lookup(): pl.pallas_call(lookup_kernel, out_shape=jax.ShapeDtypeStruct((count, dept...  2.92 us

profile of v4, /device:TPU:1, one launch (start us, length us, event | category | flops | bytes accessed | tf_op | source)
XLA Modules:
  0.0 91.4 jit_solution(8382444632073824948)
XLA Ops:
  0.0 0.0 copy-start.2
  0.0 1.1 %copy-done.2 = bf16[128,2432]{1,0:T(8,128)(2,1)S(1)} copy-done((bf16[128,2432]{1,0:T(8,128)(2,1)S(1)}, bf16[128,2432]{1,0:T(8,128)(2,1)}, u32[]{:S(2)}) %copy-start.2) | copy-done | bytes 622616
  1.1 0.0 copy-start.4
  1.1 0.7 copy-done.4
  1.7 0.0 copy-start.3
  1.7 0.4 shard_map.55
  2.1 27.5 %all_to_all.15.got_ref = bf16[64,2,2560]{2,1,0:T(2,128)(2,1)S(1)} all-to-all(bf16[64,2,2560]{2,1,0:T(2,128)(2,1)S(1)} %shard_map.55), channel_id=1, replica_groups=mesh['song'=2,'seq'=64] {'seq'}, dimensions={0} | all-to-all | bytes 1310720 | tf_op jit(solution)/shard_map/all_to_all | solution.py:231
  29.6 0.1 fusion
  29.7 0.1 copy.10
  29.8 0.1 copy.11
  29.9 0.1 copy.12.codes_ref
  30.0 0.0 copy-done.3
  30.0 0.0 copy-start
  30.0 0.0 copy-start.1
  30.1 2.9 %shard_map.56 = bf16[64,38,128]{2,1,0:T(8,128)(2,1)S(1)} custom-call(s32[64,128]{1,0:T(8,128)S(1)} %copy.12.codes_ref, bf16[38,2048]{1,0:T(8,128)(2,1)S(1)} %bitcast.9), custom_call_target="tpu_custom_call" | custom-call | flops 60000002048 | bytes 180000000 | tf_op jit(solution)/shard_map/pallas_call | solution.py:198
  33.0 20.1 %all_to_all.16.found_ref = bf16[64,38,128]{2,1,0:T(8,128)(2,1)S(1)} all-to-all(bf16[64,38,128]{2,1,0:T(8,128)(2,1)S(1)} %shard_map.56), channel_id=1, replica_groups=mesh['song'=2,'seq'=64] {'seq'}, dimensions={0} | all-to-all | bytes 1245184 | tf_op jit(solution)/shard_map/all_to_all | solution.py:231
  53.0 0.0 copy-done
  53.0 0.0 copy-done.1
  53.0 9.1 %shard_map.57 = bf16[64,2,3632]{2,1,0:T(2,128)(2,1)S(1)} custom-call(bf16[64,38,128]{2,1,0:T(8,128)(2,1)S(1)} %all_to_all.16.found_ref, bf16[64,2,2560]{2,1,0:T(2,128)(2,1)S(1)} %all_to_all.15.got_ref, bf16[2,1800,2432]{2,1,0:T(8,128)(2,1)S(1)} %bitcast.7, bf16[2,600,2432]{2,1,0:T(8,128)(2,1)S(1)} %copy-done.1), custom_call_target="tpu_custom_call" | custom-call | flops 20000000000 | bytes 60000000 | tf_op jit(solution)/shard_map/pallas_call | solution.py:95
  62.1 22.7 %all_to_all.17.got_ref = bf16[64,2,3632]{2,1,0:T(2,128)(2,1)S(1)} all-to-all(bf16[64,2,3632]{2,1,0:T(2,128)(2,1)S(1)} %shard_map.57), channel_id=1, replica_groups=mesh['song'=2,'seq'=64] {'seq'}, dimensions={0} | all-to-all | bytes 1859584 | tf_op jit(solution)/shard_map/all_to_all | solution.py:231
  84.8 6.6 %shard_map.58 = bf16[128,2432]{1,0:T(8,128)(2,1)} custom-call(bf16[64,2,3632]{2,1,0:T(2,128)(2,1)S(1)} %all_to_all.17.got_ref, bf16[2,1800,2432]{2,1,0:T(8,128)(2,1)S(1)} %bitcast.8, bf16[2,600,2432]{2,1,0:T(8,128)(2,1)S(1)} %copy-done.1), custom_call_target="tpu_custom_call" | custom-call | flops 20000000000 | bytes 60000000 | tf_op jit(solution)/shard_map/pallas_call | solution.py:155
Async XLA Ops:
  0.0 1.1 %copy-start.2 = (bf16[128,2432]{1,0:T(8,128)(2,1)S(1)}, bf16[128,2432]{1,0:T(8,128)(2,1)}, u32[]{:S(2)}) copy-start(bf16[128,2432]{1,0:T(8,128)(2,1)} %position_ref.1) | copy-start | bytes 1867780
  1.1 0.7 copy-start.4
  1.7 28.3 %copy-start.3 = (bf16[2048,38]{0,1:T(8,128)(2,1)S(1)}, bf16[2048,38]{0,1:T(8,128)(2,1)}, u32[]{:S(2)}) copy-start(bf16[2048,38]{0,1:T(8,128)(2,1)} %param.6) | copy-start | bytes 466948
  30.0 23.0 %copy-start = (bf16[2,2432,1800]{1,2,0:T(8,128)(2,1)S(1)}, bf16[2,2432,1800]{1,2,0:T(8,128)(2,1)}, u32[]{:S(2)}) copy-start(bf16[2,2432,1800]{1,2,0:T(8,128)(2,1)} %param.8) | copy-start | bytes 52531204
  30.0 23.0 %copy-start.1 = (bf16[2,600,2432]{2,1,0:T(8,128)(2,1)S(1)}, bf16[2,600,2432]{2,1,0:T(8,128)(2,1)}, u32[]{:S(2)}) copy-start(bf16[2,600,2432]{2,1,0:T(8,128)(2,1)} %w_out_ref.3) | copy-start | bytes 17510404

commit v5 on v4

--- a/solution.py
+++ b/solution.py
@@ -12,7 +12,11 @@
 HEAD = 150
 GROUPS = 8
 DIGIT = 64
-VMEM_LIMIT = 12 * 1024 * 1024
+VMEM_LIMIT = 8 * 1024 * 1024
+FLIP = 3
+PARTS = 4
+FULL_LIMIT = 60 * 1024 * 1024
+AT_ONCE = 4
 
 epsilon = 1e-05
 
@@ -31,10 +35,33 @@
         normed_ref[:, b] = ((x_ref[:, b] - mean) * scale).astype(jnp.bfloat16)
 
 
-def joint(normed_ref, weight):
-    return lax.dot_general(
-        normed_ref[...], weight, (((1,), (1,)), ((), ())), preferred_element_type=jnp.float32
-    ).astype(jnp.bfloat16)
+def flip_kernel(stored_ref, out_ref):
+    for j in range(out_ref.shape[0]):
+        out_ref[j] = jnp.transpose(stored_ref[0, j * 128 : (j + 1) * 128])
+
+
+def flip(stored, layer):
+    _, columns, width = stored.shape
+    return pl.pallas_call(
+        flip_kernel,
+        grid=(-(-columns // (128 * FLIP)),),
+        out_shape=jax.ShapeDtypeStruct((-(-columns // 128), width, 128), jnp.bfloat16),
+        in_specs=[pl.BlockSpec((1, 128 * FLIP, width), lambda j: (layer, j, 0))],
+        out_specs=pl.BlockSpec((FLIP, width, 128), lambda j: (j, 0, 0)),
+        cost_estimate=hint(10),
+        compiler_params=pltpu.CompilerParams(vmem_limit_bytes=FULL_LIMIT),
+    )(stored)
+
+
+def joint(normed_ref, strips_ref, joined_ref):
+    columns = joined_ref.shape[1]
+    for j in range(0, strips_ref.shape[0], 2):
+        last = min(j + 2, strips_ref.shape[0])
+        weight = jnp.concatenate([strips_ref[i] for i in range(j, last)], axis=1)
+        stop = min(last * 128, columns)
+        joined_ref[:, j * 128 : stop] = jnp.dot(
+            normed_ref[...], weight[:, : stop - j * 128], preferred_element_type=jnp.float32
+        ).astype(jnp.bfloat16)
 
 
 def hint(microseconds):
@@ -43,7 +70,7 @@
     )
 
 
-def column_kernel(found_ref, got_ref, w_in_ref, w_out_ref, out_ref, flat_ref, x_ref, normed_ref):
+def column_kernel(found_ref, got_ref, w_in_ref, strips_ref, w_out_ref, out_ref, flat_ref, x_ref, normed_ref, joined_ref):
     rows, depth, tokens = found_ref.shape
     per = out_ref.shape[1]
     width = w_in_ref.shape[2]
@@ -54,7 +81,9 @@
     for i in range(0, width, 128):
         x_ref[:, i : i + 128] += jnp.transpose(flat_ref[i : i + 128])
     normalize(x_ref, normed_ref)
-    joined = joint(normed_ref, w_in_ref[0])
+    joined = lax.dot_general(
+        normed_ref[...], w_in_ref[0], (((1,), (1,)), ((), ())), preferred_element_type=jnp.float32
+    ).astype(jnp.bfloat16)
     row_of = lax.broadcasted_iota(jnp.int32, (tokens, tokens), 0)
     col_of = lax.broadcasted_iota(jnp.int32, (tokens, tokens), 1)
     allowed = (row_of % per == col_of % per) & (row_of >= col_of)
@@ -76,7 +105,8 @@
     mixed = jnp.concatenate(pieces, axis=1)
     x_ref[...] += jnp.dot(mixed, w_out_ref[0], preferred_element_type=jnp.float32)
     normalize(x_ref, normed_ref)
-    joined = joint(normed_ref, w_in_ref[1])
+    joint(normed_ref, strips_ref, joined_ref)
+    joined = joined_ref[...]
     keyed = jnp.concatenate(
         [joined[:, 3 * HEAD * h + HEAD : 3 * HEAD * (h + 1)] for h in range(HEADS)], axis=1
     )
@@ -88,35 +118,37 @@
             out_ref[r + 1, :, width:] = keyed[r * per : (r + 1) * per]
 
 
-def column_sublayer(found, got, w_in, w_out):
+def column_sublayer(found, got, w_in, strips, w_out):
     rows, depth, tokens = found.shape
     width = w_in.shape[2]
     per = tokens // rows
     return pl.pallas_call(
         column_kernel,
         out_shape=jax.ShapeDtypeStruct((rows, per, width + 2 * HEADS * HEAD), jnp.bfloat16),
-        in_specs=[pl.BlockSpec(memory_space=pltpu.VMEM)] * 4,
+        in_specs=[pl.BlockSpec(memory_space=pltpu.VMEM)] * 5,
         out_specs=pl.BlockSpec(memory_space=pltpu.VMEM),
         scratch_shapes=[
             pltpu.VMEM((width, tokens), jnp.float32),
             pltpu.VMEM((tokens, width), jnp.float32),
             pltpu.VMEM((tokens, width), jnp.bfloat16),
+            pltpu.VMEM((tokens, 3 * HEADS * HEAD), jnp.bfloat16),
         ],
         cost_estimate=hint(20),
         compiler_params=pltpu.CompilerParams(vmem_limit_bytes=VMEM_LIMIT),
-    )(found, got, w_in, w_out)
-
-
-def row_kernel(got_ref, w_in_ref, w_out_ref, out_ref, x_ref, normed_ref, before_ref):
+    )(found, got, w_in, strips, w_out)
+
+
+def row_kernel(got_ref, strips_ref, w_out_ref, out_ref, x_ref, normed_ref, before_ref, joined_ref):
     rows, per, _ = got_ref.shape
-    width = w_in_ref.shape[2]
+    width = strips_ref.shape[1]
     has_before = lax.axis_index("seq") > 0
     inv_root = 1.0 / math.sqrt(HEAD)
     for r in range(rows):
         x_ref[r * per : (r + 1) * per] = got_ref[r, :, :width].astype(jnp.float32)
         before_ref[r * per : (r + 1) * per] = got_ref[r, :, width:]
     normalize(x_ref, normed_ref)
-    joined = joint(normed_ref, w_in_ref[1])
+    joint(normed_ref, strips_ref, joined_ref)
+    joined = joined_ref[...]
     before = before_ref[...]
     pieces = []
     for h in range(HEADS):
@@ -148,10 +180,10 @@
     ).astype(jnp.bfloat16)
 
 
-def row_sublayer(got, w_in, w_out):
+def row_sublayer(got, strips, w_out):
     rows, per, _ = got.shape
     tokens = rows * per
-    width = w_in.shape[2]
+    width = strips.shape[1]
     return pl.pallas_call(
         row_kernel,
         out_shape=jax.ShapeDtypeStruct((tokens, width), jnp.bfloat16),
@@ -161,10 +193,11 @@
             pltpu.VMEM((tokens, width), jnp.float32),
             pltpu.VMEM((tokens, width), jnp.bfloat16),
             pltpu.VMEM((tokens, 2 * HEADS * HEAD), jnp.bfloat16),
+            pltpu.VMEM((tokens, 3 * HEADS * HEAD), jnp.bfloat16),
         ],
         cost_estimate=hint(20),
         compiler_params=pltpu.CompilerParams(vmem_limit_bytes=VMEM_LIMIT),
-    )(got, w_in, w_out)
+    )(got, strips, w_out)
 
 
 def lookup_kernel(codes_ref, table_ref, out_ref):
@@ -179,17 +212,18 @@
     stacked = jnp.concatenate(
         [flipped[:, g * step : (g + 1) * step] for g in range(GROUPS)], axis=0
     ).astype(jnp.bfloat16)
-    slots = lax.broadcasted_iota(jnp.int32, (step, 128), 0)
-    for d in range(count):
-        codes = codes_ref[d : d + 1, :]
+    slots = lax.broadcasted_iota(jnp.int32, (step, AT_ONCE * 128), 0)
+    for d in range(0, count, AT_ONCE):
+        codes = jnp.concatenate([codes_ref[d + e : d + e + 1, :] for e in range(AT_ONCE)], axis=1)
         low = codes % step
         high = codes // step
         onehot = jnp.where(slots == low, 1.0, 0.0).astype(jnp.bfloat16)
         found = jnp.dot(stacked, onehot, preferred_element_type=jnp.float32)
-        chosen = jnp.zeros((padded, 128), jnp.float32)
+        chosen = jnp.zeros((padded, AT_ONCE * 128), jnp.float32)
         for g in range(GROUPS):
             chosen = jnp.where(high == g, found[g * padded : (g + 1) * padded], chosen)
-        out_ref[d] = chosen[:depth].astype(jnp.bfloat16)
+        for e in range(AT_ONCE):
+            out_ref[d + e] = chosen[:depth, e * 128 : (e + 1) * 128].astype(jnp.bfloat16)
 
 
 def lookup(codes, table):
@@ -200,30 +234,55 @@
         out_shape=jax.ShapeDtypeStruct((count, depth, 128), jnp.bfloat16),
         in_specs=[pl.BlockSpec(memory_space=pltpu.VMEM)] * 2,
         out_specs=pl.BlockSpec(memory_space=pltpu.VMEM),
-        cost_estimate=hint(60),
+        cost_estimate=hint(140),
         compiler_params=pltpu.CompilerParams(vmem_limit_bytes=VMEM_LIMIT),
     )(codes, table)
 
 
-def pack_kernel(codes_ref, position_ref, out_ref):
+def pack_kernel(codes_hbm, position_hbm, out_hbm, codes_ref, position_ref, out_ref, sem):
     rows, per, _ = out_ref.shape
-    width = position_ref.shape[1]
+    tokens, width = position_ref.shape
+    part = rows // PARTS
+    fetch = [pltpu.make_async_copy(codes_hbm, codes_ref, sem.at[0])]
+    for i in range(PARTS):
+        span = pl.ds(i * part * per, part * per)
+        fetch.append(
+            pltpu.make_async_copy(position_hbm.at[span], position_ref.at[span], sem.at[1 + i])
+        )
+    for copy in fetch:
+        copy.start()
+    fetch[0].wait()
     codes = codes_ref[...]
     digits = jnp.concatenate([codes // DIGIT, codes % DIGIT], axis=0).astype(jnp.bfloat16)
-    for r in range(rows):
-        out_ref[r, :, :width] = position_ref[r * per : (r + 1) * per]
-        out_ref[r, :, width:] = digits
+    store = []
+    for i in range(PARTS):
+        fetch[1 + i].wait()
+        for r in range(i * part, (i + 1) * part):
+            out_ref[r, :, :width] = position_ref[r * per : (r + 1) * per]
+            out_ref[r, :, width:] = digits
+        span = pl.ds(i * part, part)
+        store.append(pltpu.make_async_copy(out_ref.at[span], out_hbm.at[span], sem.at[1 + PARTS + i]))
+        store[-1].start()
+    for copy in store:
+        copy.wait()
 
 
 def pack(song_ids, position_table, rows):
     tokens, width = position_table.shape
+    shape = (rows, tokens // rows, width + tokens)
     return pl.pallas_call(
         pack_kernel,
-        out_shape=jax.ShapeDtypeStruct((rows, tokens // rows, width + tokens), jnp.bfloat16),
-        in_specs=[pl.BlockSpec(memory_space=pltpu.VMEM)] * 2,
-        out_specs=pl.BlockSpec(memory_space=pltpu.VMEM),
+        out_shape=jax.ShapeDtypeStruct(shape, jnp.bfloat16),
+        in_specs=[pl.BlockSpec(memory_space=pl.ANY)] * 2,
+        out_specs=pl.BlockSpec(memory_space=pl.ANY),
+        scratch_shapes=[
+            pltpu.VMEM((1, tokens), jnp.int32),
+            pltpu.VMEM((tokens, width), jnp.bfloat16),
+            pltpu.VMEM(shape, jnp.bfloat16),
+            pltpu.SemaphoreType.DMA((1 + 2 * PARTS,)),
+        ],
         cost_estimate=hint(60),
-        compiler_params=pltpu.CompilerParams(vmem_limit_bytes=VMEM_LIMIT),
+        compiler_params=pltpu.CompilerParams(vmem_limit_bytes=FULL_LIMIT),
     )(song_ids.reshape(1, tokens), position_table)
 
 
@@ -237,12 +296,14 @@
     per = tokens // rows
 
     got = exchange(pack(song_ids, position_table, rows))
+    w_in = jnp.swapaxes(w_qkv, 1, 2)
+    strips = flip(w_in, 1)
+    got, strips = lax.optimization_barrier((got, strips))
     codes = got[:, 0, width:].astype(jnp.int32) * DIGIT + got[:, 1, width:].astype(jnp.int32)
     codes = jnp.transpose(codes.reshape(rows, rows, per), (1, 0, 2)).reshape(rows, tokens)
     found = exchange(lookup(codes, jnp.transpose(table)))
-    w_in = jnp.swapaxes(w_qkv, 1, 2)
-    got = exchange(column_sublayer(found, got, w_in, w_out))
-    return row_sublayer(got, w_in, w_out)
+    got = exchange(column_sublayer(found, got, w_in, strips, w_out))
+    return row_sublayer(got, strips, w_out)
 
 
 def solution(mesh):

time: 91.6 us -> 88.3 us (0.964)
  blocking collectives: 70.3 us -> 42.8 us
  starting transfers between devices: 0 us -> 12.5 us
  Pallas kernels: 19 us -> 26.6 us
  waiting for transfers between devices: 0 us -> 5.59 us
  local copies, waits for them, and re-layouts: 2.01 us -> 0.29 us
    all_to_all x3 -> x2, blocking collectives: 70.3 us -> 42.8 us  [exchange(): return lax.all_to_all(value, 'seq', split_axis=0, concat_axis=0, tiled=True)]
    all_to_all x0 -> x1, starting transfers between devices: none -> 12.5 us  [exchange(): return lax.all_to_all(value, 'seq', split_axis=0, concat_axis=0, tiled=True)]
    pallas_call x1 -> x2, Pallas kernels: 0.38 us -> 11.7 us  [the longest x1 9.65 us: flip(): pl.pallas_call(flip_kernel, grid=(-(-columns // (128 * FLIP)),), out_shap...]
    all_to_all x0 -> x1, waiting for transfers between devices: none -> 5.59 us  [exchange(): return lax.all_to_all(value, 'seq', split_axis=0, concat_axis=0, tiled=True)]
    pallas_call x1, Pallas kernels: 6.58 us -> 4.64 us  [row_sublayer(): pl.pallas_call(row_kernel, out_shape=jax.ShapeDtypeStruct((tokens, width)...]
    unnamed x10 -> x8, local copies, waits for them, and re-layouts: 1.76 us -> 0.04 us
    pallas_call x1, Pallas kernels: 9.09 us -> 7.76 us  [column_sublayer(): pl.pallas_call(column_kernel, out_shape=jax.ShapeDtypeStruct((rows, per,...]
  transfers between devices with their start and end apart: 0 -> 1, of which waited for: 0 -> 1; matrix products, arithmetic and copies ran while one was open for 0% -> 0% of each run, Pallas kernels for 0% -> 11%
where the time goes in v5:
time: 88.3 us; the launch traced here: 87.9 us
  blocking collectives  42.8 us (48%)
  Pallas kernels  26.6 us (30%)
  starting transfers between devices  12.5 us (14%)
  waiting for transfers between devices  5.59 us (6%)
    all_to_all x2, blocking collectives, exchange(): return lax.all_to_all(value, 'seq', split_axis=0, concat_axis=0, tiled=True)  42.8 us
    all_to_all x1, starting transfers between devices, exchange(): return lax.all_to_all(value, 'seq', split_axis=0, concat_axis=0, tiled=True)  12.5 us
    pallas_call x1, Pallas kernels, flip(): pl.pallas_call(flip_kernel, grid=(-(-columns // (128 * FLIP)),), out_shap...  9.65 us
    pallas_call x1, Pallas kernels, column_sublayer(): pl.pallas_call(column_kernel, out_shape=jax.ShapeDtypeStruct((rows, per,...  7.76 us
    all_to_all x1, waiting for transfers between devices, exchange(): return lax.all_to_all(value, 'seq', split_axis=0, concat_axis=0, tiled=True)  5.59 us
    pallas_call x1, Pallas kernels, row_sublayer(): pl.pallas_call(row_kernel, out_shape=jax.ShapeDtypeStruct((tokens, width)...  4.64 us
    pallas_call x1, Pallas kernels, lookup(): pl.pallas_call(lookup_kernel, out_shape=jax.ShapeDtypeStruct((count, dept...  2.5 us
    pallas_call x1, Pallas kernels, pack(): pl.pallas_call(pack_kernel, out_shape=jax.ShapeDtypeStruct(shape, jnp.bfl...  2.06 us
  transfers between devices with their start and end apart: 1, of which 1 were waited for; matrix products, arithmetic and copies ran while one was open for 0% of the time, Pallas kernels for 11%

profile of v5, /device:TPU:1, one launch (start us, length us, event | category | flops | bytes accessed | tf_op | source)
XLA Modules:
  0.0 87.9 jit_solution(9744066834911463103)
XLA Ops:
  0.0 2.1 %shard_map.55 = bf16[64,2,2560]{2,1,0:T(2,128)(2,1)} custom-call(s32[1,128]{1,0:T(1,128)} %bitcast.12, bf16[128,2432]{1,0:T(8,128)(2,1)} %position_hbm.1), custom_call_target="tpu_custom_call" | custom-call | flops 60000002048 | bytes 180000000 | tf_op jit(solution)/shard_map/pallas_call | solution.py:273
  2.1 12.5 %all-to-all-start = ((bf16[64,2,2560]{2,1,0:T(2,128)(2,1)}), bf16[64,2,2560]{2,1,0:T(2,128)(2,1)S(1)}, u32[]{:S(2)}, u32[]{:S(2)}) async-start(bf16[64,2,2560]{2,1,0:T(2,128)(2,1)} %shard_map.55), calls=%async_computation | async-start | bytes 1310720 | tf_op jit(solution)/shard_map/all_to_all | solution.py:290
  14.5 0.0 copy-start.2
  14.6 9.6 %shard_map.56.strips_ref = bf16[15,2432,128]{2,1,0:T(8,128)(2,1)} custom-call(bf16[2,1800,2432]{2,1,0:T(8,128)(2,1)} %bitcast.7), custom_call_target="tpu_custom_call" | custom-call | flops 10000000000 | bytes 30000000 | tf_op jit(solution)/shard_map/pallas_call | solution.py:45
  24.2 5.6 %all-to-all-done.got_ref = bf16[64,2,2560]{2,1,0:T(2,128)(2,1)S(1)} async-done(((bf16[64,2,2560]{2,1,0:T(2,128)(2,1)}), bf16[64,2,2560]{2,1,0:T(2,128)(2,1)S(1)}, u32[]{:S(2)}, u32[]{:S(2)}) %all-to-all-start) | async-done | bytes 655392 | tf_op jit(solution)/shard_map/all_to_all | solution.py:290
  29.8 0.1 convert_add_fusion
  29.9 0.1 copy.10
  30.0 0.1 copy.11
  30.1 0.1 copy.12.codes_ref
  30.2 0.0 copy-done.2
  30.2 0.0 copy-start
  30.2 0.0 copy-start.1
  30.2 0.0 copy-start.3
  30.2 2.5 %shard_map.57 = bf16[64,38,128]{2,1,0:T(8,128)(2,1)S(1)} custom-call(s32[64,128]{1,0:T(8,128)S(1)} %copy.12.codes_ref, bf16[38,2048]{1,0:T(8,128)(2,1)S(1)} %bitcast.9), custom_call_target="tpu_custom_call" | custom-call | flops 140000002048 | bytes 420000000 | tf_op jit(solution)/shard_map/pallas_call | solution.py:232
  32.7 20.1 %all_to_all.15.found_ref = bf16[64,38,128]{2,1,0:T(8,128)(2,1)S(1)} all-to-all(bf16[64,38,128]{2,1,0:T(8,128)(2,1)S(1)} %shard_map.57), channel_id=1, replica_groups=mesh['song'=2,'seq'=64] {'seq'}, dimensions={0} | all-to-all | bytes 1245184 | tf_op jit(solution)/shard_map/all_to_all | solution.py:290
  52.8 0.0 copy-done
  52.8 0.0 copy-done.1
  52.8 0.0 copy-done.3
  52.8 7.8 %shard_map.58 = bf16[64,2,3632]{2,1,0:T(2,128)(2,1)S(1)} custom-call(bf16[64,38,128]{2,1,0:T(8,128)(2,1)S(1)} %all_to_all.15.found_ref, bf16[64,2,2560]{2,1,0:T(2,128)(2,1)S(1)} %all-to-all-done.got_ref, bf16[2,1800,2432]{2,1,0:T(8,128)(2,1)S(1)} %bitcast.8, bf16[15,2432,128]{2,1,0:T(8,128)(2,1)S(1)} %copy-done.3, bf16[2,600,2432]{2,1,0:T(8,128)(2,1)S(1)} %copy-done.1), custom_call_target="tpu_custom_call" | custom-call | flops 20000000000 | bytes 60000000 | tf_op jit(solution)/shard_map/pallas_call | solution.py:125
  60.6 22.7 %all_to_all.16.got_ref = bf16[64,2,3632]{2,1,0:T(2,128)(2,1)S(1)} all-to-all(bf16[64,2,3632]{2,1,0:T(2,128)(2,1)S(1)} %shard_map.58), channel_id=1, replica_groups=mesh['song'=2,'seq'=64] {'seq'}, dimensions={0} | all-to-all | bytes 1859584 | tf_op jit(solution)/shard_map/all_to_all | solution.py:290
  83.3 4.6 %shard_map.59 = bf16[128,2432]{1,0:T(8,128)(2,1)} custom-call(bf16[64,2,3632]{2,1,0:T(2,128)(2,1)S(1)} %all_to_all.16.got_ref, bf16[15,2432,128]{2,1,0:T(8,128)(2,1)S(1)} %copy-done.3, bf16[2,600,2432]{2,1,0:T(8,128)(2,1)S(1)} %copy-done.1), custom_call_target="tpu_custom_call" | custom-call | flops 20000000000 | bytes 60000000 | tf_op jit(solution)/shard_map/pallas_call | solution.py:187
Async XLA Ops:
  2.1 27.7 %all-to-all-start = ((bf16[64,2,2560]{2,1,0:T(2,128)(2,1)}), bf16[64,2,2560]{2,1,0:T(2,128)(2,1)S(1)}, u32[]{:S(2)}, u32[]{:S(2)}) async-start(bf16[64,2,2560]{2,1,0:T(2,128)(2,1)} %shard_map.55), calls=%async_computation | async-start | bytes 1310720 | tf_op jit(solution)/shard_map/all_to_all | solution.py:290
  14.5 15.6 %copy-start.2 = (bf16[2048,38]{0,1:T(8,128)(2,1)S(1)}, bf16[2048,38]{0,1:T(8,128)(2,1)}, u32[]{:S(2)}) copy-start(bf16[2048,38]{0,1:T(8,128)(2,1)} %param.6) | copy-start | bytes 466948
  30.2 22.6 %copy-start = (bf16[2,2432,1800]{1,2,0:T(8,128)(2,1)S(1)}, bf16[2,2432,1800]{1,2,0:T(8,128)(2,1)}, u32[]{:S(2)}) copy-start(bf16[2,2432,1800]{1,2,0:T(8,128)(2,1)} %param.8) | copy-start | bytes 52531204
  30.2 22.6 %copy-start.1 = (bf16[2,600,2432]{2,1,0:T(8,128)(2,1)S(1)}, bf16[2,600,2432]{2,1,0:T(8,128)(2,1)}, u32[]{:S(2)}) copy-start(bf16[2,600,2432]{2,1,0:T(8,128)(2,1)} %w_out_ref.3) | copy-start | bytes 17510404
  30.2 22.6 %copy-start.3 = (bf16[15,2432,128]{2,1,0:T(8,128)(2,1)S(1)}, bf16[15,2432,128]{2,1,0:T(8,128)(2,1)}, u32[]{:S(2)}) copy-start(bf16[15,2432,128]{2,1,0:T(8,128)(2,1)} %shard_map.56.strips_ref) | copy-start | bytes 28016644

commit v6 on v5

--- a/solution.py
+++ b/solution.py
@@ -13,8 +13,7 @@
 GROUPS = 8
 DIGIT = 64
 VMEM_LIMIT = 8 * 1024 * 1024
-FLIP = 3
-PARTS = 4
+PARTS = 8
 FULL_LIMIT = 60 * 1024 * 1024
 AT_ONCE = 4
 
@@ -35,19 +34,60 @@
         normed_ref[:, b] = ((x_ref[:, b] - mean) * scale).astype(jnp.bfloat16)
 
 
-def flip_kernel(stored_ref, out_ref):
-    for j in range(out_ref.shape[0]):
-        out_ref[j] = jnp.transpose(stored_ref[0, j * 128 : (j + 1) * 128])
+def stored_columns(start, stop):
+    runs = [(2 * HEAD * h, 3 * HEAD * h + HEAD, 2 * HEAD) for h in range(HEADS)]
+    runs += [(2 * HEAD * HEADS + HEAD * h, 3 * HEAD * h, HEAD) for h in range(HEADS)]
+    pieces = []
+    for first, where, count in runs:
+        low, high = max(first, start), min(first + count, stop)
+        if low < high:
+            pieces.append((where + low - first, where + high - first))
+    return pieces
+
+
+def flip_kernel(layer, stored_hbm, strips_hbm, stored_ref, strips_ref, sem):
+    columns, width = stored_ref.shape
+    step = columns // PARTS // 8 * 8
+    cuts = [step * i for i in range(PARTS)] + [columns]
+    fetch = [
+        pltpu.make_async_copy(
+            stored_hbm.at[layer, low:high], stored_ref.at[low:high], sem.at[i]
+        )
+        for i, (low, high) in enumerate(zip(cuts, cuts[1:]))
+    ]
+    for copy in fetch:
+        copy.start()
+    ready = 0
+    store = []
+    for j in range(strips_ref.shape[0]):
+        pieces = stored_columns(j * 128, (j + 1) * 128)
+        while ready < PARTS and cuts[ready] < max(high for _, high in pieces):
+            fetch[ready].wait()
+            ready += 1
+        rows = [stored_ref[low:high] for low, high in pieces]
+        missing = 128 - sum(high - low for low, high in pieces)
+        if missing:
+            rows.append(jnp.zeros((missing, width), jnp.bfloat16))
+        strips_ref[j] = jnp.transpose(jnp.concatenate(rows, axis=0))
+        store.append(pltpu.make_async_copy(strips_ref.at[j], strips_hbm.at[j], sem.at[PARTS + j]))
+        store[-1].start()
+    for copy in fetch[ready:] + store:
+        copy.wait()
 
 
 def flip(stored, layer):
     _, columns, width = stored.shape
-    return pl.pallas_call(
-        flip_kernel,
-        grid=(-(-columns // (128 * FLIP)),),
-        out_shape=jax.ShapeDtypeStruct((-(-columns // 128), width, 128), jnp.bfloat16),
-        in_specs=[pl.BlockSpec((1, 128 * FLIP, width), lambda j: (layer, j, 0))],
-        out_specs=pl.BlockSpec((FLIP, width, 128), lambda j: (j, 0, 0)),
+    shape = (-(-columns // 128), width, 128)
+    return pl.pallas_call(
+        functools.partial(flip_kernel, layer),
+        out_shape=jax.ShapeDtypeStruct(shape, jnp.bfloat16),
+        in_specs=[pl.BlockSpec(memory_space=pl.ANY)],
+        out_specs=pl.BlockSpec(memory_space=pl.ANY),
+        scratch_shapes=[
+            pltpu.VMEM((columns, width), jnp.bfloat16),
+            pltpu.VMEM(shape, jnp.bfloat16),
+            pltpu.SemaphoreType.DMA((PARTS + shape[0],)),
+        ],
         cost_estimate=hint(10),
         compiler_params=pltpu.CompilerParams(vmem_limit_bytes=FULL_LIMIT),
     )(stored)
@@ -55,7 +95,7 @@
 
 def joint(normed_ref, strips_ref, joined_ref):
     columns = joined_ref.shape[1]
-    for j in range(0, strips_ref.shape[0], 2):
+    for j in range(0, -(-columns // 128), 2):
         last = min(j + 2, strips_ref.shape[0])
         weight = jnp.concatenate([strips_ref[i] for i in range(j, last)], axis=1)
         stop = min(last * 128, columns)
@@ -64,13 +104,17 @@
         ).astype(jnp.bfloat16)
 
 
+def product(left, right, dims):
+    return lax.dot_general(left, right, (((dims[0],), (dims[1],)), ((), ())), preferred_element_type=jnp.float32)
+
+
 def hint(microseconds):
     return pl.CostEstimate(
         flops=int(microseconds * 1e9), bytes_accessed=int(microseconds * 3e6), transcendentals=0
     )
 
 
-def column_kernel(found_ref, got_ref, w_in_ref, strips_ref, w_out_ref, out_ref, flat_ref, x_ref, normed_ref, joined_ref):
+def column_kernel(found_ref, got_ref, w_in_ref, strips_ref, w_out_ref, out_ref, flat_ref, x_ref, normed_ref, keyed_ref):
     rows, depth, tokens = found_ref.shape
     per = out_ref.shape[1]
     width = w_in_ref.shape[2]
@@ -84,38 +128,31 @@
     joined = lax.dot_general(
         normed_ref[...], w_in_ref[0], (((1,), (1,)), ((), ())), preferred_element_type=jnp.float32
     ).astype(jnp.bfloat16)
-    row_of = lax.broadcasted_iota(jnp.int32, (tokens, tokens), 0)
-    col_of = lax.broadcasted_iota(jnp.int32, (tokens, tokens), 1)
-    allowed = (row_of % per == col_of % per) & (row_of >= col_of)
-    pieces = []
-    for h in range(HEADS):
-        base = 3 * HEAD * h
-        query = joined[:, base : base + HEAD]
-        key = joined[:, base + HEAD : base + 2 * HEAD]
-        value = joined[:, base + 2 * HEAD : base + 3 * HEAD]
-        scores = lax.dot_general(
-            query, key, (((1,), (1,)), ((), ())), preferred_element_type=jnp.float32
-        ) * (1.0 / math.sqrt(HEAD))
-        scores = jnp.where(allowed, scores, -jnp.inf)
-        lifted = jnp.exp(scores - jnp.max(scores, axis=1, keepdims=True))
-        probs = (lifted / jnp.sum(lifted, axis=1, keepdims=True)).astype(jnp.bfloat16)
-        pieces.append(
-            jnp.dot(probs, value, preferred_element_type=jnp.float32).astype(jnp.bfloat16)
-        )
-    mixed = jnp.concatenate(pieces, axis=1)
+    key_of = lax.broadcasted_iota(jnp.int32, (tokens, tokens), 0)
+    query_of = lax.broadcasted_iota(jnp.int32, (tokens, tokens), 1)
+    allowed = (key_of % per == query_of % per) & (key_of <= query_of)
+    query, key, value = (
+        [joined[:, 3 * HEAD * h + HEAD * i : 3 * HEAD * h + HEAD * (i + 1)] for h in range(HEADS)]
+        for i in range(3)
+    )
+    scores = [product(k, q, (1, 1)) * (1.0 / math.sqrt(HEAD)) for q, k in zip(query, key)]
+    scores = [jnp.where(allowed, s, -jnp.inf) for s in scores]
+    top = [jnp.max(s, axis=0, keepdims=True) for s in scores]
+    lifted = [jnp.exp(s - m) for s, m in zip(scores, top)]
+    share = [1.0 / jnp.sum(e, axis=0, keepdims=True) for e in lifted]
+    probs = [(e * r).astype(jnp.bfloat16) for e, r in zip(lifted, share)]
+    mixed = jnp.concatenate(
+        [product(p, v, (0, 0)).astype(jnp.bfloat16) for p, v in zip(probs, value)], axis=1
+    )
     x_ref[...] += jnp.dot(mixed, w_out_ref[0], preferred_element_type=jnp.float32)
     normalize(x_ref, normed_ref)
-    joint(normed_ref, strips_ref, joined_ref)
-    joined = joined_ref[...]
-    keyed = jnp.concatenate(
-        [joined[:, 3 * HEAD * h + HEAD : 3 * HEAD * (h + 1)] for h in range(HEADS)], axis=1
-    )
+    joint(normed_ref, strips_ref, keyed_ref)
     resid = x_ref[...].astype(jnp.bfloat16)
-    out_ref[0, :, width:] = jnp.zeros((per, keyed.shape[1]), jnp.bfloat16)
+    out_ref[0, :, width:] = jnp.zeros((per, keyed_ref.shape[1]), jnp.bfloat16)
     for r in range(rows):
         out_ref[r, :, :width] = resid[r * per : (r + 1) * per]
         if r + 1 < rows:
-            out_ref[r + 1, :, width:] = keyed[r * per : (r + 1) * per]
+            out_ref[r + 1, :, width:] = keyed_ref[r * per : (r + 1) * per]
 
 
 def column_sublayer(found, got, w_in, strips, w_out):
@@ -131,7 +168,7 @@
             pltpu.VMEM((width, tokens), jnp.float32),
             pltpu.VMEM((tokens, width), jnp.float32),
             pltpu.VMEM((tokens, width), jnp.bfloat16),
-            pltpu.VMEM((tokens, 3 * HEADS * HEAD), jnp.bfloat16),
+            pltpu.VMEM((tokens, 2 * HEADS * HEAD), jnp.bfloat16),
         ],
         cost_estimate=hint(20),
         compiler_params=pltpu.CompilerParams(vmem_limit_bytes=VMEM_LIMIT),
@@ -150,31 +187,38 @@
     joint(normed_ref, strips_ref, joined_ref)
     joined = joined_ref[...]
     before = before_ref[...]
-    pieces = []
-    for h in range(HEADS):
-        base = 3 * HEAD * h
-        query = joined[:, base : base + HEAD]
-        key = joined[:, base + HEAD : base + 2 * HEAD].astype(jnp.float32)
-        value = joined[:, base + 2 * HEAD : base + 3 * HEAD].astype(jnp.float32)
-        far_key = before[:, 2 * HEAD * h : 2 * HEAD * h + HEAD]
-        far_value = before[:, 2 * HEAD * h + HEAD : 2 * HEAD * (h + 1)]
-        far_scores = (
-            lax.dot_general(
-                query, far_key, (((1,), (1,)), ((), ())), preferred_element_type=jnp.float32
-            )
-            * inv_root
-        )
-        far_scores = jnp.where(has_before, far_scores, -jnp.inf)
-        own_scores = jnp.sum(query.astype(jnp.float32) * key, axis=1, keepdims=True) * inv_root
-        top_score = jnp.maximum(jnp.max(far_scores, axis=1, keepdims=True), own_scores)
-        far_lifted = jnp.exp(far_scores - top_score)
-        own_lifted = jnp.exp(own_scores - top_score)
-        total = jnp.sum(far_lifted, axis=1, keepdims=True) + own_lifted
-        far_probs = (far_lifted / total).astype(jnp.bfloat16)
-        own_probs = (own_lifted / total).astype(jnp.bfloat16).astype(jnp.float32)
-        far_part = jnp.dot(far_probs, far_value, preferred_element_type=jnp.float32)
-        pieces.append((far_part + own_probs * value).astype(jnp.bfloat16))
-    mixed = jnp.concatenate(pieces, axis=1)
+    tokens = joined.shape[0]
+    own = lax.broadcasted_iota(jnp.int32, (tokens, tokens), 0) == lax.broadcasted_iota(
+        jnp.int32, (tokens, tokens), 1
+    )
+    start = 2 * HEADS * HEAD
+    query = [joined[:, start + HEAD * h : start + HEAD * (h + 1)] for h in range(HEADS)]
+    own_key, far_key, own_value, far_value = (
+        [part[:, HEAD * (2 * h + i) : HEAD * (2 * h + i + 1)] for h in range(HEADS)]
+        for i in range(2)
+        for part in (joined, before)
+    )
+    far = [product(k, q, (1, 1)) * inv_root for q, k in zip(query, far_key)]
+    far = [jnp.where(has_before, s, -jnp.inf) for s in far]
+    near = [product(k, q, (1, 1)) * inv_root for q, k in zip(query, own_key)]
+    near = [jnp.sum(jnp.where(own, s, 0.0), axis=0, keepdims=True) for s in near]
+    top = [jnp.maximum(jnp.max(f, axis=0, keepdims=True), n) for f, n in zip(far, near)]
+    far = [jnp.exp(f - m) for f, m in zip(far, top)]
+    near = [jnp.exp(n - m) for n, m in zip(near, top)]
+    share = [1.0 / (jnp.sum(f, axis=0, keepdims=True) + n) for f, n in zip(far, near)]
+    far = [(f * r).astype(jnp.bfloat16) for f, r in zip(far, share)]
+    near = [jnp.where(own, n * r, 0.0).astype(jnp.bfloat16) for n, r in zip(near, share)]
+    mixed = jnp.concatenate(
+        [
+            product(
+                jnp.concatenate([far[h], near[h]], axis=0),
+                jnp.concatenate([far_value[h], own_value[h]], axis=0),
+                (0, 0),
+            ).astype(jnp.bfloat16)
+            for h in range(HEADS)
+        ],
+        axis=1,
+    )
     out_ref[...] = (
         x_ref[...] + jnp.dot(mixed, w_out_ref[1], preferred_element_type=jnp.float32)
     ).astype(jnp.bfloat16)

time: 88.3 us -> 87.1 us (0.986)
  Pallas kernels: 26.6 us -> 23.4 us
  waiting for transfers between devices: 5.59 us -> 7.66 us
    pallas_call x1, Pallas kernels: 9.65 us -> 7.57 us  [flip(): pl.pallas_call(functools.partial(flip_kernel, layer), out_shape=jax.Shape...]
    all_to_all x1, waiting for transfers between devices: 5.59 us -> 7.66 us  [exchange(): return lax.all_to_all(value, 'seq', split_axis=0, concat_axis=0, tiled=True)]
    pallas_call x1, Pallas kernels: 7.76 us -> 6.82 us  [column_sublayer(): pl.pallas_call(column_kernel, out_shape=jax.ShapeDtypeStruct((rows, per,...]
  transfers between devices with their start and end apart: 1 -> 1, of which waited for: 1 -> 1; matrix products, arithmetic and copies ran while one was open for 0% -> 0% of each run, Pallas kernels for 11% -> 9%
where the time goes in v6:
time: 87.1 us; the launch traced here: 86.8 us
  blocking collectives  42.8 us (49%)
  Pallas kernels  23.4 us (27%)
  starting transfers between devices  12.5 us (14%)
  waiting for transfers between devices  7.66 us (9%)
    all_to_all x2, blocking collectives, exchange(): return lax.all_to_all(value, 'seq', split_axis=0, concat_axis=0, tiled=True)  42.8 us
    all_to_all x1, starting transfers between devices, exchange(): return lax.all_to_all(value, 'seq', split_axis=0, concat_axis=0, tiled=True)  12.5 us
    all_to_all x1, waiting for transfers between devices, exchange(): return lax.all_to_all(value, 'seq', split_axis=0, concat_axis=0, tiled=True)  7.66 us
    pallas_call x1, Pallas kernels, flip(): pl.pallas_call(functools.partial(flip_kernel, layer), out_shape=jax.Shape...  7.57 us
    pallas_call x1, Pallas kernels, column_sublayer(): pl.pallas_call(column_kernel, out_shape=jax.ShapeDtypeStruct((rows, per,...  6.82 us
    pallas_call x1, Pallas kernels, row_sublayer(): pl.pallas_call(row_kernel, out_shape=jax.ShapeDtypeStruct((tokens, width)...  4.43 us
    pallas_call x1, Pallas kernels, lookup(): pl.pallas_call(lookup_kernel, out_shape=jax.ShapeDtypeStruct((count, dept...  2.5 us
    pallas_call x1, Pallas kernels, pack(): pl.pallas_call(pack_kernel, out_shape=jax.ShapeDtypeStruct(shape, jnp.bfl...  2.08 us
  transfers between devices with their start and end apart: 1, of which 1 were waited for; matrix products, arithmetic and copies ran while one was open for 0% of the time, Pallas kernels for 9%

profile of v6, /device:TPU:1, one launch (start us, length us, event | category | flops | bytes accessed | tf_op | source)
XLA Modules:
  0.0 86.8 jit_solution(9365808062783730974)
XLA Ops:
  0.0 2.1 %shard_map.55 = bf16[64,2,2560]{2,1,0:T(2,128)(2,1)} custom-call(s32[1,128]{1,0:T(1,128)} %bitcast.12, bf16[128,2432]{1,0:T(8,128)(2,1)} %position_hbm.1), custom_call_target="tpu_custom_call" | custom-call | flops 60000002048 | bytes 180000000 | tf_op jit(solution)/shard_map/pallas_call | solution.py:317
  2.1 12.5 %all-to-all-start = ((bf16[64,2,2560]{2,1,0:T(2,128)(2,1)}), bf16[64,2,2560]{2,1,0:T(2,128)(2,1)S(1)}, u32[]{:S(2)}, u32[]{:S(2)}) async-start(bf16[64,2,2560]{2,1,0:T(2,128)(2,1)} %shard_map.55), calls=%async_computation | async-start | bytes 1310720 | tf_op jit(solution)/shard_map/all_to_all | solution.py:334
  14.6 0.0 copy-start.2
  14.6 7.6 %shard_map.56.strips_ref = bf16[15,2432,128]{2,1,0:T(8,128)(2,1)} custom-call(bf16[2,1800,2432]{2,1,0:T(8,128)(2,1)} %bitcast.7), custom_call_target="tpu_custom_call" | custom-call | flops 10000000000 | bytes 30000000 | tf_op jit(solution)/shard_map/pallas_call | solution.py:81
  22.2 7.7 %all-to-all-done.got_ref = bf16[64,2,2560]{2,1,0:T(2,128)(2,1)S(1)} async-done(((bf16[64,2,2560]{2,1,0:T(2,128)(2,1)}), bf16[64,2,2560]{2,1,0:T(2,128)(2,1)S(1)}, u32[]{:S(2)}, u32[]{:S(2)}) %all-to-all-start) | async-done | bytes 655392 | tf_op jit(solution)/shard_map/all_to_all | solution.py:334
  29.8 0.1 convert_add_fusion
  29.9 0.1 copy.10
  30.0 0.1 copy.11
  30.1 0.1 copy.12.codes_ref
  30.2 0.0 copy-done.2
  30.2 0.0 copy-start
  30.2 0.0 copy-start.1
  30.3 0.0 copy-start.3
  30.3 2.5 %shard_map.57 = bf16[64,38,128]{2,1,0:T(8,128)(2,1)S(1)} custom-call(s32[64,128]{1,0:T(8,128)S(1)} %copy.12.codes_ref, bf16[38,2048]{1,0:T(8,128)(2,1)S(1)} %bitcast.9), custom_call_target="tpu_custom_call" | custom-call | flops 140000002048 | bytes 420000000 | tf_op jit(solution)/shard_map/pallas_call | solution.py:276
  32.8 20.1 %all_to_all.15.found_ref = bf16[64,38,128]{2,1,0:T(8,128)(2,1)S(1)} all-to-all(bf16[64,38,128]{2,1,0:T(8,128)(2,1)S(1)} %shard_map.57), channel_id=1, replica_groups=mesh['song'=2,'seq'=64] {'seq'}, dimensions={0} | all-to-all | bytes 1245184 | tf_op jit(solution)/shard_map/all_to_all | solution.py:334
  52.8 0.0 copy-done
  52.8 0.0 copy-done.1
  52.8 0.0 copy-done.3
  52.8 6.8 %shard_map.58 = bf16[64,2,3632]{2,1,0:T(2,128)(2,1)S(1)} custom-call(bf16[64,38,128]{2,1,0:T(8,128)(2,1)S(1)} %all_to_all.15.found_ref, bf16[64,2,2560]{2,1,0:T(2,128)(2,1)S(1)} %all-to-all-done.got_ref, bf16[2,1800,2432]{2,1,0:T(8,128)(2,1)S(1)} %bitcast.8, bf16[15,2432,128]{2,1,0:T(8,128)(2,1)S(1)} %copy-done.3, bf16[2,600,2432]{2,1,0:T(8,128)(2,1)S(1)} %copy-done.1), custom_call_target="tpu_custom_call" | custom-call | flops 20000000000 | bytes 60000000 | tf_op jit(solution)/shard_map/pallas_call | solution.py:162
  59.7 22.7 %all_to_all.16.got_ref = bf16[64,2,3632]{2,1,0:T(2,128)(2,1)S(1)} all-to-all(bf16[64,2,3632]{2,1,0:T(2,128)(2,1)S(1)} %shard_map.58), channel_id=1, replica_groups=mesh['song'=2,'seq'=64] {'seq'}, dimensions={0} | all-to-all | bytes 1859584 | tf_op jit(solution)/shard_map/all_to_all | solution.py:334
  82.4 4.4 %shard_map.59 = bf16[128,2432]{1,0:T(8,128)(2,1)} custom-call(bf16[64,2,3632]{2,1,0:T(2,128)(2,1)S(1)} %all_to_all.16.got_ref, bf16[15,2432,128]{2,1,0:T(8,128)(2,1)S(1)} %copy-done.3, bf16[2,600,2432]{2,1,0:T(8,128)(2,1)S(1)} %copy-done.1), custom_call_target="tpu_custom_call" | custom-call | flops 20000000000 | bytes 60000000 | tf_op jit(solution)/shard_map/pallas_call | solution.py:231
Async XLA Ops:
  2.1 27.7 %all-to-all-start = ((bf16[64,2,2560]{2,1,0:T(2,128)(2,1)}), bf16[64,2,2560]{2,1,0:T(2,128)(2,1)S(1)}, u32[]{:S(2)}, u32[]{:S(2)}) async-start(bf16[64,2,2560]{2,1,0:T(2,128)(2,1)} %shard_map.55), calls=%async_computation | async-start | bytes 1310720 | tf_op jit(solution)/shard_map/all_to_all | solution.py:334
  14.6 15.6 %copy-start.2 = (bf16[2048,38]{0,1:T(8,128)(2,1)S(1)}, bf16[2048,38]{0,1:T(8,128)(2,1)}, u32[]{:S(2)}) copy-start(bf16[2048,38]{0,1:T(8,128)(2,1)} %param.6) | copy-start | bytes 466948
  30.2 22.6 %copy-start = (bf16[2,2432,1800]{1,2,0:T(8,128)(2,1)S(1)}, bf16[2,2432,1800]{1,2,0:T(8,128)(2,1)}, u32[]{:S(2)}) copy-start(bf16[2,2432,1800]{1,2,0:T(8,128)(2,1)} %param.8) | copy-start | bytes 52531204
  30.2 22.6 %copy-start.1 = (bf16[2,600,2432]{2,1,0:T(8,128)(2,1)S(1)}, bf16[2,600,2432]{2,1,0:T(8,128)(2,1)}, u32[]{:S(2)}) copy-start(bf16[2,600,2432]{2,1,0:T(8,128)(2,1)} %w_out_ref.3) | copy-start | bytes 17510404
  30.3 22.6 %copy-start.3 = (bf16[15,2432,128]{2,1,0:T(8,128)(2,1)S(1)}, bf16[15,2432,128]{2,1,0:T(8,128)(2,1)}, u32[]{:S(2)}) copy-start(bf16[15,2432,128]{2,1,0:T(8,128)(2,1)} %shard_map.56.strips_ref) | copy-start | bytes 28016644

commit v7 on v6

--- a/solution.py
+++ b/solution.py
@@ -14,6 +14,8 @@
 DIGIT = 64
 VMEM_LIMIT = 8 * 1024 * 1024
 PARTS = 8
+OUT_STEP = 512
+EARLY = (512, 1280)
 FULL_LIMIT = 60 * 1024 * 1024
 AT_ONCE = 4
 
@@ -45,17 +47,26 @@
     return pieces
 
 
-def flip_kernel(layer, stored_hbm, strips_hbm, stored_ref, strips_ref, sem):
+def flip_kernel(
+    stored_hbm, strips_hbm, early_hbm, stored_ref, strips_ref, early_in_ref, early_ref, sem
+):
     columns, width = stored_ref.shape
     step = columns // PARTS // 8 * 8
     cuts = [step * i for i in range(PARTS)] + [columns]
     fetch = [
         pltpu.make_async_copy(
-            stored_hbm.at[layer, low:high], stored_ref.at[low:high], sem.at[i]
+            stored_hbm.at[1, low:high], stored_ref.at[low:high], sem.at[i]
         )
         for i, (low, high) in enumerate(zip(cuts, cuts[1:]))
     ]
-    for copy in fetch:
+    extra = PARTS + strips_ref.shape[0]
+    early = [
+        pltpu.make_async_copy(
+            stored_hbm.at[0, low : low + 256], early_in_ref.at[i], sem.at[extra + i]
+        )
+        for i, low in enumerate(EARLY)
+    ]
+    for copy in fetch + early:
         copy.start()
     ready = 0
     store = []
@@ -71,22 +82,34 @@
         strips_ref[j] = jnp.transpose(jnp.concatenate(rows, axis=0))
         store.append(pltpu.make_async_copy(strips_ref.at[j], strips_hbm.at[j], sem.at[PARTS + j]))
         store[-1].start()
+    extra += len(EARLY)
+    for i, copy in enumerate(early):
+        copy.wait()
+        early_ref[i] = jnp.transpose(early_in_ref[i])
+        store.append(pltpu.make_async_copy(early_ref.at[i], early_hbm.at[i], sem.at[extra + i]))
+        store[-1].start()
     for copy in fetch[ready:] + store:
         copy.wait()
 
 
-def flip(stored, layer):
+def flip(stored):
     _, columns, width = stored.shape
     shape = (-(-columns // 128), width, 128)
+    count = len(EARLY)
     return pl.pallas_call(
-        functools.partial(flip_kernel, layer),
-        out_shape=jax.ShapeDtypeStruct(shape, jnp.bfloat16),
+        flip_kernel,
+        out_shape=(
+            jax.ShapeDtypeStruct(shape, jnp.bfloat16),
+            jax.ShapeDtypeStruct((count, width, 256), jnp.bfloat16),
+        ),
         in_specs=[pl.BlockSpec(memory_space=pl.ANY)],
-        out_specs=pl.BlockSpec(memory_space=pl.ANY),
+        out_specs=(pl.BlockSpec(memory_space=pl.ANY),) * 2,
         scratch_shapes=[
             pltpu.VMEM((columns, width), jnp.bfloat16),
             pltpu.VMEM(shape, jnp.bfloat16),
-            pltpu.SemaphoreType.DMA((PARTS + shape[0],)),
+            pltpu.VMEM((count, 256, width), jnp.bfloat16),
+            pltpu.VMEM((count, width, 256), jnp.bfloat16),
+            pltpu.SemaphoreType.DMA((PARTS + shape[0] + 2 * count,)),
         ],
         cost_estimate=hint(10),
         compiler_params=pltpu.CompilerParams(vmem_limit_bytes=FULL_LIMIT),
@@ -114,7 +137,10 @@
     )
 
 
-def column_kernel(found_ref, got_ref, w_in_ref, strips_ref, w_out_ref, out_ref, flat_ref, x_ref, normed_ref, keyed_ref):
+def column_kernel(
+    found_ref, got_ref, w_in_ref, strips_ref, early_ref, w_out_ref, out_ref,
+    flat_ref, x_ref, normed_ref, joined_ref, keyed_ref,
+):
     rows, depth, tokens = found_ref.shape
     per = out_ref.shape[1]
     width = w_in_ref.shape[2]
@@ -125,9 +151,19 @@
     for i in range(0, width, 128):
         x_ref[:, i : i + 128] += jnp.transpose(flat_ref[i : i + 128])
     normalize(x_ref, normed_ref)
-    joined = lax.dot_general(
-        normed_ref[...], w_in_ref[0], (((1,), (1,)), ((), ())), preferred_element_type=jnp.float32
-    ).astype(jnp.bfloat16)
+    columns = joined_ref.shape[1]
+    stop = 0
+    for i, low in enumerate(EARLY + (columns,)):
+        if stop < low:
+            joined_ref[:, stop:low] = product(
+                normed_ref[...], w_in_ref[0, stop:low], (1, 1)
+            ).astype(jnp.bfloat16)
+        if low < columns:
+            joined_ref[:, low : low + 256] = product(
+                normed_ref[...], early_ref[i], (1, 0)
+            ).astype(jnp.bfloat16)
+        stop = low + 256
+    joined = joined_ref[...]
     key_of = lax.broadcasted_iota(jnp.int32, (tokens, tokens), 0)
     query_of = lax.broadcasted_iota(jnp.int32, (tokens, tokens), 1)
     allowed = (key_of % per == query_of % per) & (key_of <= query_of)
@@ -144,7 +180,11 @@
     mixed = jnp.concatenate(
         [product(p, v, (0, 0)).astype(jnp.bfloat16) for p, v in zip(probs, value)], axis=1
     )
-    x_ref[...] += jnp.dot(mixed, w_out_ref[0], preferred_element_type=jnp.float32)
+    for i in range(0, width, OUT_STEP):
+        span = slice(i, min(i + OUT_STEP, width))
+        x_ref[:, span] += jnp.dot(
+            mixed, w_out_ref[0, :, span], preferred_element_type=jnp.float32
+        )
     normalize(x_ref, normed_ref)
     joint(normed_ref, strips_ref, keyed_ref)
     resid = x_ref[...].astype(jnp.bfloat16)
@@ -155,24 +195,25 @@
             out_ref[r + 1, :, width:] = keyed_ref[r * per : (r + 1) * per]
 
 
-def column_sublayer(found, got, w_in, strips, w_out):
+def column_sublayer(found, got, w_in, strips, early, w_out):
     rows, depth, tokens = found.shape
     width = w_in.shape[2]
     per = tokens // rows
     return pl.pallas_call(
         column_kernel,
         out_shape=jax.ShapeDtypeStruct((rows, per, width + 2 * HEADS * HEAD), jnp.bfloat16),
-        in_specs=[pl.BlockSpec(memory_space=pltpu.VMEM)] * 5,
+        in_specs=[pl.BlockSpec(memory_space=pltpu.VMEM)] * 6,
         out_specs=pl.BlockSpec(memory_space=pltpu.VMEM),
         scratch_shapes=[
             pltpu.VMEM((width, tokens), jnp.float32),
             pltpu.VMEM((tokens, width), jnp.float32),
             pltpu.VMEM((tokens, width), jnp.bfloat16),
+            pltpu.VMEM((tokens, 3 * HEADS * HEAD), jnp.bfloat16),
             pltpu.VMEM((tokens, 2 * HEADS * HEAD), jnp.bfloat16),
         ],
         cost_estimate=hint(20),
         compiler_params=pltpu.CompilerParams(vmem_limit_bytes=VMEM_LIMIT),
-    )(found, got, w_in, strips, w_out)
+    )(found, got, w_in, strips, early, w_out)
 
 
 def row_kernel(got_ref, strips_ref, w_out_ref, out_ref, x_ref, normed_ref, before_ref, joined_ref):
@@ -219,9 +260,12 @@
         ],
         axis=1,
     )
-    out_ref[...] = (
-        x_ref[...] + jnp.dot(mixed, w_out_ref[1], preferred_element_type=jnp.float32)
-    ).astype(jnp.bfloat16)
+    for i in range(0, width, OUT_STEP):
+        span = slice(i, min(i + OUT_STEP, width))
+        out_ref[:, span] = (
+            x_ref[:, span]
+            + jnp.dot(mixed, w_out_ref[1, :, span], preferred_element_type=jnp.float32)
+        ).astype(jnp.bfloat16)
 
 
 def row_sublayer(got, strips, w_out):
@@ -257,11 +301,12 @@
         [flipped[:, g * step : (g + 1) * step] for g in range(GROUPS)], axis=0
     ).astype(jnp.bfloat16)
     slots = lax.broadcasted_iota(jnp.int32, (step, AT_ONCE * 128), 0)
+    slots = slots.astype(jnp.float32).astype(jnp.bfloat16)
     for d in range(0, count, AT_ONCE):
         codes = jnp.concatenate([codes_ref[d + e : d + e + 1, :] for e in range(AT_ONCE)], axis=1)
-        low = codes % step
+        low = (codes % step).astype(jnp.float32).astype(jnp.bfloat16)
         high = codes // step
-        onehot = jnp.where(slots == low, 1.0, 0.0).astype(jnp.bfloat16)
+        onehot = jnp.where(slots == low, jnp.bfloat16(1), jnp.bfloat16(0))
         found = jnp.dot(stacked, onehot, preferred_element_type=jnp.float32)
         chosen = jnp.zeros((padded, AT_ONCE * 128), jnp.float32)
         for g in range(GROUPS):
@@ -341,12 +386,12 @@
 
     got = exchange(pack(song_ids, position_table, rows))
     w_in = jnp.swapaxes(w_qkv, 1, 2)
-    strips = flip(w_in, 1)
-    got, strips = lax.optimization_barrier((got, strips))
+    strips, early = flip(w_in)
+    got, strips, early = lax.optimization_barrier((got, strips, early))
     codes = got[:, 0, width:].astype(jnp.int32) * DIGIT + got[:, 1, width:].astype(jnp.int32)
     codes = jnp.transpose(codes.reshape(rows, rows, per), (1, 0, 2)).reshape(rows, tokens)
     found = exchange(lookup(codes, jnp.transpose(table)))
-    got = exchange(column_sublayer(found, got, w_in, strips, w_out))
+    got = exchange(column_sublayer(found, got, w_in, strips, early, w_out))
     return row_sublayer(got, strips, w_out)
 
 

time: 87.1 us -> 85.8 us (0.985)
  transfers between devices with their start and end apart: 1 -> 1, of which waited for: 1 -> 1; matrix products, arithmetic and copies ran while one was open for 0% -> 0% of each run, Pallas kernels for 9% -> 10%
where the time goes in v7:
time: 85.8 us; the launch traced here: 85.5 us
  blocking collectives  42.7 us (50%)
  Pallas kernels  22.9 us (27%)
  starting transfers between devices  12.5 us (15%)
  waiting for transfers between devices  6.84 us (8%)
    all_to_all x2, blocking collectives, exchange(): return lax.all_to_all(value, 'seq', split_axis=0, concat_axis=0, tiled=True)  42.7 us
    all_to_all x1, starting transfers between devices, exchange(): return lax.all_to_all(value, 'seq', split_axis=0, concat_axis=0, tiled=True)  12.5 us
    pallas_call x1, Pallas kernels, flip(): pl.pallas_call(flip_kernel, out_shape=(jax.ShapeDtypeStruct(shape, jnp.bf...  8.39 us
    all_to_all x1, waiting for transfers between devices, exchange(): return lax.all_to_all(value, 'seq', split_axis=0, concat_axis=0, tiled=True)  6.84 us
    pallas_call x1, Pallas kernels, column_sublayer(): pl.pallas_call(column_kernel, out_shape=jax.ShapeDtypeStruct((rows, per,...  6.38 us
    pallas_call x1, Pallas kernels, row_sublayer(): pl.pallas_call(row_kernel, out_shape=jax.ShapeDtypeStruct((tokens, width)...  4.43 us
    pallas_call x1, Pallas kernels, pack(): pl.pallas_call(pack_kernel, out_shape=jax.ShapeDtypeStruct(shape, jnp.bfl...  2.09 us
  transfers between devices with their start and end apart: 1, of which 1 were waited for; matrix products, arithmetic and copies ran while one was open for 0% of the time, Pallas kernels for 10%

profile of v7, /device:TPU:1, one launch (start us, length us, event | category | flops | bytes accessed | tf_op | source)
XLA Modules:
  0.0 85.5 jit_solution(8518891558891986112)
XLA Ops:
  0.0 2.1 %shard_map.55 = bf16[64,2,2560]{2,1,0:T(2,128)(2,1)} custom-call(s32[1,128]{1,0:T(1,128)} %bitcast.12, bf16[128,2432]{1,0:T(8,128)(2,1)} %position_hbm.1), custom_call_target="tpu_custom_call" | custom-call | flops 60000002048 | bytes 180000000 | tf_op jit(solution)/shard_map/pallas_call | solution.py:362
  2.1 12.5 %all-to-all-start = ((bf16[64,2,2560]{2,1,0:T(2,128)(2,1)}), bf16[64,2,2560]{2,1,0:T(2,128)(2,1)S(1)}, u32[]{:S(2)}, u32[]{:S(2)}) async-start(bf16[64,2,2560]{2,1,0:T(2,128)(2,1)} %shard_map.55), calls=%async_computation | async-start | bytes 1310720 | tf_op jit(solution)/shard_map/all_to_all | solution.py:379
  14.6 0.0 copy-start.2
  14.6 8.4 %shard_map.56 = (bf16[15,2432,128]{2,1,0:T(8,128)(2,1)}, bf16[2,2432,256]{2,1,0:T(8,128)(2,1)}) custom-call(bf16[2,1800,2432]{2,1,0:T(8,128)(2,1)} %bitcast.7), custom_call_target="tpu_custom_call" | custom-call | flops 10000000000 | bytes 30000000 | tf_op jit(solution)/shard_map/pallas_call | solution.py:99
  23.0 6.8 %all-to-all-done.got_ref = bf16[64,2,2560]{2,1,0:T(2,128)(2,1)S(1)} async-done(((bf16[64,2,2560]{2,1,0:T(2,128)(2,1)}), bf16[64,2,2560]{2,1,0:T(2,128)(2,1)S(1)}, u32[]{:S(2)}, u32[]{:S(2)}) %all-to-all-start) | async-done | bytes 655392 | tf_op jit(solution)/shard_map/all_to_all | solution.py:379
  29.8 0.1 convert_add_fusion
  29.9 0.1 copy.10
  30.0 0.1 copy.11
  30.1 0.1 copy.12.codes_ref
  30.2 0.0 copy-done.2
  30.2 0.0 copy-start
  30.2 0.0 copy-start.1
  30.3 0.0 copy-start.3
  30.3 0.0 copy-start.4
  30.3 1.6 %shard_map.57 = bf16[64,38,128]{2,1,0:T(8,128)(2,1)S(1)} custom-call(s32[64,128]{1,0:T(8,128)S(1)} %copy.12.codes_ref, bf16[38,2048]{1,0:T(8,128)(2,1)S(1)} %bitcast.9), custom_call_target="tpu_custom_call" | custom-call | flops 140000002048 | bytes 420000000 | tf_op jit(solution)/shard_map/pallas_call | solution.py:321
  31.9 20.1 %all_to_all.15.found_ref = bf16[64,38,128]{2,1,0:T(8,128)(2,1)S(1)} all-to-all(bf16[64,38,128]{2,1,0:T(8,128)(2,1)S(1)} %shard_map.57), channel_id=1, replica_groups=mesh['song'=2,'seq'=64] {'seq'}, dimensions={0} | all-to-all | bytes 1245184 | tf_op jit(solution)/shard_map/all_to_all | solution.py:379
  52.0 0.0 copy-done
  52.0 0.0 copy-done.1
  52.0 0.0 copy-done.3
  52.0 0.0 copy-done.4
  52.0 6.4 %shard_map.58 = bf16[64,2,3632]{2,1,0:T(2,128)(2,1)S(1)} custom-call(bf16[64,38,128]{2,1,0:T(8,128)(2,1)S(1)} %all_to_all.15.found_ref, bf16[64,2,2560]{2,1,0:T(2,128)(2,1)S(1)} %all-to-all-done.got_ref, bf16[2,1800,2432]{2,1,0:T(8,128)(2,1)S(1)} %bitcast.8, bf16[15,2432,128]{2,1,0:T(8,128)(2,1)S(1)} %copy-done.3, bf16[2,2432,256]{2,1,0:T(8,128)(2,1)S(1)} %copy-done.4, ...), custom_call_target="tpu_custom_call" | custom-call | flops 20000000000 | bytes 60000000 | tf_op jit(solution)/shard_map/pallas_call | solution.py:202
  58.4 22.7 %all_to_all.16.got_ref = bf16[64,2,3632]{2,1,0:T(2,128)(2,1)S(1)} all-to-all(bf16[64,2,3632]{2,1,0:T(2,128)(2,1)S(1)} %shard_map.58), channel_id=1, replica_groups=mesh['song'=2,'seq'=64] {'seq'}, dimensions={0} | all-to-all | bytes 1859584 | tf_op jit(solution)/shard_map/all_to_all | solution.py:379
  81.1 4.4 %shard_map.59 = bf16[128,2432]{1,0:T(8,128)(2,1)} custom-call(bf16[64,2,3632]{2,1,0:T(2,128)(2,1)S(1)} %all_to_all.16.got_ref, bf16[15,2432,128]{2,1,0:T(8,128)(2,1)S(1)} %copy-done.3, bf16[2,600,2432]{2,1,0:T(8,128)(2,1)S(1)} %copy-done.1), custom_call_target="tpu_custom_call" | custom-call | flops 20000000000 | bytes 60000000 | tf_op jit(solution)/shard_map/pallas_call | solution.py:275
Async XLA Ops:
  2.1 27.7 %all-to-all-start = ((bf16[64,2,2560]{2,1,0:T(2,128)(2,1)}), bf16[64,2,2560]{2,1,0:T(2,128)(2,1)S(1)}, u32[]{:S(2)}, u32[]{:S(2)}) async-start(bf16[64,2,2560]{2,1,0:T(2,128)(2,1)} %shard_map.55), calls=%async_computation | async-start | bytes 1310720 | tf_op jit(solution)/shard_map/all_to_all | solution.py:379
  14.6 15.6 %copy-start.2 = (bf16[2048,38]{0,1:T(8,128)(2,1)S(1)}, bf16[2048,38]{0,1:T(8,128)(2,1)}, u32[]{:S(2)}) copy-start(bf16[2048,38]{0,1:T(8,128)(2,1)} %param.6) | copy-start | bytes 466948
  30.2 21.8 %copy-start = (bf16[2,2432,1800]{1,2,0:T(8,128)(2,1)S(1)}, bf16[2,2432,1800]{1,2,0:T(8,128)(2,1)}, u32[]{:S(2)}) copy-start(bf16[2,2432,1800]{1,2,0:T(8,128)(2,1)} %param.8) | copy-start | bytes 52531204
  30.2 21.7 %copy-start.1 = (bf16[2,600,2432]{2,1,0:T(8,128)(2,1)S(1)}, bf16[2,600,2432]{2,1,0:T(8,128)(2,1)}, u32[]{:S(2)}) copy-start(bf16[2,600,2432]{2,1,0:T(8,128)(2,1)} %w_out_ref.3) | copy-start | bytes 17510404
  30.3 21.7 %copy-start.3 = (bf16[15,2432,128]{2,1,0:T(8,128)(2,1)S(1)}, bf16[15,2432,128]{2,1,0:T(8,128)(2,1)}, u32[]{:S(2)}) copy-start(bf16[15,2432,128]{2,1,0:T(8,128)(2,1)} %get-tuple-element.13.strips_ref) | copy-start | bytes 28016644
  30.3 21.7 %copy-start.4 = (bf16[2,2432,256]{2,1,0:T(8,128)(2,1)S(1)}, bf16[2,2432,256]{2,1,0:T(8,128)(2,1)}, u32[]{:S(2)}) copy-start(bf16[2,2432,256]{2,1,0:T(8,128)(2,1)} %get-tuple-element.14.early_ref) | copy-start | bytes 7471108

commit v8 on v7

--- a/solution.py
+++ b/solution.py
@@ -15,7 +15,7 @@
 VMEM_LIMIT = 8 * 1024 * 1024
 PARTS = 8
 OUT_STEP = 512
-EARLY = (512, 1280)
+EARLY = (128, 384, 640, 896)
 FULL_LIMIT = 60 * 1024 * 1024
 AT_ONCE = 4
 
@@ -62,7 +62,7 @@
     extra = PARTS + strips_ref.shape[0]
     early = [
         pltpu.make_async_copy(
-            stored_hbm.at[0, low : low + 256], early_in_ref.at[i], sem.at[extra + i]
+            stored_hbm.at[0, low : low + 128], early_in_ref.at[i], sem.at[extra + i]
         )
         for i, low in enumerate(EARLY)
     ]
@@ -100,15 +100,15 @@
         flip_kernel,
         out_shape=(
             jax.ShapeDtypeStruct(shape, jnp.bfloat16),
-            jax.ShapeDtypeStruct((count, width, 256), jnp.bfloat16),
+            jax.ShapeDtypeStruct((count, width, 128), jnp.bfloat16),
         ),
         in_specs=[pl.BlockSpec(memory_space=pl.ANY)],
         out_specs=(pl.BlockSpec(memory_space=pl.ANY),) * 2,
         scratch_shapes=[
             pltpu.VMEM((columns, width), jnp.bfloat16),
             pltpu.VMEM(shape, jnp.bfloat16),
-            pltpu.VMEM((count, 256, width), jnp.bfloat16),
-            pltpu.VMEM((count, width, 256), jnp.bfloat16),
+            pltpu.VMEM((count, 128, width), jnp.bfloat16),
+            pltpu.VMEM((count, width, 128), jnp.bfloat16),
             pltpu.SemaphoreType.DMA((PARTS + shape[0] + 2 * count,)),
         ],
         cost_estimate=hint(10),
@@ -151,18 +151,17 @@
     for i in range(0, width, 128):
         x_ref[:, i : i + 128] += jnp.transpose(flat_ref[i : i + 128])
     normalize(x_ref, normed_ref)
-    columns = joined_ref.shape[1]
-    stop = 0
-    for i, low in enumerate(EARLY + (columns,)):
-        if stop < low:
-            joined_ref[:, stop:low] = product(
-                normed_ref[...], w_in_ref[0, stop:low], (1, 1)
-            ).astype(jnp.bfloat16)
-        if low < columns:
-            joined_ref[:, low : low + 256] = product(
-                normed_ref[...], early_ref[i], (1, 0)
-            ).astype(jnp.bfloat16)
-        stop = low + 256
+    for i, low in enumerate(EARLY):
+        weight = jnp.concatenate(
+            [jnp.transpose(w_in_ref[0, low - 128 : low]), early_ref[i]], axis=1
+        )
+        joined_ref[:, low - 128 : low + 128] = product(
+            normed_ref[...], weight, (1, 0)
+        ).astype(jnp.bfloat16)
+    stop = EARLY[-1] + 128
+    joined_ref[:, stop:] = product(
+        normed_ref[...], w_in_ref[0, stop:], (1, 1)
+    ).astype(jnp.bfloat16)
     joined = joined_ref[...]
     key_of = lax.broadcasted_iota(jnp.int32, (tokens, tokens), 0)
     query_of = lax.broadcasted_iota(jnp.int32, (tokens, tokens), 1)

time: 85.8 us -> 85.5 us (level)
  no operation moved by 1% of the time
where the time goes in v8:
time: 85.5 us; the launch traced here: 85.2 us
  blocking collectives  42.7 us (50%)
  Pallas kernels  22.7 us (27%)
  starting transfers between devices  12.5 us (15%)
  waiting for transfers between devices  6.81 us (8%)
    all_to_all x2, blocking collectives, exchange(): return lax.all_to_all(value, 'seq', split_axis=0, concat_axis=0, tiled=True)  42.7 us
    all_to_all x1, starting transfers between devices, exchange(): return lax.all_to_all(value, 'seq', split_axis=0, concat_axis=0, tiled=True)  12.5 us
    pallas_call x1, Pallas kernels, flip(): pl.pallas_call(flip_kernel, out_shape=(jax.ShapeDtypeStruct(shape, jnp.bf...  8.42 us
    all_to_all x1, waiting for transfers between devices, exchange(): return lax.all_to_all(value, 'seq', split_axis=0, concat_axis=0, tiled=True)  6.81 us
    pallas_call x1, Pallas kernels, column_sublayer(): pl.pallas_call(column_kernel, out_shape=jax.ShapeDtypeStruct((rows, per,...  6.08 us
    pallas_call x1, Pallas kernels, row_sublayer(): pl.pallas_call(row_kernel, out_shape=jax.ShapeDtypeStruct((tokens, width)...  4.43 us
    pallas_call x1, Pallas kernels, pack(): pl.pallas_call(pack_kernel, out_shape=jax.ShapeDtypeStruct(shape, jnp.bfl...  2.09 us
  transfers between devices with their start and end apart: 1, of which 1 were waited for; matrix products, arithmetic and copies ran while one was open for 0% of the time, Pallas kernels for 10%

profile of v8, /device:TPU:1, one launch (start us, length us, event | category | flops | bytes accessed | tf_op | source)
XLA Modules:
  0.0 85.2 jit_solution(9531531174661482960)
XLA Ops:
  0.0 2.1 %shard_map.55 = bf16[64,2,2560]{2,1,0:T(2,128)(2,1)} custom-call(s32[1,128]{1,0:T(1,128)} %bitcast.12, bf16[128,2432]{1,0:T(8,128)(2,1)} %position_hbm.1), custom_call_target="tpu_custom_call" | custom-call | flops 60000002048 | bytes 180000000 | tf_op jit(solution)/shard_map/pallas_call | solution.py:361
  2.1 12.5 %all-to-all-start = ((bf16[64,2,2560]{2,1,0:T(2,128)(2,1)}), bf16[64,2,2560]{2,1,0:T(2,128)(2,1)S(1)}, u32[]{:S(2)}, u32[]{:S(2)}) async-start(bf16[64,2,2560]{2,1,0:T(2,128)(2,1)} %shard_map.55), calls=%async_computation | async-start | bytes 1310720 | tf_op jit(solution)/shard_map/all_to_all | solution.py:378
  14.6 0.0 copy-start.2
  14.6 8.4 %shard_map.56 = (bf16[15,2432,128]{2,1,0:T(8,128)(2,1)}, bf16[4,2432,128]{2,1,0:T(8,128)(2,1)}) custom-call(bf16[2,1800,2432]{2,1,0:T(8,128)(2,1)} %bitcast.7), custom_call_target="tpu_custom_call" | custom-call | flops 10000000000 | bytes 30000000 | tf_op jit(solution)/shard_map/pallas_call | solution.py:99
  23.0 6.8 %all-to-all-done.got_ref = bf16[64,2,2560]{2,1,0:T(2,128)(2,1)S(1)} async-done(((bf16[64,2,2560]{2,1,0:T(2,128)(2,1)}), bf16[64,2,2560]{2,1,0:T(2,128)(2,1)S(1)}, u32[]{:S(2)}, u32[]{:S(2)}) %all-to-all-start) | async-done | bytes 655392 | tf_op jit(solution)/shard_map/all_to_all | solution.py:378
  29.8 0.1 convert_add_fusion
  29.9 0.1 copy.10
  30.0 0.1 copy.11
  30.1 0.1 copy.12.codes_ref
  30.2 0.0 copy-done.2
  30.2 0.0 copy-start
  30.2 0.0 copy-start.1
  30.3 0.0 copy-start.3
  30.3 0.0 copy-start.4
  30.3 1.6 %shard_map.57 = bf16[64,38,128]{2,1,0:T(8,128)(2,1)S(1)} custom-call(s32[64,128]{1,0:T(8,128)S(1)} %copy.12.codes_ref, bf16[38,2048]{1,0:T(8,128)(2,1)S(1)} %bitcast.9), custom_call_target="tpu_custom_call" | custom-call | flops 140000002048 | bytes 420000000 | tf_op jit(solution)/shard_map/pallas_call | solution.py:320
  31.9 20.1 %all_to_all.15.found_ref = bf16[64,38,128]{2,1,0:T(8,128)(2,1)S(1)} all-to-all(bf16[64,38,128]{2,1,0:T(8,128)(2,1)S(1)} %shard_map.57), channel_id=1, replica_groups=mesh['song'=2,'seq'=64] {'seq'}, dimensions={0} | all-to-all | bytes 1245184 | tf_op jit(solution)/shard_map/all_to_all | solution.py:378
  52.0 0.0 copy-done
  52.0 0.0 copy-done.1
  52.0 0.0 copy-done.3
  52.0 0.0 copy-done.4
  52.0 6.1 %shard_map.58 = bf16[64,2,3632]{2,1,0:T(2,128)(2,1)S(1)} custom-call(bf16[64,38,128]{2,1,0:T(8,128)(2,1)S(1)} %all_to_all.15.found_ref, bf16[64,2,2560]{2,1,0:T(2,128)(2,1)S(1)} %all-to-all-done.got_ref, bf16[2,1800,2432]{2,1,0:T(8,128)(2,1)S(1)} %bitcast.8, bf16[15,2432,128]{2,1,0:T(8,128)(2,1)S(1)} %copy-done.3, bf16[4,2432,128]{2,1,0:T(8,128)(2,1)S(1)} %copy-done.4, ...), custom_call_target="tpu_custom_call" | custom-call | flops 20000000000 | bytes 60000000 | tf_op jit(solution)/shard_map/pallas_call | solution.py:201
  58.1 22.7 %all_to_all.16.got_ref = bf16[64,2,3632]{2,1,0:T(2,128)(2,1)S(1)} all-to-all(bf16[64,2,3632]{2,1,0:T(2,128)(2,1)S(1)} %shard_map.58), channel_id=1, replica_groups=mesh['song'=2,'seq'=64] {'seq'}, dimensions={0} | all-to-all | bytes 1859584 | tf_op jit(solution)/shard_map/all_to_all | solution.py:378
  80.8 4.4 %shard_map.59 = bf16[128,2432]{1,0:T(8,128)(2,1)} custom-call(bf16[64,2,3632]{2,1,0:T(2,128)(2,1)S(1)} %all_to_all.16.got_ref, bf16[15,2432,128]{2,1,0:T(8,128)(2,1)S(1)} %copy-done.3, bf16[2,600,2432]{2,1,0:T(8,128)(2,1)S(1)} %copy-done.1), custom_call_target="tpu_custom_call" | custom-call | flops 20000000000 | bytes 60000000 | tf_op jit(solution)/shard_map/pallas_call | solution.py:274
Async XLA Ops:
  2.1 27.7 %all-to-all-start = ((bf16[64,2,2560]{2,1,0:T(2,128)(2,1)}), bf16[64,2,2560]{2,1,0:T(2,128)(2,1)S(1)}, u32[]{:S(2)}, u32[]{:S(2)}) async-start(bf16[64,2,2560]{2,1,0:T(2,128)(2,1)} %shard_map.55), calls=%async_computation | async-start | bytes 1310720 | tf_op jit(solution)/shard_map/all_to_all | solution.py:378
  14.6 15.6 %copy-start.2 = (bf16[2048,38]{0,1:T(8,128)(2,1)S(1)}, bf16[2048,38]{0,1:T(8,128)(2,1)}, u32[]{:S(2)}) copy-start(bf16[2048,38]{0,1:T(8,128)(2,1)} %param.6) | copy-start | bytes 466948
  30.2 21.8 %copy-start = (bf16[2,2432,1800]{1,2,0:T(8,128)(2,1)S(1)}, bf16[2,2432,1800]{1,2,0:T(8,128)(2,1)}, u32[]{:S(2)}) copy-start(bf16[2,2432,1800]{1,2,0:T(8,128)(2,1)} %param.8) | copy-start | bytes 52531204
  30.2 21.7 %copy-start.1 = (bf16[2,600,2432]{2,1,0:T(8,128)(2,1)S(1)}, bf16[2,600,2432]{2,1,0:T(8,128)(2,1)}, u32[]{:S(2)}) copy-start(bf16[2,600,2432]{2,1,0:T(8,128)(2,1)} %w_out_ref.3) | copy-start | bytes 17510404
  30.3 21.7 %copy-start.3 = (bf16[15,2432,128]{2,1,0:T(8,128)(2,1)S(1)}, bf16[15,2432,128]{2,1,0:T(8,128)(2,1)}, u32[]{:S(2)}) copy-start(bf16[15,2432,128]{2,1,0:T(8,128)(2,1)} %get-tuple-element.13.strips_ref) | copy-start | bytes 28016644
  30.3 21.7 %copy-start.4 = (bf16[4,2432,128]{2,1,0:T(8,128)(2,1)S(1)}, bf16[4,2432,128]{2,1,0:T(8,128)(2,1)}, u32[]{:S(2)}) copy-start(bf16[4,2432,128]{2,1,0:T(8,128)(2,1)} %get-tuple-element.14.early_ref) | copy-start | bytes 7471108

commit v9 on v8

--- a/solution.py
+++ b/solution.py
@@ -145,11 +145,13 @@
     per = out_ref.shape[1]
     width = w_in_ref.shape[2]
     for s in range(rows):
-        flat_ref[s * depth : (s + 1) * depth] = found_ref[s].astype(jnp.float32)
+        flat_ref[s * depth : (s + 1) * depth] = found_ref[s]
     for r in range(rows):
-        x_ref[r * per : (r + 1) * per] = got_ref[r, :, :width].astype(jnp.float32)
+        normed_ref[r * per : (r + 1) * per] = got_ref[r, :, :width]
     for i in range(0, width, 128):
-        x_ref[:, i : i + 128] += jnp.transpose(flat_ref[i : i + 128])
+        x_ref[:, i : i + 128] = jnp.transpose(flat_ref[i : i + 128]).astype(
+            jnp.float32
+        ) + normed_ref[:, i : i + 128].astype(jnp.float32)
     normalize(x_ref, normed_ref)
     for i, low in enumerate(EARLY):
         weight = jnp.concatenate(
@@ -204,7 +206,7 @@
         in_specs=[pl.BlockSpec(memory_space=pltpu.VMEM)] * 6,
         out_specs=pl.BlockSpec(memory_space=pltpu.VMEM),
         scratch_shapes=[
-            pltpu.VMEM((width, tokens), jnp.float32),
+            pltpu.VMEM((width, tokens), jnp.bfloat16),
             pltpu.VMEM((tokens, width), jnp.float32),
             pltpu.VMEM((tokens, width), jnp.bfloat16),
             pltpu.VMEM((tokens, 3 * HEADS * HEAD), jnp.bfloat16),
@@ -221,8 +223,9 @@
     has_before = lax.axis_index("seq") > 0
     inv_root = 1.0 / math.sqrt(HEAD)
     for r in range(rows):
-        x_ref[r * per : (r + 1) * per] = got_ref[r, :, :width].astype(jnp.float32)
+        normed_ref[r * per : (r + 1) * per] = got_ref[r, :, :width]
         before_ref[r * per : (r + 1) * per] = got_ref[r, :, width:]
+    x_ref[...] = normed_ref[...].astype(jnp.float32)
     normalize(x_ref, normed_ref)
     joint(normed_ref, strips_ref, joined_ref)
     joined = joined_ref[...]
@@ -287,7 +290,7 @@
     )(got, strips, w_out)
 
 
-def lookup_kernel(codes_ref, table_ref, out_ref):
+def lookup_kernel(got_ref, table_ref, out_ref, turned_ref, codes_ref):
     depth, entries = table_ref.shape
     step = entries // GROUPS
     count = out_ref.shape[0]
@@ -299,6 +302,23 @@
     stacked = jnp.concatenate(
         [flipped[:, g * step : (g + 1) * step] for g in range(GROUPS)], axis=0
     ).astype(jnp.bfloat16)
+    rows, per, total = got_ref.shape
+    tokens = rows * per
+    for i in range(2):
+        digits = got_ref[:, i, total - tokens :].astype(jnp.float32)
+        turned_ref[i] = jnp.transpose(
+            jnp.concatenate([digits, jnp.zeros((tokens - rows, tokens), jnp.float32)], axis=0)
+        )
+    row_of = lax.broadcasted_iota(jnp.int32, (tokens, tokens), 0)
+    place_of = lax.broadcasted_iota(jnp.int32, (tokens, tokens), 1)
+    moved = jnp.zeros((2 * rows, tokens), jnp.float32)
+    for c in range(per):
+        picked = jnp.concatenate(
+            [turned_ref[i, pl.ds(c, rows, stride=per), :] for i in range(2)], axis=0
+        ).astype(jnp.bfloat16)
+        spread = jnp.where(place_of == per * row_of + c, 1.0, 0.0).astype(jnp.bfloat16)
+        moved += jnp.dot(picked, spread, preferred_element_type=jnp.float32)
+    codes_ref[...] = moved[:rows].astype(jnp.int32) * DIGIT + moved[rows:].astype(jnp.int32)
     slots = lax.broadcasted_iota(jnp.int32, (step, AT_ONCE * 128), 0)
     slots = slots.astype(jnp.float32).astype(jnp.bfloat16)
     for d in range(0, count, AT_ONCE):
@@ -314,17 +334,22 @@
             out_ref[d + e] = chosen[:depth, e * 128 : (e + 1) * 128].astype(jnp.bfloat16)
 
 
-def lookup(codes, table):
-    count = codes.shape[0]
+def lookup(got, table):
+    count = got.shape[0]
+    tokens = count * got.shape[1]
     depth = table.shape[0]
     return pl.pallas_call(
         lookup_kernel,
         out_shape=jax.ShapeDtypeStruct((count, depth, 128), jnp.bfloat16),
         in_specs=[pl.BlockSpec(memory_space=pltpu.VMEM)] * 2,
         out_specs=pl.BlockSpec(memory_space=pltpu.VMEM),
+        scratch_shapes=[
+            pltpu.VMEM((2, tokens, tokens), jnp.float32),
+            pltpu.VMEM((count, tokens), jnp.int32),
+        ],
         cost_estimate=hint(140),
         compiler_params=pltpu.CompilerParams(vmem_limit_bytes=VMEM_LIMIT),
-    )(codes, table)
+    )(got, table)
 
 
 def pack_kernel(codes_hbm, position_hbm, out_hbm, codes_ref, position_ref, out_ref, sem):
@@ -387,9 +412,7 @@
     w_in = jnp.swapaxes(w_qkv, 1, 2)
     strips, early = flip(w_in)
     got, strips, early = lax.optimization_barrier((got, strips, early))
-    codes = got[:, 0, width:].astype(jnp.int32) * DIGIT + got[:, 1, width:].astype(jnp.int32)
-    codes = jnp.transpose(codes.reshape(rows, rows, per), (1, 0, 2)).reshape(rows, tokens)
-    found = exchange(lookup(codes, jnp.transpose(table)))
+    found = exchange(lookup(got, jnp.transpose(table)))
     got = exchange(column_sublayer(found, got, w_in, strips, early, w_out))
     return row_sublayer(got, strips, w_out)
 

time: 85.5 us -> 85.4 us (level)
  no operation moved by 1% of the time
where the time goes in v9:
time: 85.4 us; the launch traced here: 85.1 us
  blocking collectives  42.7 us (50%)
  Pallas kernels  23 us (27%)
  starting transfers between devices  12.5 us (15%)
  waiting for transfers between devices  6.81 us (8%)
    all_to_all x2, blocking collectives, exchange(): return lax.all_to_all(value, 'seq', split_axis=0, concat_axis=0, tiled=True)  42.7 us
    all_to_all x1, starting transfers between devices, exchange(): return lax.all_to_all(value, 'seq', split_axis=0, concat_axis=0, tiled=True)  12.5 us
    pallas_call x1, Pallas kernels, flip(): pl.pallas_call(flip_kernel, out_shape=(jax.ShapeDtypeStruct(shape, jnp.bf...  8.42 us
    all_to_all x1, waiting for transfers between devices, exchange(): return lax.all_to_all(value, 'seq', split_axis=0, concat_axis=0, tiled=True)  6.81 us
    pallas_call x1, Pallas kernels, column_sublayer(): pl.pallas_call(column_kernel, out_shape=jax.ShapeDtypeStruct((rows, per,...  6.02 us
    pallas_call x1, Pallas kernels, row_sublayer(): pl.pallas_call(row_kernel, out_shape=jax.ShapeDtypeStruct((tokens, width)...  4.54 us
    pallas_call x1, Pallas kernels, pack(): pl.pallas_call(pack_kernel, out_shape=jax.ShapeDtypeStruct(shape, jnp.bfl...  2.09 us
    pallas_call x1, Pallas kernels, lookup(): pl.pallas_call(lookup_kernel, out_shape=jax.ShapeDtypeStruct((count, dept...  1.92 us
  transfers between devices with their start and end apart: 1, of which 1 were waited for; matrix products, arithmetic and copies ran while one was open for 0% of the time, Pallas kernels for 10%

profile of v9, /device:TPU:1, one launch (start us, length us, event | category | flops | bytes accessed | tf_op | source)
XLA Modules:
  0.0 85.1 jit_solution(14614876744902823126)
XLA Ops:
  0.0 2.1 %shard_map.55 = bf16[64,2,2560]{2,1,0:T(2,128)(2,1)} custom-call(s32[1,128]{1,0:T(1,128)} %bitcast.6, bf16[128,2432]{1,0:T(8,128)(2,1)} %position_hbm.1), custom_call_target="tpu_custom_call" | custom-call | flops 60000002048 | bytes 180000000 | tf_op jit(solution)/shard_map/pallas_call | solution.py:386
  2.1 12.5 %all-to-all-start = ((bf16[64,2,2560]{2,1,0:T(2,128)(2,1)}), bf16[64,2,2560]{2,1,0:T(2,128)(2,1)S(1)}, u32[]{:S(2)}, u32[]{:S(2)}) async-start(bf16[64,2,2560]{2,1,0:T(2,128)(2,1)} %shard_map.55), calls=%async_computation | async-start | bytes 1310720 | tf_op jit(solution)/shard_map/all_to_all | solution.py:403
  14.6 0.0 copy-start.2
  14.6 8.4 %shard_map.56 = (bf16[15,2432,128]{2,1,0:T(8,128)(2,1)}, bf16[4,2432,128]{2,1,0:T(8,128)(2,1)}) custom-call(bf16[2,1800,2432]{2,1,0:T(8,128)(2,1)} %bitcast.3), custom_call_target="tpu_custom_call" | custom-call | flops 10000000000 | bytes 30000000 | tf_op jit(solution)/shard_map/pallas_call | solution.py:99
  23.0 6.8 %all-to-all-done.got_ref = bf16[64,2,2560]{2,1,0:T(2,128)(2,1)S(1)} async-done(((bf16[64,2,2560]{2,1,0:T(2,128)(2,1)}), bf16[64,2,2560]{2,1,0:T(2,128)(2,1)S(1)}, u32[]{:S(2)}, u32[]{:S(2)}) %all-to-all-start) | async-done | bytes 655392 | tf_op jit(solution)/shard_map/all_to_all | solution.py:403
  29.8 0.0 copy-done.2
  29.8 0.0 copy-start
  29.8 0.0 copy-start.1
  29.8 0.0 copy-start.3
  29.8 0.0 copy-start.4
  29.9 1.9 %shard_map.57 = bf16[64,38,128]{2,1,0:T(8,128)(2,1)S(1)} custom-call(bf16[64,2,2560]{2,1,0:T(2,128)(2,1)S(1)} %all-to-all-done.got_ref, bf16[38,2048]{1,0:T(8,128)(2,1)S(1)} %bitcast.5), custom_call_target="tpu_custom_call" | custom-call | flops 140000002048 | bytes 420000000 | tf_op jit(solution)/shard_map/pallas_call | solution.py:341
  31.8 20.1 %all_to_all.15.found_ref = bf16[64,38,128]{2,1,0:T(8,128)(2,1)S(1)} all-to-all(bf16[64,38,128]{2,1,0:T(8,128)(2,1)S(1)} %shard_map.57), channel_id=1, replica_groups=mesh['song'=2,'seq'=64] {'seq'}, dimensions={0} | all-to-all | bytes 1245184 | tf_op jit(solution)/shard_map/all_to_all | solution.py:403
  51.9 0.0 copy-done
  51.9 0.0 copy-done.1
  51.9 0.0 copy-done.3
  51.9 0.0 copy-done.4
  51.9 6.0 %shard_map.58 = bf16[64,2,3632]{2,1,0:T(2,128)(2,1)S(1)} custom-call(bf16[64,38,128]{2,1,0:T(8,128)(2,1)S(1)} %all_to_all.15.found_ref, bf16[64,2,2560]{2,1,0:T(2,128)(2,1)S(1)} %all-to-all-done.got_ref, bf16[2,1800,2432]{2,1,0:T(8,128)(2,1)S(1)} %bitcast.4, bf16[15,2432,128]{2,1,0:T(8,128)(2,1)S(1)} %copy-done.3, bf16[4,2432,128]{2,1,0:T(8,128)(2,1)S(1)} %copy-done.4, ...), custom_call_target="tpu_custom_call" | custom-call | flops 20000000000 | bytes 60000000 | tf_op jit(solution)/shard_map/pallas_call | solution.py:203
  57.9 22.7 %all_to_all.16.got_ref = bf16[64,2,3632]{2,1,0:T(2,128)(2,1)S(1)} all-to-all(bf16[64,2,3632]{2,1,0:T(2,128)(2,1)S(1)} %shard_map.58), channel_id=1, replica_groups=mesh['song'=2,'seq'=64] {'seq'}, dimensions={0} | all-to-all | bytes 1859584 | tf_op jit(solution)/shard_map/all_to_all | solution.py:403
  80.6 4.5 %shard_map.59 = bf16[128,2432]{1,0:T(8,128)(2,1)} custom-call(bf16[64,2,3632]{2,1,0:T(2,128)(2,1)S(1)} %all_to_all.16.got_ref, bf16[15,2432,128]{2,1,0:T(8,128)(2,1)S(1)} %copy-done.3, bf16[2,600,2432]{2,1,0:T(8,128)(2,1)S(1)} %copy-done.1), custom_call_target="tpu_custom_call" | custom-call | flops 20000000000 | bytes 60000000 | tf_op jit(solution)/shard_map/pallas_call | solution.py:277
Async XLA Ops:
  2.1 27.7 %all-to-all-start = ((bf16[64,2,2560]{2,1,0:T(2,128)(2,1)}), bf16[64,2,2560]{2,1,0:T(2,128)(2,1)S(1)}, u32[]{:S(2)}, u32[]{:S(2)}) async-start(bf16[64,2,2560]{2,1,0:T(2,128)(2,1)} %shard_map.55), calls=%async_computation | async-start | bytes 1310720 | tf_op jit(solution)/shard_map/all_to_all | solution.py:403
  14.6 15.3 %copy-start.2 = (bf16[2048,38]{0,1:T(8,128)(2,1)S(1)}, bf16[2048,38]{0,1:T(8,128)(2,1)}, u32[]{:S(2)}) copy-start(bf16[2048,38]{0,1:T(8,128)(2,1)} %param.6) | copy-start | bytes 466948
  29.8 22.0 %copy-start = (bf16[2,2432,1800]{1,2,0:T(8,128)(2,1)S(1)}, bf16[2,2432,1800]{1,2,0:T(8,128)(2,1)}, u32[]{:S(2)}) copy-start(bf16[2,2432,1800]{1,2,0:T(8,128)(2,1)} %param.8) | copy-start | bytes 52531204
  29.8 22.0 %copy-start.1 = (bf16[2,600,2432]{2,1,0:T(8,128)(2,1)S(1)}, bf16[2,600,2432]{2,1,0:T(8,128)(2,1)}, u32[]{:S(2)}) copy-start(bf16[2,600,2432]{2,1,0:T(8,128)(2,1)} %w_out_ref.3) | copy-start | bytes 17510404
  29.8 22.0 %copy-start.3 = (bf16[15,2432,128]{2,1,0:T(8,128)(2,1)S(1)}, bf16[15,2432,128]{2,1,0:T(8,128)(2,1)}, u32[]{:S(2)}) copy-start(bf16[15,2432,128]{2,1,0:T(8,128)(2,1)} %get-tuple-element.13.strips_ref) | copy-start | bytes 28016644
  29.8 22.0 %copy-start.4 = (bf16[4,2432,128]{2,1,0:T(8,128)(2,1)S(1)}, bf16[4,2432,128]{2,1,0:T(8,128)(2,1)}, u32[]{:S(2)}) copy-start(bf16[4,2432,128]{2,1,0:T(8,128)(2,1)} %get-tuple-element.14.early_ref) | copy-start | bytes 7471108

commit v10 on v9

--- a/solution.py
+++ b/solution.py
@@ -12,10 +12,10 @@
 HEAD = 150
 GROUPS = 8
 DIGIT = 64
-VMEM_LIMIT = 8 * 1024 * 1024
+VMEM_LIMIT = 6 * 1024 * 1024
 PARTS = 8
 OUT_STEP = 512
-EARLY = (128, 384, 640, 896)
+EARLY = (128, 384, 640, 896, 1152, 1408)
 FULL_LIMIT = 60 * 1024 * 1024
 AT_ONCE = 4
 

time: 85.4 us -> 85.1 us (level)
  no operation moved by 1% of the time
where the time goes in v10:
time: 85.1 us; the launch traced here: 84.9 us
  blocking collectives  42.8 us (50%)
  Pallas kernels  23.1 us (27%)
  starting transfers between devices  12.5 us (15%)
  waiting for transfers between devices  6.44 us (8%)
    all_to_all x2, blocking collectives, exchange(): return lax.all_to_all(value, 'seq', split_axis=0, concat_axis=0, tiled=True)  42.8 us
    all_to_all x1, starting transfers between devices, exchange(): return lax.all_to_all(value, 'seq', split_axis=0, concat_axis=0, tiled=True)  12.5 us
    pallas_call x1, Pallas kernels, flip(): pl.pallas_call(flip_kernel, out_shape=(jax.ShapeDtypeStruct(shape, jnp.bf...  8.79 us
    all_to_all x1, waiting for transfers between devices, exchange(): return lax.all_to_all(value, 'seq', split_axis=0, concat_axis=0, tiled=True)  6.44 us
    pallas_call x1, Pallas kernels, column_sublayer(): pl.pallas_call(column_kernel, out_shape=jax.ShapeDtypeStruct((rows, per,...  5.77 us
    pallas_call x1, Pallas kernels, row_sublayer(): pl.pallas_call(row_kernel, out_shape=jax.ShapeDtypeStruct((tokens, width)...  4.53 us
    pallas_call x1, Pallas kernels, pack(): pl.pallas_call(pack_kernel, out_shape=jax.ShapeDtypeStruct(shape, jnp.bfl...  2.09 us
    pallas_call x1, Pallas kernels, lookup(): pl.pallas_call(lookup_kernel, out_shape=jax.ShapeDtypeStruct((count, dept...  1.92 us
  transfers between devices with their start and end apart: 1, of which 1 were waited for; matrix products, arithmetic and copies ran while one was open for 0% of the time, Pallas kernels for 10%

profile of v10, /device:TPU:1, one launch (start us, length us, event | category | flops | bytes accessed | tf_op | source)
XLA Modules:
  0.0 84.9 jit_solution(10736825275679472968)
XLA Ops:
  0.0 2.1 %shard_map.55 = bf16[64,2,2560]{2,1,0:T(2,128)(2,1)} custom-call(s32[1,128]{1,0:T(1,128)} %bitcast.6, bf16[128,2432]{1,0:T(8,128)(2,1)} %position_hbm.1), custom_call_target="tpu_custom_call" | custom-call | flops 60000002048 | bytes 180000000 | tf_op jit(solution)/shard_map/pallas_call | solution.py:386
  2.1 12.5 %all-to-all-start = ((bf16[64,2,2560]{2,1,0:T(2,128)(2,1)}), bf16[64,2,2560]{2,1,0:T(2,128)(2,1)S(1)}, u32[]{:S(2)}, u32[]{:S(2)}) async-start(bf16[64,2,2560]{2,1,0:T(2,128)(2,1)} %shard_map.55), calls=%async_computation | async-start | bytes 1310720 | tf_op jit(solution)/shard_map/all_to_all | solution.py:403
  14.6 0.0 copy-start.2
  14.6 8.8 %shard_map.56 = (bf16[15,2432,128]{2,1,0:T(8,128)(2,1)}, bf16[6,2432,128]{2,1,0:T(8,128)(2,1)}) custom-call(bf16[2,1800,2432]{2,1,0:T(8,128)(2,1)} %bitcast.3), custom_call_target="tpu_custom_call" | custom-call | flops 10000000000 | bytes 30000000 | tf_op jit(solution)/shard_map/pallas_call | solution.py:99
  23.4 6.4 %all-to-all-done.got_ref = bf16[64,2,2560]{2,1,0:T(2,128)(2,1)S(1)} async-done(((bf16[64,2,2560]{2,1,0:T(2,128)(2,1)}), bf16[64,2,2560]{2,1,0:T(2,128)(2,1)S(1)}, u32[]{:S(2)}, u32[]{:S(2)}) %all-to-all-start) | async-done | bytes 655392 | tf_op jit(solution)/shard_map/all_to_all | solution.py:403
  29.8 0.0 copy-done.2
  29.8 0.0 copy-start
  29.8 0.0 copy-start.1
  29.8 0.0 copy-start.3
  29.8 0.0 copy-start.4
  29.9 1.9 %shard_map.57 = bf16[64,38,128]{2,1,0:T(8,128)(2,1)S(1)} custom-call(bf16[64,2,2560]{2,1,0:T(2,128)(2,1)S(1)} %all-to-all-done.got_ref, bf16[38,2048]{1,0:T(8,128)(2,1)S(1)} %bitcast.5), custom_call_target="tpu_custom_call" | custom-call | flops 140000002048 | bytes 420000000 | tf_op jit(solution)/shard_map/pallas_call | solution.py:341
  31.8 20.1 %all_to_all.15.found_ref = bf16[64,38,128]{2,1,0:T(8,128)(2,1)S(1)} all-to-all(bf16[64,38,128]{2,1,0:T(8,128)(2,1)S(1)} %shard_map.57), channel_id=1, replica_groups=mesh['song'=2,'seq'=64] {'seq'}, dimensions={0} | all-to-all | bytes 1245184 | tf_op jit(solution)/shard_map/all_to_all | solution.py:403
  51.8 0.0 copy-done
  51.8 0.0 copy-done.1
  51.8 0.0 copy-done.3
  51.9 0.0 copy-done.4
  51.9 5.8 %shard_map.58 = bf16[64,2,3632]{2,1,0:T(2,128)(2,1)S(1)} custom-call(bf16[64,38,128]{2,1,0:T(8,128)(2,1)S(1)} %all_to_all.15.found_ref, bf16[64,2,2560]{2,1,0:T(2,128)(2,1)S(1)} %all-to-all-done.got_ref, bf16[2,1800,2432]{2,1,0:T(8,128)(2,1)S(1)} %bitcast.4, bf16[15,2432,128]{2,1,0:T(8,128)(2,1)S(1)} %copy-done.3, bf16[6,2432,128]{2,1,0:T(8,128)(2,1)S(1)} %copy-done.4, ...), custom_call_target="tpu_custom_call" | custom-call | flops 20000000000 | bytes 60000000 | tf_op jit(solution)/shard_map/pallas_call | solution.py:203
  57.6 22.7 %all_to_all.16.got_ref = bf16[64,2,3632]{2,1,0:T(2,128)(2,1)S(1)} all-to-all(bf16[64,2,3632]{2,1,0:T(2,128)(2,1)S(1)} %shard_map.58), channel_id=1, replica_groups=mesh['song'=2,'seq'=64] {'seq'}, dimensions={0} | all-to-all | bytes 1859584 | tf_op jit(solution)/shard_map/all_to_all | solution.py:403
  80.3 4.5 %shard_map.59 = bf16[128,2432]{1,0:T(8,128)(2,1)} custom-call(bf16[64,2,3632]{2,1,0:T(2,128)(2,1)S(1)} %all_to_all.16.got_ref, bf16[15,2432,128]{2,1,0:T(8,128)(2,1)S(1)} %copy-done.3, bf16[2,600,2432]{2,1,0:T(8,128)(2,1)S(1)} %copy-done.1), custom_call_target="tpu_custom_call" | custom-call | flops 20000000000 | bytes 60000000 | tf_op jit(solution)/shard_map/pallas_call | solution.py:277
Async XLA Ops:
  2.1 27.7 %all-to-all-start = ((bf16[64,2,2560]{2,1,0:T(2,128)(2,1)}), bf16[64,2,2560]{2,1,0:T(2,128)(2,1)S(1)}, u32[]{:S(2)}, u32[]{:S(2)}) async-start(bf16[64,2,2560]{2,1,0:T(2,128)(2,1)} %shard_map.55), calls=%async_computation | async-start | bytes 1310720 | tf_op jit(solution)/shard_map/all_to_all | solution.py:403
  14.6 15.3 %copy-start.2 = (bf16[2048,38]{0,1:T(8,128)(2,1)S(1)}, bf16[2048,38]{0,1:T(8,128)(2,1)}, u32[]{:S(2)}) copy-start(bf16[2048,38]{0,1:T(8,128)(2,1)} %param.6) | copy-start | bytes 466948
  29.8 22.0 %copy-start = (bf16[2,2432,1800]{1,2,0:T(8,128)(2,1)S(1)}, bf16[2,2432,1800]{1,2,0:T(8,128)(2,1)}, u32[]{:S(2)}) copy-start(bf16[2,2432,1800]{1,2,0:T(8,128)(2,1)} %param.8) | copy-start | bytes 52531204
  29.8 22.0 %copy-start.1 = (bf16[2,600,2432]{2,1,0:T(8,128)(2,1)S(1)}, bf16[2,600,2432]{2,1,0:T(8,128)(2,1)}, u32[]{:S(2)}) copy-start(bf16[2,600,2432]{2,1,0:T(8,128)(2,1)} %w_out_ref.3) | copy-start | bytes 17510404
  29.8 22.0 %copy-start.3 = (bf16[15,2432,128]{2,1,0:T(8,128)(2,1)S(1)}, bf16[15,2432,128]{2,1,0:T(8,128)(2,1)}, u32[]{:S(2)}) copy-start(bf16[15,2432,128]{2,1,0:T(8,128)(2,1)} %get-tuple-element.13.strips_ref) | copy-start | bytes 28016644
  29.8 22.0 %copy-start.4 = (bf16[6,2432,128]{2,1,0:T(8,128)(2,1)S(1)}, bf16[6,2432,128]{2,1,0:T(8,128)(2,1)}, u32[]{:S(2)}) copy-start(bf16[6,2432,128]{2,1,0:T(8,128)(2,1)} %get-tuple-element.14.early_ref) | copy-start | bytes 11206660

commit v11 on v10

--- a/solution.py
+++ b/solution.py
@@ -14,7 +14,7 @@
 DIGIT = 64
 VMEM_LIMIT = 6 * 1024 * 1024
 PARTS = 8
-OUT_STEP = 512
+OUT_STEP = 256
 EARLY = (128, 384, 640, 896, 1152, 1408)
 FULL_LIMIT = 60 * 1024 * 1024
 AT_ONCE = 4

time: 85.1 us -> 85.1 us (level)
  no operation moved by 1% of the time
where the time goes in v11:
time: 85.1 us; the launch traced here: 84.9 us
  blocking collectives  42.8 us (50%)
  Pallas kernels  23.1 us (27%)
  starting transfers between devices  12.5 us (15%)
  waiting for transfers between devices  6.44 us (8%)
    all_to_all x2, blocking collectives, exchange(): return lax.all_to_all(value, 'seq', split_axis=0, concat_axis=0, tiled=True)  42.8 us
    all_to_all x1, starting transfers between devices, exchange(): return lax.all_to_all(value, 'seq', split_axis=0, concat_axis=0, tiled=True)  12.5 us
    pallas_call x1, Pallas kernels, flip(): pl.pallas_call(flip_kernel, out_shape=(jax.ShapeDtypeStruct(shape, jnp.bf...  8.79 us
    all_to_all x1, waiting for transfers between devices, exchange(): return lax.all_to_all(value, 'seq', split_axis=0, concat_axis=0, tiled=True)  6.44 us
    pallas_call x1, Pallas kernels, column_sublayer(): pl.pallas_call(column_kernel, out_shape=jax.ShapeDtypeStruct((rows, per,...  5.77 us
    pallas_call x1, Pallas kernels, row_sublayer(): pl.pallas_call(row_kernel, out_shape=jax.ShapeDtypeStruct((tokens, width)...  4.53 us
    pallas_call x1, Pallas kernels, pack(): pl.pallas_call(pack_kernel, out_shape=jax.ShapeDtypeStruct(shape, jnp.bfl...  2.09 us
    pallas_call x1, Pallas kernels, lookup(): pl.pallas_call(lookup_kernel, out_shape=jax.ShapeDtypeStruct((count, dept...  1.92 us
  transfers between devices with their start and end apart: 1, of which 1 were waited for; matrix products, arithmetic and copies ran while one was open for 0% of the time, Pallas kernels for 10%

profile of v11, /device:TPU:1, one launch (start us, length us, event | category | flops | bytes accessed | tf_op | source)
XLA Modules:
  0.0 84.9 jit_solution(10736825275679472968)
XLA Ops:
  0.0 2.1 %shard_map.55 = bf16[64,2,2560]{2,1,0:T(2,128)(2,1)} custom-call(s32[1,128]{1,0:T(1,128)} %bitcast.6, bf16[128,2432]{1,0:T(8,128)(2,1)} %position_hbm.1), custom_call_target="tpu_custom_call" | custom-call | flops 60000002048 | bytes 180000000 | tf_op jit(solution)/shard_map/pallas_call | solution.py:386
  2.1 12.5 %all-to-all-start = ((bf16[64,2,2560]{2,1,0:T(2,128)(2,1)}), bf16[64,2,2560]{2,1,0:T(2,128)(2,1)S(1)}, u32[]{:S(2)}, u32[]{:S(2)}) async-start(bf16[64,2,2560]{2,1,0:T(2,128)(2,1)} %shard_map.55), calls=%async_computation | async-start | bytes 1310720 | tf_op jit(solution)/shard_map/all_to_all | solution.py:403
  14.6 0.0 copy-start.2
  14.6 8.8 %shard_map.56 = (bf16[15,2432,128]{2,1,0:T(8,128)(2,1)}, bf16[6,2432,128]{2,1,0:T(8,128)(2,1)}) custom-call(bf16[2,1800,2432]{2,1,0:T(8,128)(2,1)} %bitcast.3), custom_call_target="tpu_custom_call" | custom-call | flops 10000000000 | bytes 30000000 | tf_op jit(solution)/shard_map/pallas_call | solution.py:99
  23.4 6.4 %all-to-all-done.got_ref = bf16[64,2,2560]{2,1,0:T(2,128)(2,1)S(1)} async-done(((bf16[64,2,2560]{2,1,0:T(2,128)(2,1)}), bf16[64,2,2560]{2,1,0:T(2,128)(2,1)S(1)}, u32[]{:S(2)}, u32[]{:S(2)}) %all-to-all-start) | async-done | bytes 655392 | tf_op jit(solution)/shard_map/all_to_all | solution.py:403
  29.8 0.0 copy-done.2
  29.8 0.0 copy-start
  29.8 0.0 copy-start.1
  29.8 0.0 copy-start.3
  29.8 0.0 copy-start.4
  29.9 1.9 %shard_map.57 = bf16[64,38,128]{2,1,0:T(8,128)(2,1)S(1)} custom-call(bf16[64,2,2560]{2,1,0:T(2,128)(2,1)S(1)} %all-to-all-done.got_ref, bf16[38,2048]{1,0:T(8,128)(2,1)S(1)} %bitcast.5), custom_call_target="tpu_custom_call" | custom-call | flops 140000002048 | bytes 420000000 | tf_op jit(solution)/shard_map/pallas_call | solution.py:341
  31.8 20.1 %all_to_all.15.found_ref = bf16[64,38,128]{2,1,0:T(8,128)(2,1)S(1)} all-to-all(bf16[64,38,128]{2,1,0:T(8,128)(2,1)S(1)} %shard_map.57), channel_id=1, replica_groups=mesh['song'=2,'seq'=64] {'seq'}, dimensions={0} | all-to-all | bytes 1245184 | tf_op jit(solution)/shard_map/all_to_all | solution.py:403
  51.8 0.0 copy-done
  51.8 0.0 copy-done.1
  51.8 0.0 copy-done.3
  51.9 0.0 copy-done.4
  51.9 5.8 %shard_map.58 = bf16[64,2,3632]{2,1,0:T(2,128)(2,1)S(1)} custom-call(bf16[64,38,128]{2,1,0:T(8,128)(2,1)S(1)} %all_to_all.15.found_ref, bf16[64,2,2560]{2,1,0:T(2,128)(2,1)S(1)} %all-to-all-done.got_ref, bf16[2,1800,2432]{2,1,0:T(8,128)(2,1)S(1)} %bitcast.4, bf16[15,2432,128]{2,1,0:T(8,128)(2,1)S(1)} %copy-done.3, bf16[6,2432,128]{2,1,0:T(8,128)(2,1)S(1)} %copy-done.4, ...), custom_call_target="tpu_custom_call" | custom-call | flops 20000000000 | bytes 60000000 | tf_op jit(solution)/shard_map/pallas_call | solution.py:203
  57.6 22.7 %all_to_all.16.got_ref = bf16[64,2,3632]{2,1,0:T(2,128)(2,1)S(1)} all-to-all(bf16[64,2,3632]{2,1,0:T(2,128)(2,1)S(1)} %shard_map.58), channel_id=1, replica_groups=mesh['song'=2,'seq'=64] {'seq'}, dimensions={0} | all-to-all | bytes 1859584 | tf_op jit(solution)/shard_map/all_to_all | solution.py:403
  80.3 4.5 %shard_map.59 = bf16[128,2432]{1,0:T(8,128)(2,1)} custom-call(bf16[64,2,3632]{2,1,0:T(2,128)(2,1)S(1)} %all_to_all.16.got_ref, bf16[15,2432,128]{2,1,0:T(8,128)(2,1)S(1)} %copy-done.3, bf16[2,600,2432]{2,1,0:T(8,128)(2,1)S(1)} %copy-done.1), custom_call_target="tpu_custom_call" | custom-call | flops 20000000000 | bytes 60000000 | tf_op jit(solution)/shard_map/pallas_call | solution.py:277
Async XLA Ops:
  2.1 27.7 %all-to-all-start = ((bf16[64,2,2560]{2,1,0:T(2,128)(2,1)}), bf16[64,2,2560]{2,1,0:T(2,128)(2,1)S(1)}, u32[]{:S(2)}, u32[]{:S(2)}) async-start(bf16[64,2,2560]{2,1,0:T(2,128)(2,1)} %shard_map.55), calls=%async_computation | async-start | bytes 1310720 | tf_op jit(solution)/shard_map/all_to_all | solution.py:403
  14.6 15.3 %copy-start.2 = (bf16[2048,38]{0,1:T(8,128)(2,1)S(1)}, bf16[2048,38]{0,1:T(8,128)(2,1)}, u32[]{:S(2)}) copy-start(bf16[2048,38]{0,1:T(8,128)(2,1)} %param.6) | copy-start | bytes 466948
  29.8 22.0 %copy-start = (bf16[2,2432,1800]{1,2,0:T(8,128)(2,1)S(1)}, bf16[2,2432,1800]{1,2,0:T(8,128)(2,1)}, u32[]{:S(2)}) copy-start(bf16[2,2432,1800]{1,2,0:T(8,128)(2,1)} %param.8) | copy-start | bytes 52531204
  29.8 22.0 %copy-start.1 = (bf16[2,600,2432]{2,1,0:T(8,128)(2,1)S(1)}, bf16[2,600,2432]{2,1,0:T(8,128)(2,1)}, u32[]{:S(2)}) copy-start(bf16[2,600,2432]{2,1,0:T(8,128)(2,1)} %w_out_ref.3) | copy-start | bytes 17510404
  29.8 22.0 %copy-start.3 = (bf16[15,2432,128]{2,1,0:T(8,128)(2,1)S(1)}, bf16[15,2432,128]{2,1,0:T(8,128)(2,1)}, u32[]{:S(2)}) copy-start(bf16[15,2432,128]{2,1,0:T(8,128)(2,1)} %get-tuple-element.13.strips_ref) | copy-start | bytes 28016644
  29.8 22.0 %copy-start.4 = (bf16[6,2432,128]{2,1,0:T(8,128)(2,1)S(1)}, bf16[6,2432,128]{2,1,0:T(8,128)(2,1)}, u32[]{:S(2)}) copy-start(bf16[6,2432,128]{2,1,0:T(8,128)(2,1)} %get-tuple-element.14.early_ref) | copy-start | bytes 11206660
